TPU v7x, 256 devices: a whole 4x4x8 slice. The times are simulated.
256 devices in a mesh: dp: 8 (over y, core), seq: 32 (over z, x).
Axes of the slice: x: 4, y: 4, z: 8, core: 2. Of those that a mesh axis runs over, the one named last changes fastest.
Arguments:
- query_rows: bfloat16 [8, 8192, 1536], P('dp', 'seq'), may hold values from -36 to 36, as said below
- key_rows: bfloat16 [8, 8192, 1536], P('dp', 'seq'), may hold values from -6 to 6
- value_rows: bfloat16 [8, 8192, 1536], P('dp', 'seq'), may hold values from -6 to 6
- norm_gain: float32 [1536], replicated, may hold values from 0.1 to 1.9
- grad_output: bfloat16 [8, 8192, 1536], P('dp', 'seq'), may hold values from -6 to 6
Outputs:
- attended: bfloat16 [8, 8192, 1536], P('dp', 'seq')
- grad_query: bfloat16 [8, 8192, 1536], P('dp', 'seq')
- grad_key: bfloat16 [8, 8192, 1536], P('dp', 'seq')
- grad_value: bfloat16 [8, 8192, 1536], P('dp', 'seq')
- grad_gain: float32 [1536], replicated
Inputs may be any that keep to these rules, and one draw needn't show every extreme that they name: `query_rows`: query features.
All inputs are finite; a program needn't handle non-finite values.
Results may differ from a plain program's by a relative error of at most 0.0057.
Values sent between devices are 32-bit elements; how exact they have to be, the bound alone decides.
A program may use at most 128 MiB of HBM per device.

v0:
```python
import jax
import jax.numpy as jnp
from jax import lax
from jax.sharding import PartitionSpec as P

HEADS = 12
HEAD_DIM = 128
BLOCK = 256


norm_eps = 1e-05


def carried_in(value, axis, backward, extra=None):
    count = lax.axis_size(axis)
    lanes = value.shape[-1]
    rows = value.reshape(count, -1, lanes)
    depth = rows.shape[1]
    if extra is not None:
        spread = extra.reshape(count, 1, -1)
        spread = jnp.pad(spread, ((0, 0), (0, 0), (0, lanes - spread.shape[2])))
        rows = jnp.concatenate([rows, spread], axis=1)
    parts = lax.all_to_all(rows, axis, 0, 0)
    running = lax.cumsum(parts, axis=0, reverse=backward)
    empty = jnp.zeros_like(running[:1])
    if backward:
        shifted = jnp.concatenate([running[1:], empty], axis=0)
    else:
        shifted = jnp.concatenate([empty, running[:-1]], axis=0)
    if extra is not None:
        total = running[-1:] if not backward else running[:1]
        row = lax.broadcasted_iota(jnp.int32, shifted.shape, 1)
        shifted = jnp.where(row < depth, shifted, total)
    back = lax.all_to_all(shifted, axis, 0, 0)
    state = back[:, :depth].reshape(value.shape)
    if extra is None:
        return state
    return state, back[:, depth, : extra.size // count].reshape(extra.shape)


def lower_mask(length):
    row_index = lax.broadcasted_iota(jnp.int32, (length, length), 0)
    col_index = lax.broadcasted_iota(jnp.int32, (length, length), 1)
    return row_index >= col_index


def local(query_rows, key_rows, value_rows, norm_gain, grad_output):
    tokens = query_rows.shape[1]
    features = query_rows.shape[2]
    blocks = tokens // BLOCK
    block_shape = (blocks, BLOCK, HEADS, HEAD_DIM)
    queries = query_rows.reshape(block_shape)
    key_blocks = key_rows.reshape(block_shape)
    value_blocks = value_rows.reshape(block_shape)
    causal = lower_mask(BLOCK)
    local_states = jnp.einsum(
        "nchd,nche->nhde", key_blocks, value_blocks, preferred_element_type=jnp.float32
    )
    device_total = jnp.sum(local_states, axis=0)
    carried = carried_in(device_total, "seq", False)
    running = jnp.cumsum(local_states, axis=0)
    before = jnp.concatenate([local_states[:1] * 0.0, running[:-1]], axis=0)
    states = (carried[None] + before).astype(jnp.bfloat16)
    scores = jnp.einsum("nchd,nthd->nhct", queries, key_blocks, preferred_element_type=jnp.float32)
    weights = jnp.where(causal, scores, 0.0).astype(jnp.bfloat16)
    combined = jnp.einsum("nchd,nhde->nche", queries, states, preferred_element_type=jnp.float32)
    combined = combined + jnp.einsum(
        "nhct,nthe->nche", weights, value_blocks, preferred_element_type=jnp.float32
    )
    combined = combined.reshape(1, tokens, features)
    inverse = lax.rsqrt(jnp.mean(combined * combined, axis=-1, keepdims=True) + norm_eps)
    normed = combined * inverse
    attended = (normed * norm_gain).astype(jnp.bfloat16)
    upstream = grad_output.astype(jnp.float32)
    gain_terms = jnp.sum(upstream * normed, axis=(0, 1))
    grad_normed = upstream * norm_gain
    grad_combined = inverse * (
        grad_normed - normed * jnp.mean(grad_normed * normed, axis=-1, keepdims=True)
    )
    grad_blocks = grad_combined.astype(jnp.bfloat16).reshape(block_shape)
    query_parts = jnp.einsum(
        "nchd,nche->nhde", queries, grad_blocks, preferred_element_type=jnp.float32
    )
    suffix, gain_seq = carried_in(jnp.sum(query_parts, axis=0), "seq", True, gain_terms)
    grad_gain = lax.psum(gain_seq, "dp")
    from_end = jnp.cumsum(query_parts[::-1], axis=0)[::-1]
    behind = jnp.concatenate([from_end[1:], jnp.zeros_like(query_parts)], axis=0)
    suffix_states = (suffix[None] + behind).astype(jnp.bfloat16)
    grad_scores = jnp.einsum(
        "nche,nthe->nhct", grad_blocks, value_blocks, preferred_element_type=jnp.float32
    )
    grad_weights = jnp.where(causal, grad_scores, 0.0).astype(jnp.bfloat16)
    grad_query = jnp.einsum(
        "nche,nhde->nchd", grad_blocks, states, preferred_element_type=jnp.float32
    )
    grad_query = grad_query + jnp.einsum(
        "nhct,nthd->nchd", grad_weights, key_blocks, preferred_element_type=jnp.float32
    )
    grad_key = jnp.einsum(
        "nche,nhde->nchd", value_blocks, suffix_states, preferred_element_type=jnp.float32
    )
    grad_key = grad_key + jnp.einsum(
        "nhct,nchd->nthd", grad_weights, queries, preferred_element_type=jnp.float32
    )
    grad_value = jnp.einsum(
        "nchd,nhde->nche", key_blocks, suffix_states, preferred_element_type=jnp.float32
    )
    grad_value = grad_value + jnp.einsum(
        "nhct,nche->nthe", weights, grad_blocks, preferred_element_type=jnp.float32
    )
    out_shape = (1, tokens, features)
    return (
        attended,
        grad_query.reshape(out_shape).astype(jnp.bfloat16),
        grad_key.reshape(out_shape).astype(jnp.bfloat16),
        grad_value.reshape(out_shape).astype(jnp.bfloat16),
        grad_gain,
    )


def solution(mesh):
    placed = (
        P("dp", "seq", None),
        P("dp", "seq", None),
        P("dp", "seq", None),
        P(),
        P("dp", "seq", None),
    )
    return jax.shard_map(
        local,
        mesh=mesh,
        in_specs=placed,
        out_specs=(
            P("dp", "seq", None),
            P("dp", "seq", None),
            P("dp", "seq", None),
            P("dp", "seq", None),
            P(),
        ),
        check_vma=False,
    )
```

profile of v0, /device:TPU:1, one launch (start us, length us, event | category | flops | bytes accessed | tf_op | source)
XLA Modules:
  0.0 161.1 jit_solution(12790451784885239742)
XLA Ops:
  0.6 1.5 copy.32
  2.8 32.7 %all_to_all.20 = f32[32,48,128]{2,1,0:T(8,128)S(1)} all-to-all(f32[32,48,128]{2,1,0:T(8,128)S(1)} %bitcast.96), channel_id=1, replica_groups=mesh['dp'=8,'seq'=32] {'seq'}, dimensions={0} | all-to-all | bytes 1572864 | tf_op jit(solution)/shard_map/all_to_all | solution.py:23
  35.5 3.2 %fusion.9 = f32[32,48,128]{2,1,0:T(8,128)S(1)} fusion(f32[32,48,128]{2,1,0:T(8,128)S(1)} %all_to_all.20), kind=kOutput, calls=%fused_computation.31 | output fusion | flops 6094848 | bytes 1572864 | tf_op jit(solution)/shard_map/carried_in/reduce_window_sum | solution.py:24
  39.7 5.9 %all-to-all-start.1 = ((f32[32,48,128]{2,1,0:T(8,128)}), f32[32,48,128]{2,1,0:T(8,128)}, u32[]{:S(2)}, u32[]{:S(2)}) async-start(f32[32,48,128]{2,1,0:T(8,128)} %concatenate.9), calls=%async_computation.1 | async-start | bytes 1572864 | tf_op jit(solution)/shard_map/all_to_all | solution.py:34
  45.9 1.7 %copy.35 = bf16[1,256,1536]{1,2,0:T(8,128)(2,1)S(1)} copy(bf16[1,256,1536]{2,1,0:T(8,128)(2,1)} %param.5) | data formatting | bytes 1572864 | tf_op args[0]
  49.5 1.8 %fusion.12 = f32[12,256,128]{1,2,0:T(8,128)} fusion(bf16[12,256,256]{2,1,0:T(8,128)(2,1)S(1)} %select_convert_fusion.1, bf16[256,12,128]{0,2,1:T(8,128)(2,1)S(1)} %bitcast.81), kind=kOutput, calls=%fused_computation.34 | convolution fusion | flops 201326592 | bytes 3932160 | tf_op jit(solution)/shard_map/nhct,nthe->nche/dot_general | solution.py:67
  51.3 14.1 %all-to-all-done.1 = f32[32,48,128]{2,1,0:T(8,128)} async-done(((f32[32,48,128]{2,1,0:T(8,128)}), f32[32,48,128]{2,1,0:T(8,128)}, u32[]{:S(2)}, u32[]{:S(2)}) %all-to-all-start.1) | async-done | bytes 786464 | tf_op jit(solution)/shard_map/all_to_all | solution.py:34
  65.4 1.6 add_convert_fusion.1
  68.0 1.3 fusion.5
  69.3 2.5 %fusion.4 = (bf16[1,256,1536]{1,2,0:T(8,128)(2,1)S(1)}, bf16[1,256,1536]{1,2,0:T(8,128)(2,1)}) fusion(bf16[1,256,1536]{1,2,0:T(8,128)(2,1)} %copy-done.3, f32[12,128,256]{2,1,0:T(8,128)S(1)} %get-tuple-element.20, f32[256]{0:T(256)S(1)} %broadcast_multiply_fusion, f32[1536]{0:T(1024)S(1)} %copy-done.10, f32[256]{0:T(256)S(1)} %add_rsqrt_fusion), kind=kLoop, calls=%fused_computation.8 | loop fusion | flops 3538944 | bytes 3940352 | tf_op jit(solution)/shard_map/convert_element_type | solution.py:80
  73.9 6.8 %all-to-all-start.2 = ((f32[32,49,128]{2,1,0:T(8,128)}), f32[32,49,128]{2,1,0:T(8,128)}, u32[]{:S(2)}, u32[]{:S(2)}) async-start(f32[32,49,128]{2,1,0:T(8,128)} %select_maximum_fusion), calls=%async_computation.2 | async-start | bytes 1835008 | tf_op jit(solution)/shard_map/all_to_all | solution.py:23
  80.8 2.3 %copy.48 = bf16[1,256,1536]{2,1,0:T(8,128)(2,1)} copy(bf16[1,256,1536]{1,2,0:T(8,128)(2,1)} %get-tuple-element.18) | data formatting | bytes 1572864
  83.1 19.9 %all-to-all-done.2 = f32[32,49,128]{2,1,0:T(8,128)} async-done(((f32[32,49,128]{2,1,0:T(8,128)}), f32[32,49,128]{2,1,0:T(8,128)}, u32[]{:S(2)}, u32[]{:S(2)}) %all-to-all-start.2) | async-done | bytes 802848 | tf_op jit(solution)/shard_map/all_to_all | solution.py:23
  103.0 1.6 %fusion.10 = f32[32,49,128]{2,1,0:T(8,128)S(1)} fusion(f32[32,49,128]{2,1,0:T(8,128)} %all-to-all-done.2), kind=kOutput, calls=%fused_computation.32 | output fusion | flops 6221824 | bytes 1605632 | tf_op jit(solution)/shard_map/carried_in/reduce_window_sum | solution.py:24
  105.8 6.7 %all-to-all-start.3 = ((f32[32,49,128]{2,1,0:T(8,128)}), f32[32,49,128]{2,1,0:T(8,128)}, u32[]{:S(2)}, u32[]{:S(2)}) async-start(f32[32,49,128]{2,1,0:T(8,128)} %pad_select_fusion), calls=%async_computation.3 | async-start | bytes 1835008 | tf_op jit(solution)/shard_map/all_to_all | solution.py:34
  112.5 1.5 select_convert_fusion
  115.1 1.2 fusion.7
  116.4 2.3 %copy.49 = bf16[1,256,1536]{2,1,0:T(8,128)(2,1)} copy(bf16[1,256,1536]{1,2,0:T(8,128)(2,1)} %bitcast.100) | data formatting | bytes 1572864
  118.7 3.1 %fusion.15 = f32[12,128,256]{2,1,0:T(8,128)} fusion(bf16[256,12,128]{0,2,1:T(8,128)(2,1)S(1)} %bitcast.95, bf16[12,256,256]{2,1,0:T(8,128)(2,1)} %copy-done), kind=kOutput, calls=%fused_computation.37 | convolution fusion | flops 201326592 | bytes 3932160 | tf_op jit(solution)/shard_map/nhct,nche->nthe/dot_general | solution.py:108
  121.7 1.5 fusion.16
  123.3 11.3 %all-to-all-done.3 = f32[32,49,128]{2,1,0:T(8,128)} async-done(((f32[32,49,128]{2,1,0:T(8,128)}), f32[32,49,128]{2,1,0:T(8,128)}, u32[]{:S(2)}, u32[]{:S(2)}) %all-to-all-start.3) | async-done | bytes 802848 | tf_op jit(solution)/shard_map/all_to_all | solution.py:34
  136.8 2.7 %add_convert_fusion = bf16[12,128,256]{2,1,0:T(8,128)(2,1)} fusion(f32[12,128,256]{2,1,0:T(8,128)} %fusion.15, bf16[12,128,128]{2,1,0:T(8,128)(2,1)S(1)} %bitcast.97, bf16[256,12,128]{0,2,1:T(8,128)(2,1)S(1)} %bitcast.87), kind=kOutput, calls=%fused_computation.18 | convolution fusion | flops 101449728 | bytes 3538944 | tf_op jit(solution)/shard_map/nchd,nhde->nche/dot_general | solution.py:105
  139.5 2.4 %copy.51 = bf16[1,256,1536]{2,1,0:T(8,128)(2,1)} copy(bf16[1,256,1536]{1,2,0:T(8,128)(2,1)} %bitcast.101) | data formatting | bytes 1572864
  141.9 17.7 %psum.7 = f32[1536]{0:T(1024)} all-reduce(f32[1536]{0:T(1024)S(1)} %reshape_squeeze.3), channel_id=1, replica_groups=mesh['dp'=8,'seq'=32] {'dp'}, use_global_device_ids=true, to_apply=%region_5.6 | all-reduce | flops 1536 | bytes 12288 | tf_op jit(solution)/shard_map/psum | solution.py:85
  (45 shorter events, 12.8 us)
Async XLA Ops:
  0.6 1.5 copy-start.7
  2.8 35.9 %copy-start.4 = (f32[12,128,128]{2,1,0:T(8,128)}, f32[12,128,128]{2,1,0:T(8,128)S(1)}, u32[]{:S(2)}) copy-start(f32[12,128,128]{2,1,0:T(8,128)S(1)} %fusion.11) | copy-start | bytes 2359300
  38.8 6.8 %copy-start.8 = (bf16[1,256,1536]{2,1,0:T(8,128)(2,1)S(1)}, bf16[1,256,1536]{2,1,0:T(8,128)(2,1)}, u32[]{:S(2)}) copy-start(bf16[1,256,1536]{2,1,0:T(8,128)(2,1)} %param.9) | copy-start | bytes 2359300
  39.7 25.7 %all-to-all-start.1 = ((f32[32,48,128]{2,1,0:T(8,128)}), f32[32,48,128]{2,1,0:T(8,128)}, u32[]{:S(2)}, u32[]{:S(2)}) async-start(f32[32,48,128]{2,1,0:T(8,128)} %concatenate.9), calls=%async_computation.1 | async-start | bytes 1572864 | tf_op jit(solution)/shard_map/all_to_all | solution.py:34
  45.9 21.8 %copy-start.3 = (bf16[1,256,1536]{1,2,0:T(8,128)(2,1)}, bf16[1,256,1536]{1,2,0:T(8,128)(2,1)S(1)}, u32[]{:S(2)}) copy-start(bf16[1,256,1536]{1,2,0:T(8,128)(2,1)S(1)} %copy.40) | copy-start | bytes 2359300
  47.7 0.7 copy-start.9
  48.3 1.2 copy-start
  65.4 1.9 %copy-start.6 = (f32[12,256,128]{1,2,0:T(8,128)S(1)}, f32[12,256,128]{1,2,0:T(8,128)}, u32[]{:S(2)}) copy-start(f32[12,256,128]{1,2,0:T(8,128)} %fusion.12) | copy-start | bytes 4718596
  67.3 0.7 copy-start.10
  73.9 29.1 %all-to-all-start.2 = ((f32[32,49,128]{2,1,0:T(8,128)}), f32[32,49,128]{2,1,0:T(8,128)}, u32[]{:S(2)}, u32[]{:S(2)}) async-start(f32[32,49,128]{2,1,0:T(8,128)} %select_maximum_fusion), calls=%async_computation.2 | async-start | bytes 1835008 | tf_op jit(solution)/shard_map/all_to_all | solution.py:23
  105.8 28.8 %all-to-all-start.3 = ((f32[32,49,128]{2,1,0:T(8,128)}), f32[32,49,128]{2,1,0:T(8,128)}, u32[]{:S(2)}, u32[]{:S(2)}) async-start(f32[32,49,128]{2,1,0:T(8,128)} %pad_select_fusion), calls=%async_computation.3 | async-start | bytes 1835008 | tf_op jit(solution)/shard_map/all_to_all | solution.py:34
  114.0 1.1 copy-start.1
  118.7 3.1 %copy-start.2 = (bf16[12,256,256]{2,1,0:T(8,128)(2,1)S(1)}, bf16[12,256,256]{2,1,0:T(8,128)(2,1)}, u32[]{:S(2)}) copy-start(bf16[12,256,256]{2,1,0:T(8,128)(2,1)} %copy-done.1) | copy-start | bytes 4718596
  139.5 20.1 %copy-start.5 = (f32[12,256,128]{1,2,0:T(8,128)S(1)}, f32[12,256,128]{1,2,0:T(8,128)}, u32[]{:S(2)}) copy-start(f32[12,256,128]{1,2,0:T(8,128)} %fusion.16) | copy-start | bytes 4718596
where the time goes:
time: 162 us; the launch traced here: 161 us
  blocking collectives  50.5 us (31%)
  waiting for transfers between devices  45.4 us (28%)
  starting transfers between devices  19.4 us (12%)
  local copies, waits for them, and re-layouts  18.1 us (11%)
  matrix products  14.6 us (9%)
  other arithmetic  12.3 us (8%)
    all_to_all x1, blocking collectives, carried_in(): parts = lax.all_to_all(rows, axis, 0, 0)  32.7 us
    all_to_all x2, waiting for transfers between devices, carried_in(): back = lax.all_to_all(shifted, axis, 0, 0)  25.4 us
    all_to_all x1, waiting for transfers between devices, carried_in(): parts = lax.all_to_all(rows, axis, 0, 0)  19.9 us
    psum x1, blocking collectives, local(): grad_gain = lax.psum(gain_seq, 'dp')  17.7 us
    unnamed x30, local copies, waits for them, and re-layouts  14 us
    all_to_all x2, starting transfers between devices, carried_in(): back = lax.all_to_all(shifted, axis, 0, 0)  12.6 us
    all_to_all x1, starting transfers between devices, carried_in(): parts = lax.all_to_all(rows, axis, 0, 0)  6.81 us
    another operation x2, other arithmetic, carried_in(): running = lax.cumsum(parts, axis=0, reverse=backward)  4.83 us
  transfers between devices with their start and end apart: 3, of which 3 were waited for; matrix products, arithmetic and copies ran while one was open for 11% of the time, Pallas kernels for 0%

commit v1 on v0

--- a/solution.py
+++ b/solution.py
@@ -11,15 +11,10 @@
 norm_eps = 1e-05
 
 
-def carried_in(value, axis, backward, extra=None):
+def carried_in(value, axis, backward):
     count = lax.axis_size(axis)
     lanes = value.shape[-1]
     rows = value.reshape(count, -1, lanes)
-    depth = rows.shape[1]
-    if extra is not None:
-        spread = extra.reshape(count, 1, -1)
-        spread = jnp.pad(spread, ((0, 0), (0, 0), (0, lanes - spread.shape[2])))
-        rows = jnp.concatenate([rows, spread], axis=1)
     parts = lax.all_to_all(rows, axis, 0, 0)
     running = lax.cumsum(parts, axis=0, reverse=backward)
     empty = jnp.zeros_like(running[:1])
@@ -27,15 +22,17 @@
         shifted = jnp.concatenate([running[1:], empty], axis=0)
     else:
         shifted = jnp.concatenate([empty, running[:-1]], axis=0)
-    if extra is not None:
-        total = running[-1:] if not backward else running[:1]
-        row = lax.broadcasted_iota(jnp.int32, shifted.shape, 1)
-        shifted = jnp.where(row < depth, shifted, total)
     back = lax.all_to_all(shifted, axis, 0, 0)
-    state = back[:, :depth].reshape(value.shape)
-    if extra is None:
-        return state
-    return state, back[:, depth, : extra.size // count].reshape(extra.shape)
+    return back.reshape(value.shape)
+
+
+def butterfly_sum(value, axis):
+    count = lax.axis_size(axis)
+    step = 1
+    while step < count:
+        value = value + lax.ppermute(value, axis, [(i, i ^ step) for i in range(count)])
+        step *= 2
+    return value
 
 
 def lower_mask(length):
@@ -81,10 +78,10 @@
     query_parts = jnp.einsum(
         "nchd,nche->nhde", queries, grad_blocks, preferred_element_type=jnp.float32
     )
-    suffix, gain_seq = carried_in(jnp.sum(query_parts, axis=0), "seq", True, gain_terms)
-    grad_gain = lax.psum(gain_seq, "dp")
-    from_end = jnp.cumsum(query_parts[::-1], axis=0)[::-1]
-    behind = jnp.concatenate([from_end[1:], jnp.zeros_like(query_parts)], axis=0)
+    suffix = carried_in(jnp.sum(query_parts, axis=0), "seq", True)
+    grad_gain = butterfly_sum(butterfly_sum(gain_terms, "dp"), "seq")
+    from_end = lax.cumsum(query_parts, axis=0, reverse=True)
+    behind = jnp.concatenate([from_end[1:], query_parts[-1:] * 0.0], axis=0)
     suffix_states = (suffix[None] + behind).astype(jnp.bfloat16)
     grad_scores = jnp.einsum(
         "nche,nthe->nhct", grad_blocks, value_blocks, preferred_element_type=jnp.float32

time: 162 us -> 147 us (0.907)
  the two profiles are of different devices: /device:TPU:1 before, /device:TPU:16 now
where the time goes in v1:
time: 147 us
  waiting for transfers between devices  44.9 us (31%)
  blocking collectives  34 us (23%)
  starting transfers between devices  28.8 us (20%)
  local copies, waits for them, and re-layouts  14.1 us (10%)
  matrix products  12.3 us (8%)
  other arithmetic  11.5 us (8%)
    all_to_all x1, blocking collectives, carried_in(): parts = lax.all_to_all(rows, axis, 0, 0)  34 us
    ppermute x8, waiting for transfers between devices, butterfly_sum(): lax.ppermute(value, axis, [(i, i ^ step) for i in range(count)])  18.9 us
    all_to_all x2, waiting for transfers between devices, carried_in(): back = lax.all_to_all(shifted, axis, 0, 0)  16.2 us
    ppermute x8, starting transfers between devices, butterfly_sum(): lax.ppermute(value, axis, [(i, i ^ step) for i in range(count)])  13.5 us
    unnamed x34, local copies, waits for them, and re-layouts  12.1 us
    all_to_all x2, starting transfers between devices, carried_in(): back = lax.all_to_all(shifted, axis, 0, 0)  10.2 us
    all_to_all x1, waiting for transfers between devices, carried_in(): parts = lax.all_to_all(rows, axis, 0, 0)  9.85 us
    all_to_all x1, starting transfers between devices, carried_in(): parts = lax.all_to_all(rows, axis, 0, 0)  5.14 us
  transfers between devices with their start and end apart: 11, of which 8 were waited for; matrix products, arithmetic and copies ran while one was open for 12% of the time, Pallas kernels for 0%

profile of v1, /device:TPU:16, one launch (start us, length us, event | category | flops | bytes accessed | tf_op | source)
XLA Modules:
  0.0 146.6 jit_solution(18407745339282803398)
XLA Ops:
  0.6 1.5 %copy.32 = bf16[1,256,1536]{1,2,0:T(8,128)(2,1)S(1)} copy(bf16[1,256,1536]{2,1,0:T(8,128)(2,1)} %param.6) | data formatting | bytes 1572864 | tf_op args[1]
  2.8 34.0 %all_to_all.20 = f32[32,48,128]{2,1,0:T(8,128)S(1)} all-to-all(f32[32,48,128]{2,1,0:T(8,128)S(1)} %bitcast.100), channel_id=1, replica_groups=mesh['dp'=8,'seq'=32] {'seq'}, dimensions={0} | all-to-all | bytes 1572864 | tf_op jit(solution)/shard_map/all_to_all | solution.py:18
  36.8 3.2 %fusion.11 = f32[32,48,128]{2,1,0:T(8,128)S(1)} fusion(f32[32,48,128]{2,1,0:T(8,128)S(1)} %all_to_all.20), kind=kOutput, calls=%fused_computation.27 | output fusion | flops 6094848 | bytes 1572864 | tf_op jit(solution)/shard_map/carried_in/reduce_window_sum | solution.py:19
  41.0 5.3 %all-to-all-start.1 = ((f32[32,48,128]{2,1,0:T(8,128)}), f32[32,48,128]{2,1,0:T(8,128)}, u32[]{:S(2)}, u32[]{:S(2)}) async-start(f32[32,48,128]{2,1,0:T(8,128)} %concatenate.6), calls=%async_computation.1 | async-start | bytes 1572864 | tf_op jit(solution)/shard_map/all_to_all | solution.py:25
  46.5 1.7 %copy.35 = bf16[1,256,1536]{1,2,0:T(8,128)(2,1)S(1)} copy(bf16[1,256,1536]{2,1,0:T(8,128)(2,1)} %param.5) | data formatting | bytes 1572864 | tf_op args[0]
  50.1 1.8 %fusion.14 = f32[12,256,128]{1,2,0:T(8,128)} fusion(bf16[12,256,256]{2,1,0:T(8,128)(2,1)S(1)} %select_convert_fusion.1, bf16[256,12,128]{0,2,1:T(8,128)(2,1)S(1)} %bitcast.84), kind=kOutput, calls=%fused_computation.30 | convolution fusion | flops 201326592 | bytes 3932160 | tf_op jit(solution)/shard_map/nhct,nthe->nche/dot_general | solution.py:64
  51.9 16.2 %all-to-all-done.1 = f32[32,48,128]{2,1,0:T(8,128)} async-done(((f32[32,48,128]{2,1,0:T(8,128)}), f32[32,48,128]{2,1,0:T(8,128)}, u32[]{:S(2)}, u32[]{:S(2)}) %all-to-all-start.1) | async-done | bytes 786464 | tf_op jit(solution)/shard_map/all_to_all | solution.py:25
  68.1 1.6 %add_convert_fusion.1 = bf16[12,128,128]{2,1,0:T(8,128)(2,1)S(1)} fusion(f32[12,128,128]{2,1,0:T(8,128)} %bitcast.3, f32[12,128,128]{2,1,0:T(8,128)} %copy-done.3), kind=kLoop, calls=%fused_computation.23 | loop fusion | flops 589824 | bytes 1966080 | tf_op jit(solution)/shard_map/convert_element_type | solution.py:60
  71.4 2.5 %fusion.4 = (bf16[1,256,1536]{1,2,0:T(8,128)(2,1)S(1)}, bf16[1,256,1536]{1,2,0:T(8,128)(2,1)}) fusion(bf16[1,256,1536]{1,2,0:T(8,128)(2,1)} %copy-done.1, f32[12,128,256]{2,1,0:T(8,128)S(1)} %get-tuple-element.20, f32[256]{0:T(256)S(1)} %broadcast_multiply_fusion, f32[1536]{0:T(1024)S(1)} %copy-done.12, f32[256]{0:T(256)S(1)} %add_rsqrt_fusion), kind=kLoop, calls=%fused_computation.8 | loop fusion | flops 3538944 | bytes 3940352 | tf_op jit(solution)/shard_map/convert_element_type | solution.py:77
  75.2 5.1 %all-to-all-start.2 = ((f32[32,48,128]{2,1,0:T(8,128)}), f32[32,48,128]{2,1,0:T(8,128)}, u32[]{:S(2)}, u32[]{:S(2)}) async-start(f32[32,48,128]{2,1,0:T(8,128)} %bitcast.99), calls=%async_computation.2 | async-start | bytes 1572864 | tf_op jit(solution)/shard_map/all_to_all | solution.py:18
  82.8 2.4 %collective-permute-done.1 = f32[1536]{0:T(1024)S(1)} collective-permute-done((f32[1536]{0:T(1024)S(1)}, f32[1536]{0:T(1024)S(1)}, u32[]{:S(2)}, u32[]{:S(2)}) %collective-permute-start.1) | collective-permute-done | bytes 6176 | tf_op jit(solution)/shard_map/ppermute | solution.py:33
  85.6 4.8 %collective-permute-done.2 = f32[1536]{0:T(1024)S(1)} collective-permute-done((f32[1536]{0:T(1024)S(1)}, f32[1536]{0:T(1024)S(1)}, u32[]{:S(2)}, u32[]{:S(2)}) %collective-permute-start.2) | collective-permute-done | bytes 6176 | tf_op jit(solution)/shard_map/ppermute | solution.py:33
  90.4 1.7 %collective-permute-start.3 = (f32[1536]{0:T(1024)S(1)}, f32[1536]{0:T(1024)S(1)}, u32[]{:S(2)}, u32[]{:S(2)}) collective-permute-start(f32[1536]{0:T(1024)S(1)} %add.83), channel_id=1, source_target_pairs={{0,1},{1,0},{2,3},{3,2},{4,5},{5,4},{6,7},{7,6},{8,9},{9,8},{10,11... | collective-permute-start | bytes 18440 | tf_op jit(solution)/shard_map/ppermute | solution.py:33
  92.1 9.8 %all-to-all-done.2 = f32[32,48,128]{2,1,0:T(8,128)} async-done(((f32[32,48,128]{2,1,0:T(8,128)}), f32[32,48,128]{2,1,0:T(8,128)}, u32[]{:S(2)}, u32[]{:S(2)}) %all-to-all-start.2) | async-done | bytes 786464 | tf_op jit(solution)/shard_map/all_to_all | solution.py:18
  102.0 1.5 %fusion.12 = f32[32,48,128]{2,1,0:T(8,128)S(1)} fusion(f32[32,48,128]{2,1,0:T(8,128)} %all-to-all-done.2), kind=kOutput, calls=%fused_computation.28 | output fusion | flops 6094848 | bytes 1572864 | tf_op jit(solution)/shard_map/carried_in/reduce_window_sum | solution.py:19
  104.5 4.9 %all-to-all-start.3 = ((f32[32,48,128]{2,1,0:T(8,128)}), f32[32,48,128]{2,1,0:T(8,128)}, u32[]{:S(2)}, u32[]{:S(2)}) async-start(f32[32,48,128]{2,1,0:T(8,128)} %concatenate.7), calls=%async_computation.3 | async-start | bytes 1572864 | tf_op jit(solution)/shard_map/all_to_all | solution.py:25
  109.4 3.0 %fusion.17 = f32[12,128,256]{2,1,0:T(8,128)} fusion(bf16[256,12,128]{0,2,1:T(8,128)(2,1)S(1)} %bitcast.92, bf16[12,256,256]{2,1,0:T(8,128)(2,1)} %copy-done), kind=kOutput, calls=%fused_computation.33 | convolution fusion | flops 201326592 | bytes 3932160 | tf_op jit(solution)/shard_map/nhct,nche->nthe/dot_general | solution.py:105
  112.4 3.2 %collective-permute-start.4 = (f32[1536]{0:T(1024)S(1)}, f32[1536]{0:T(1024)S(1)}, u32[]{:S(2)}, u32[]{:S(2)}) collective-permute-start(f32[1536]{0:T(1024)S(1)} %add.84), channel_id=1, source_target_pairs={{0,2},{1,3},{2,0},{3,1},{4,6},{5,7},{6,4},{7,5},{8,10},{9,11},{10,... | collective-permute-start | bytes 18440 | tf_op jit(solution)/shard_map/ppermute | solution.py:33
  117.6 1.8 %collective-permute-start.5 = (f32[1536]{0:T(1024)S(1)}, f32[1536]{0:T(1024)S(1)}, u32[]{:S(2)}, u32[]{:S(2)}) collective-permute-start(f32[1536]{0:T(1024)S(1)} %add.85), channel_id=1, source_target_pairs={{0,4},{1,5},{2,6},{3,7},{4,0},{5,1},{6,2},{7,3},{8,12},{9,13},{10,... | collective-permute-start | bytes 18440 | tf_op jit(solution)/shard_map/ppermute | solution.py:33
  119.4 1.6 %fusion.18 = f32[12,256,128]{1,2,0:T(8,128)} fusion(bf16[256,12,128]{0,2,1:T(8,128)(2,1)S(1)} %bitcast.98, bf16[12,256,256]{2,1,0:T(8,128)(2,1)S(1)} %select_convert_fusion), kind=kOutput, calls=%fused_computation.34 | convolution fusion | flops 201326592 | bytes 3932160 | tf_op jit(solution)/shard_map/nhct,nchd->nthd/dot_general | solution.py:99
  121.0 5.8 %collective-permute-done.5 = f32[1536]{0:T(1024)S(1)} collective-permute-done((f32[1536]{0:T(1024)S(1)}, f32[1536]{0:T(1024)S(1)}, u32[]{:S(2)}, u32[]{:S(2)}) %collective-permute-start.5) | collective-permute-done | bytes 6176 | tf_op jit(solution)/shard_map/ppermute | solution.py:33
  127.9 3.4 %collective-permute-done.6 = f32[1536]{0:T(1024)S(1)} collective-permute-done((f32[1536]{0:T(1024)S(1)}, f32[1536]{0:T(1024)S(1)}, u32[]{:S(2)}, u32[]{:S(2)}) %collective-permute-start.6) | collective-permute-done | bytes 6176 | tf_op jit(solution)/shard_map/ppermute | solution.py:33
  131.4 4.5 %collective-permute-start.7 = (f32[1536]{0:T(1024)S(1)}, f32[1536]{0:T(1024)S(1)}, u32[]{:S(2)}, u32[]{:S(2)}) collective-permute-start(f32[1536]{0:T(1024)S(1)} %add.87), channel_id=1, source_target_pairs={{0,16},{1,17},{2,18},{3,19},{4,20},{5,21},{6,22},{7,23},{8,24},{9,... | collective-permute-start | bytes 18440 | tf_op jit(solution)/shard_map/ppermute | solution.py:33
  137.1 2.4 %copy.48 = bf16[1,256,1536]{2,1,0:T(8,128)(2,1)} copy(bf16[1,256,1536]{1,2,0:T(8,128)(2,1)} %get-tuple-element.18) | data formatting | bytes 1572864
  (66 shorter events, 21.9 us)
Async XLA Ops:
  0.6 1.5 %copy-start.8 = (bf16[1,256,1536]{2,1,0:T(8,128)(2,1)S(1)}, bf16[1,256,1536]{2,1,0:T(8,128)(2,1)}, u32[]{:S(2)}) copy-start(bf16[1,256,1536]{2,1,0:T(8,128)(2,1)} %param.7) | copy-start | bytes 2359300
  2.8 37.2 %copy-start.3 = (f32[12,128,128]{2,1,0:T(8,128)}, f32[12,128,128]{2,1,0:T(8,128)S(1)}, u32[]{:S(2)}) copy-start(f32[12,128,128]{2,1,0:T(8,128)S(1)} %fusion.13) | copy-start | bytes 2359300
  40.0 6.2 %copy-start.9 = (bf16[1,256,1536]{2,1,0:T(8,128)(2,1)S(1)}, bf16[1,256,1536]{2,1,0:T(8,128)(2,1)}, u32[]{:S(2)}) copy-start(bf16[1,256,1536]{2,1,0:T(8,128)(2,1)} %param.9) | copy-start | bytes 2359300
  41.0 27.1 %all-to-all-start.1 = ((f32[32,48,128]{2,1,0:T(8,128)}), f32[32,48,128]{2,1,0:T(8,128)}, u32[]{:S(2)}, u32[]{:S(2)}) async-start(f32[32,48,128]{2,1,0:T(8,128)} %concatenate.6), calls=%async_computation.1 | async-start | bytes 1572864 | tf_op jit(solution)/shard_map/all_to_all | solution.py:25
  46.5 23.9 %copy-start.1 = (bf16[1,256,1536]{1,2,0:T(8,128)(2,1)}, bf16[1,256,1536]{1,2,0:T(8,128)(2,1)S(1)}, u32[]{:S(2)}) copy-start(bf16[1,256,1536]{1,2,0:T(8,128)(2,1)S(1)} %copy.40) | copy-start | bytes 2359300
  48.3 0.7 copy-start.10
  48.9 1.2 copy-start
  68.1 1.9 %copy-start.6 = (f32[12,256,128]{1,2,0:T(8,128)S(1)}, f32[12,256,128]{1,2,0:T(8,128)}, u32[]{:S(2)}) copy-start(f32[12,256,128]{1,2,0:T(8,128)} %fusion.14) | copy-start | bytes 4718596
  69.9 0.7 copy-start.12
  75.2 26.8 %all-to-all-start.2 = ((f32[32,48,128]{2,1,0:T(8,128)}), f32[32,48,128]{2,1,0:T(8,128)}, u32[]{:S(2)}, u32[]{:S(2)}) async-start(f32[32,48,128]{2,1,0:T(8,128)} %bitcast.99), calls=%async_computation.2 | async-start | bytes 1572864 | tf_op jit(solution)/shard_map/all_to_all | solution.py:18
  80.3 1.3 collective-permute-start
  81.6 3.7 %collective-permute-start.1 = (f32[1536]{0:T(1024)S(1)}, f32[1536]{0:T(1024)S(1)}, u32[]{:S(2)}, u32[]{:S(2)}) collective-permute-start(f32[1536]{0:T(1024)S(1)} %add.81), channel_id=1, source_target_pairs={{0,64},{32,96},{64,0},{96,32},{128,192},{160,224},{192,128},{224,1... | collective-permute-start | bytes 18440 | tf_op jit(solution)/shard_map/ppermute | solution.py:33
  85.2 5.2 %collective-permute-start.2 = (f32[1536]{0:T(1024)S(1)}, f32[1536]{0:T(1024)S(1)}, u32[]{:S(2)}, u32[]{:S(2)}) collective-permute-start(f32[1536]{0:T(1024)S(1)} %add.82), channel_id=1, source_target_pairs={{0,128},{32,160},{64,192},{96,224},{128,0},{160,32},{192,64},{224,... | collective-permute-start | bytes 18440 | tf_op jit(solution)/shard_map/ppermute | solution.py:33
  90.4 22.0 %collective-permute-start.3 = (f32[1536]{0:T(1024)S(1)}, f32[1536]{0:T(1024)S(1)}, u32[]{:S(2)}, u32[]{:S(2)}) collective-permute-start(f32[1536]{0:T(1024)S(1)} %add.83), channel_id=1, source_target_pairs={{0,1},{1,0},{2,3},{3,2},{4,5},{5,4},{6,7},{7,6},{8,9},{9,8},{10,11... | collective-permute-start | bytes 18440 | tf_op jit(solution)/shard_map/ppermute | solution.py:33
  104.5 36.8 %all-to-all-start.3 = ((f32[32,48,128]{2,1,0:T(8,128)}), f32[32,48,128]{2,1,0:T(8,128)}, u32[]{:S(2)}, u32[]{:S(2)}) async-start(f32[32,48,128]{2,1,0:T(8,128)} %concatenate.7), calls=%async_computation.3 | async-start | bytes 1572864 | tf_op jit(solution)/shard_map/all_to_all | solution.py:25
  109.4 6.2 %copy-start.11 = (pred[256,256]{1,0:T(8,128)(4,1)S(1)}, pred[256,256]{1,0:T(8,128)(4,1)}, u32[]{:S(2)}) copy-start(pred[256,256]{1,0:T(8,128)(4,1)} %copy-done.10) | copy-start | bytes 196612
  112.4 5.2 %collective-permute-start.4 = (f32[1536]{0:T(1024)S(1)}, f32[1536]{0:T(1024)S(1)}, u32[]{:S(2)}, u32[]{:S(2)}) collective-permute-start(f32[1536]{0:T(1024)S(1)} %add.84), channel_id=1, source_target_pairs={{0,2},{1,3},{2,0},{3,1},{4,6},{5,7},{6,4},{7,5},{8,10},{9,11},{10,... | collective-permute-start | bytes 18440 | tf_op jit(solution)/shard_map/ppermute | solution.py:33
  117.6 9.2 %collective-permute-start.5 = (f32[1536]{0:T(1024)S(1)}, f32[1536]{0:T(1024)S(1)}, u32[]{:S(2)}, u32[]{:S(2)}) collective-permute-start(f32[1536]{0:T(1024)S(1)} %add.85), channel_id=1, source_target_pairs={{0,4},{1,5},{2,6},{3,7},{4,0},{5,1},{6,2},{7,3},{8,12},{9,13},{10,... | collective-permute-start | bytes 18440 | tf_op jit(solution)/shard_map/ppermute | solution.py:33
  126.8 4.6 %collective-permute-start.6 = (f32[1536]{0:T(1024)S(1)}, f32[1536]{0:T(1024)S(1)}, u32[]{:S(2)}, u32[]{:S(2)}) collective-permute-start(f32[1536]{0:T(1024)S(1)} %add.86), channel_id=1, source_target_pairs={{0,8},{1,9},{2,10},{3,11},{4,12},{5,13},{6,14},{7,15},{8,0},{9,1},... | collective-permute-start | bytes 18440 | tf_op jit(solution)/shard_map/ppermute | solution.py:33
  131.4 9.3 %collective-permute-start.7 = (f32[1536]{0:T(1024)S(1)}, f32[1536]{0:T(1024)S(1)}, u32[]{:S(2)}, u32[]{:S(2)}) collective-permute-start(f32[1536]{0:T(1024)S(1)} %add.87), channel_id=1, source_target_pairs={{0,16},{1,17},{2,18},{3,19},{4,20},{5,21},{6,22},{7,23},{8,24},{9,... | collective-permute-start | bytes 18440 | tf_op jit(solution)/shard_map/ppermute | solution.py:33
  137.1 2.4 %copy-start.7 = (bf16[12,128,256]{2,1,0:T(8,128)(2,1)S(1)}, bf16[12,128,256]{2,1,0:T(8,128)(2,1)}, u32[]{:S(2)}) copy-start(bf16[12,128,256]{2,1,0:T(8,128)(2,1)} %fusion.7) | copy-start | bytes 2359300
  137.1 4.2 %copy-start.2 = (f32[12,128,128]{1,2,0:T(8,128)S(1)}, f32[12,128,128]{1,2,0:T(8,128)}, u32[]{:S(2)}) copy-start(f32[12,128,128]{1,2,0:T(8,128)} %fusion.16) | copy-start | bytes 2359300
  141.3 1.6 %copy-start.4 = (f32[12,128,256]{2,1,0:T(8,128)S(1)}, f32[12,128,256]{2,1,0:T(8,128)}, u32[]{:S(2)}) copy-start(f32[12,128,256]{2,1,0:T(8,128)} %fusion.17) | copy-start | bytes 4718596
  143.3 1.7 %copy-start.5 = (f32[12,256,128]{1,2,0:T(8,128)S(1)}, f32[12,256,128]{1,2,0:T(8,128)}, u32[]{:S(2)}) copy-start(f32[12,256,128]{1,2,0:T(8,128)} %fusion.18) | copy-start | bytes 4718596

commit v2 on v1

--- a/solution.py
+++ b/solution.py
@@ -16,20 +16,25 @@
     lanes = value.shape[-1]
     rows = value.reshape(count, -1, lanes)
     parts = lax.all_to_all(rows, axis, 0, 0)
-    running = lax.cumsum(parts, axis=0, reverse=backward)
-    empty = jnp.zeros_like(running[:1])
-    if backward:
-        shifted = jnp.concatenate([running[1:], empty], axis=0)
-    else:
-        shifted = jnp.concatenate([empty, running[:-1]], axis=0)
+    row = lax.broadcasted_iota(jnp.int32, (count, count), 0)
+    col = lax.broadcasted_iota(jnp.int32, (count, count), 1)
+    strict = (row < col) if backward else (row > col)
+    shifted = jnp.einsum(
+        "ij,jkl->ikl",
+        strict.astype(jnp.float32),
+        parts,
+        precision=lax.Precision.HIGHEST,
+        preferred_element_type=jnp.float32,
+    )
     back = lax.all_to_all(shifted, axis, 0, 0)
     return back.reshape(value.shape)
 
 
-def butterfly_sum(value, axis):
+def butterfly_sum(value, axis, first=1, last=None):
     count = lax.axis_size(axis)
-    step = 1
-    while step < count:
+    last = count if last is None else last
+    step = first
+    while step < last:
         value = value + lax.ppermute(value, axis, [(i, i ^ step) for i in range(count)])
         step *= 2
     return value
@@ -79,7 +84,8 @@
         "nchd,nche->nhde", queries, grad_blocks, preferred_element_type=jnp.float32
     )
     suffix = carried_in(jnp.sum(query_parts, axis=0), "seq", True)
-    grad_gain = butterfly_sum(butterfly_sum(gain_terms, "dp"), "seq")
+    gain_near = butterfly_sum(butterfly_sum(gain_terms, "dp"), "seq", 1, 4)
+    grad_gain = butterfly_sum(gain_near, "seq", 4)
     from_end = lax.cumsum(query_parts, axis=0, reverse=True)
     behind = jnp.concatenate([from_end[1:], query_parts[-1:] * 0.0], axis=0)
     suffix_states = (suffix[None] + behind).astype(jnp.bfloat16)

time: 147 us -> 146 us (level)
  other arithmetic: 11.5 us -> 6.82 us
  matrix products: 12.3 us -> 14.9 us
    another operation x2 -> x0, other arithmetic: 4.72 us -> none  [carried_in(): running = lax.cumsum(parts, axis=0, reverse=backward)]
    dot_general x0 -> x2, local copies, waits for them, and re-layouts: none -> 2.69 us  [carried_in(): jnp.einsum('ij,jkl->ikl', strict.astype(jnp.float32), parts, precision=la...]
    dot_general x0 -> x2, matrix products: none -> 2.65 us  [carried_in(): jnp.einsum('ij,jkl->ikl', strict.astype(jnp.float32), parts, precision=la...]
    concatenate x2 -> x0, local copies, waits for them, and re-layouts: 1.89 us -> none  [the longest x1 0.96 us: carried_in(): shifted = jnp.concatenate([running[1:], empty], axis=0)]
  transfers between devices with their start and end apart: 11 -> 11, of which waited for: 8 -> 8; matrix products, arithmetic and copies ran while one was open for 12% -> 13% of each run, Pallas kernels for 0% -> 0%
where the time goes in v2:
time: 146 us; the launch traced here: 145 us
  waiting for transfers between devices  44.9 us (31%)
  blocking collectives  34 us (23%)
  starting transfers between devices  28.9 us (20%)
  matrix products  14.9 us (10%)
  local copies, waits for them, and re-layouts  14.8 us (10%)
  other arithmetic  6.82 us (5%)
    all_to_all x1, blocking collectives, carried_in(): parts = lax.all_to_all(rows, axis, 0, 0)  34 us
    ppermute x8, waiting for transfers between devices, butterfly_sum(): lax.ppermute(value, axis, [(i, i ^ step) for i in range(count)])  18.9 us
    all_to_all x2, waiting for transfers between devices, carried_in(): back = lax.all_to_all(shifted, axis, 0, 0)  16.2 us
    ppermute x8, starting transfers between devices, butterfly_sum(): lax.ppermute(value, axis, [(i, i ^ step) for i in range(count)])  13.5 us
    unnamed x34, local copies, waits for them, and re-layouts  12.1 us
    all_to_all x2, starting transfers between devices, carried_in(): back = lax.all_to_all(shifted, axis, 0, 0)  10.3 us
    all_to_all x1, waiting for transfers between devices, carried_in(): parts = lax.all_to_all(rows, axis, 0, 0)  9.85 us
    all_to_all x1, starting transfers between devices, carried_in(): parts = lax.all_to_all(rows, axis, 0, 0)  5.14 us
  transfers between devices with their start and end apart: 11, of which 8 were waited for; matrix products, arithmetic and copies ran while one was open for 13% of the time, Pallas kernels for 0%

profile of v2, /device:TPU:16, one launch (start us, length us, event | category | flops | bytes accessed | tf_op | source)
XLA Modules:
  0.0 145.3 jit_solution(6291096167966552822)
XLA Ops:
  0.6 1.5 %copy.60 = bf16[1,256,1536]{1,2,0:T(8,128)(2,1)S(1)} copy(bf16[1,256,1536]{2,1,0:T(8,128)(2,1)} %param.6) | data formatting | bytes 1572864 | tf_op args[1]
  2.8 34.0 %all_to_all.20 = f32[32,48,128]{2,1,0:T(8,128)S(1)} all-to-all(f32[32,48,128]{2,1,0:T(8,128)S(1)} %bitcast.104), channel_id=1, replica_groups=mesh['dp'=8,'seq'=32] {'seq'}, dimensions={0} | all-to-all | bytes 1572864 | tf_op jit(solution)/shard_map/all_to_all | solution.py:18
  38.9 5.4 %all-to-all-start.1 = ((f32[32,48,128]{2,1,0:T(8,128)}), f32[32,48,128]{2,1,0:T(8,128)}, u32[]{:S(2)}, u32[]{:S(2)}) async-start(f32[32,48,128]{2,1,0:T(8,128)} %copy.64), calls=%async_computation.1 | async-start | bytes 1572864 | tf_op jit(solution)/shard_map/all_to_all | solution.py:29
  44.6 1.7 %copy.65 = bf16[1,256,1536]{1,2,0:T(8,128)(2,1)S(1)} copy(bf16[1,256,1536]{2,1,0:T(8,128)(2,1)} %param.5) | data formatting | bytes 1572864 | tf_op args[0]
  48.2 1.8 %fusion.20 = f32[12,256,128]{1,2,0:T(8,128)} fusion(bf16[12,256,256]{2,1,0:T(8,128)(2,1)S(1)} %select_convert_fusion.1, bf16[256,12,128]{0,2,1:T(8,128)(2,1)S(1)} %bitcast.88), kind=kOutput, calls=%fused_computation.36 | convolution fusion | flops 201326592 | bytes 3932160 | tf_op jit(solution)/shard_map/nhct,nthe->nche/dot_general | solution.py:69
  49.9 16.2 %all-to-all-done.1 = f32[32,48,128]{2,1,0:T(8,128)} async-done(((f32[32,48,128]{2,1,0:T(8,128)}), f32[32,48,128]{2,1,0:T(8,128)}, u32[]{:S(2)}, u32[]{:S(2)}) %all-to-all-start.1) | async-done | bytes 786464 | tf_op jit(solution)/shard_map/all_to_all | solution.py:29
  66.1 1.6 %add_convert_fusion.1 = bf16[12,128,128]{2,1,0:T(8,128)(2,1)S(1)} fusion(f32[12,128,128]{2,1,0:T(8,128)} %bitcast.4, f32[12,128,128]{2,1,0:T(8,128)} %copy-done.3), kind=kLoop, calls=%fused_computation.27 | loop fusion | flops 589824 | bytes 1966080 | tf_op jit(solution)/shard_map/convert_element_type | solution.py:65
  69.5 2.5 %fusion.4 = (bf16[1,256,1536]{1,2,0:T(8,128)(2,1)S(1)}, bf16[1,256,1536]{1,2,0:T(8,128)(2,1)}) fusion(bf16[1,256,1536]{1,2,0:T(8,128)(2,1)} %copy-done.1, f32[12,128,256]{2,1,0:T(8,128)S(1)} %get-tuple-element.25, f32[256]{0:T(256)S(1)} %broadcast_multiply_fusion, f32[1536]{0:T(1024)S(1)} %copy-done.12, f32[256]{0:T(256)S(1)} %add_rsqrt_fusion), kind=kLoop, calls=%fused_computation.8 | loop fusion | flops 3538944 | bytes 3940352 | tf_op jit(solution)/shard_map/convert_element_type | solution.py:82
  73.2 5.1 %all-to-all-start.2 = ((f32[32,48,128]{2,1,0:T(8,128)}), f32[32,48,128]{2,1,0:T(8,128)}, u32[]{:S(2)}, u32[]{:S(2)}) async-start(f32[32,48,128]{2,1,0:T(8,128)} %bitcast.103), calls=%async_computation.2 | async-start | bytes 1572864 | tf_op jit(solution)/shard_map/all_to_all | solution.py:18
  80.9 2.4 %collective-permute-done.1 = f32[1536]{0:T(1024)S(1)} collective-permute-done((f32[1536]{0:T(1024)S(1)}, f32[1536]{0:T(1024)S(1)}, u32[]{:S(2)}, u32[]{:S(2)}) %collective-permute-start.1) | collective-permute-done | bytes 6176 | tf_op jit(solution)/shard_map/ppermute | solution.py:38
  83.6 4.8 %collective-permute-done.2 = f32[1536]{0:T(1024)S(1)} collective-permute-done((f32[1536]{0:T(1024)S(1)}, f32[1536]{0:T(1024)S(1)}, u32[]{:S(2)}, u32[]{:S(2)}) %collective-permute-start.2) | collective-permute-done | bytes 6176 | tf_op jit(solution)/shard_map/ppermute | solution.py:38
  88.4 1.7 %collective-permute-start.3 = (f32[1536]{0:T(1024)S(1)}, f32[1536]{0:T(1024)S(1)}, u32[]{:S(2)}, u32[]{:S(2)}) collective-permute-start(f32[1536]{0:T(1024)S(1)} %add.79), channel_id=1, source_target_pairs={{0,1},{1,0},{2,3},{3,2},{4,5},{5,4},{6,7},{7,6},{8,9},{9,8},{10,11... | collective-permute-start | bytes 18440 | tf_op jit(solution)/shard_map/ppermute | solution.py:38
  90.1 9.8 %all-to-all-done.2 = f32[32,48,128]{2,1,0:T(8,128)} async-done(((f32[32,48,128]{2,1,0:T(8,128)}), f32[32,48,128]{2,1,0:T(8,128)}, u32[]{:S(2)}, u32[]{:S(2)}) %all-to-all-start.2) | async-done | bytes 786464 | tf_op jit(solution)/shard_map/all_to_all | solution.py:18
  100.0 1.9 %fusion.11 = f32[32,48,128]{2,0,1:T(8,128)S(1)} fusion(f32[32,48,128]{2,1,0:T(8,128)} %all-to-all-done.2), kind=kOutput, calls=%fused_computation.23 | convolution fusion | flops 75498496 | bytes 1572864 | tf_op jit(solution)/shard_map/ij,jkl->ikl/dot_general | solution.py:22
  101.9 1.4 copy.76
  103.2 4.9 %all-to-all-start.3 = ((f32[32,48,128]{2,1,0:T(8,128)}), f32[32,48,128]{2,1,0:T(8,128)}, u32[]{:S(2)}, u32[]{:S(2)}) async-start(f32[32,48,128]{2,1,0:T(8,128)} %copy.76), calls=%async_computation.3 | async-start | bytes 1572864 | tf_op jit(solution)/shard_map/all_to_all | solution.py:29
  108.2 2.9 %fusion.23 = f32[12,128,256]{2,1,0:T(8,128)} fusion(bf16[256,12,128]{0,2,1:T(8,128)(2,1)S(1)} %bitcast.96, bf16[12,256,256]{2,1,0:T(8,128)(2,1)} %copy-done), kind=kOutput, calls=%fused_computation.39 | convolution fusion | flops 201326592 | bytes 3932160 | tf_op jit(solution)/shard_map/nhct,nche->nthe/dot_general | solution.py:111
  111.1 3.2 %collective-permute-start.4 = (f32[1536]{0:T(1024)S(1)}, f32[1536]{0:T(1024)S(1)}, u32[]{:S(2)}, u32[]{:S(2)}) collective-permute-start(f32[1536]{0:T(1024)S(1)} %add.80), channel_id=1, source_target_pairs={{0,2},{1,3},{2,0},{3,1},{4,6},{5,7},{6,4},{7,5},{8,10},{9,11},{10,... | collective-permute-start | bytes 18440 | tf_op jit(solution)/shard_map/ppermute | solution.py:38
  116.3 1.8 %collective-permute-start.5 = (f32[1536]{0:T(1024)S(1)}, f32[1536]{0:T(1024)S(1)}, u32[]{:S(2)}, u32[]{:S(2)}) collective-permute-start(f32[1536]{0:T(1024)S(1)} %add.81), channel_id=1, source_target_pairs={{0,4},{1,5},{2,6},{3,7},{4,0},{5,1},{6,2},{7,3},{8,12},{9,13},{10,... | collective-permute-start | bytes 18440 | tf_op jit(solution)/shard_map/ppermute | solution.py:38
  118.1 1.6 %fusion.24 = f32[12,256,128]{1,2,0:T(8,128)} fusion(bf16[256,12,128]{0,2,1:T(8,128)(2,1)S(1)} %bitcast.102, bf16[12,256,256]{2,1,0:T(8,128)(2,1)S(1)} %select_convert_fusion), kind=kOutput, calls=%fused_computation.40 | convolution fusion | flops 201326592 | bytes 3932160 | tf_op jit(solution)/shard_map/nhct,nchd->nthd/dot_general | solution.py:105
  119.7 5.8 %collective-permute-done.5 = f32[1536]{0:T(1024)S(1)} collective-permute-done((f32[1536]{0:T(1024)S(1)}, f32[1536]{0:T(1024)S(1)}, u32[]{:S(2)}, u32[]{:S(2)}) %collective-permute-start.5) | collective-permute-done | bytes 6176 | tf_op jit(solution)/shard_map/ppermute | solution.py:38
  126.7 3.4 %collective-permute-done.6 = f32[1536]{0:T(1024)S(1)} collective-permute-done((f32[1536]{0:T(1024)S(1)}, f32[1536]{0:T(1024)S(1)}, u32[]{:S(2)}, u32[]{:S(2)}) %collective-permute-start.6) | collective-permute-done | bytes 6176 | tf_op jit(solution)/shard_map/ppermute | solution.py:38
  130.1 4.5 %collective-permute-start.7 = (f32[1536]{0:T(1024)S(1)}, f32[1536]{0:T(1024)S(1)}, u32[]{:S(2)}, u32[]{:S(2)}) collective-permute-start(f32[1536]{0:T(1024)S(1)} %add.83), channel_id=1, source_target_pairs={{0,16},{1,17},{2,18},{3,19},{4,20},{5,21},{6,22},{7,23},{8,24},{9,... | collective-permute-start | bytes 18440 | tf_op jit(solution)/shard_map/ppermute | solution.py:38
  135.8 2.4 %copy.80 = bf16[1,256,1536]{2,1,0:T(8,128)(2,1)} copy(bf16[1,256,1536]{1,2,0:T(8,128)(2,1)} %get-tuple-element.23) | data formatting | bytes 1572864
  (64 shorter events, 22.0 us)
Async XLA Ops:
  0.6 1.5 %copy-start.8 = (bf16[1,256,1536]{2,1,0:T(8,128)(2,1)S(1)}, bf16[1,256,1536]{2,1,0:T(8,128)(2,1)}, u32[]{:S(2)}) copy-start(bf16[1,256,1536]{2,1,0:T(8,128)(2,1)} %param.7) | copy-start | bytes 2359300
  2.8 34.8 %copy-start.3 = (f32[12,128,128]{2,1,0:T(8,128)}, f32[12,128,128]{2,1,0:T(8,128)S(1)}, u32[]{:S(2)}) copy-start(f32[12,128,128]{2,1,0:T(8,128)S(1)} %fusion.19) | copy-start | bytes 2359300
  38.9 5.4 %copy-start.9 = (bf16[1,256,1536]{2,1,0:T(8,128)(2,1)S(1)}, bf16[1,256,1536]{2,1,0:T(8,128)(2,1)}, u32[]{:S(2)}) copy-start(bf16[1,256,1536]{2,1,0:T(8,128)(2,1)} %param.9) | copy-start | bytes 2359300
  38.9 27.2 %all-to-all-start.1 = ((f32[32,48,128]{2,1,0:T(8,128)}), f32[32,48,128]{2,1,0:T(8,128)}, u32[]{:S(2)}, u32[]{:S(2)}) async-start(f32[32,48,128]{2,1,0:T(8,128)} %copy.64), calls=%async_computation.1 | async-start | bytes 1572864 | tf_op jit(solution)/shard_map/all_to_all | solution.py:29
  44.6 23.9 %copy-start.1 = (bf16[1,256,1536]{1,2,0:T(8,128)(2,1)}, bf16[1,256,1536]{1,2,0:T(8,128)(2,1)S(1)}, u32[]{:S(2)}) copy-start(bf16[1,256,1536]{1,2,0:T(8,128)(2,1)S(1)} %copy.70) | copy-start | bytes 2359300
  46.3 0.7 copy-start.10
  47.0 1.2 copy-start
  66.1 1.9 %copy-start.6 = (f32[12,256,128]{1,2,0:T(8,128)S(1)}, f32[12,256,128]{1,2,0:T(8,128)}, u32[]{:S(2)}) copy-start(f32[12,256,128]{1,2,0:T(8,128)} %fusion.20) | copy-start | bytes 4718596
  68.0 0.7 copy-start.12
  73.2 26.8 %all-to-all-start.2 = ((f32[32,48,128]{2,1,0:T(8,128)}), f32[32,48,128]{2,1,0:T(8,128)}, u32[]{:S(2)}, u32[]{:S(2)}) async-start(f32[32,48,128]{2,1,0:T(8,128)} %bitcast.103), calls=%async_computation.2 | async-start | bytes 1572864 | tf_op jit(solution)/shard_map/all_to_all | solution.py:18
  78.3 1.3 collective-permute-start
  79.6 3.7 %collective-permute-start.1 = (f32[1536]{0:T(1024)S(1)}, f32[1536]{0:T(1024)S(1)}, u32[]{:S(2)}, u32[]{:S(2)}) collective-permute-start(f32[1536]{0:T(1024)S(1)} %add.77), channel_id=1, source_target_pairs={{0,64},{32,96},{64,0},{96,32},{128,192},{160,224},{192,128},{224,1... | collective-permute-start | bytes 18440 | tf_op jit(solution)/shard_map/ppermute | solution.py:38
  83.3 5.2 %collective-permute-start.2 = (f32[1536]{0:T(1024)S(1)}, f32[1536]{0:T(1024)S(1)}, u32[]{:S(2)}, u32[]{:S(2)}) collective-permute-start(f32[1536]{0:T(1024)S(1)} %add.78), channel_id=1, source_target_pairs={{0,128},{32,160},{64,192},{96,224},{128,0},{160,32},{192,64},{224,... | collective-permute-start | bytes 18440 | tf_op jit(solution)/shard_map/ppermute | solution.py:38
  88.4 22.7 %collective-permute-start.3 = (f32[1536]{0:T(1024)S(1)}, f32[1536]{0:T(1024)S(1)}, u32[]{:S(2)}, u32[]{:S(2)}) collective-permute-start(f32[1536]{0:T(1024)S(1)} %add.79), channel_id=1, source_target_pairs={{0,1},{1,0},{2,3},{3,2},{4,5},{5,4},{6,7},{7,6},{8,9},{9,8},{10,11... | collective-permute-start | bytes 18440 | tf_op jit(solution)/shard_map/ppermute | solution.py:38
  103.2 36.8 %all-to-all-start.3 = ((f32[32,48,128]{2,1,0:T(8,128)}), f32[32,48,128]{2,1,0:T(8,128)}, u32[]{:S(2)}, u32[]{:S(2)}) async-start(f32[32,48,128]{2,1,0:T(8,128)} %copy.76), calls=%async_computation.3 | async-start | bytes 1572864 | tf_op jit(solution)/shard_map/all_to_all | solution.py:29
  108.2 6.2 %copy-start.11 = (pred[256,256]{1,0:T(8,128)(4,1)S(1)}, pred[256,256]{1,0:T(8,128)(4,1)}, u32[]{:S(2)}) copy-start(pred[256,256]{1,0:T(8,128)(4,1)} %copy-done.10) | copy-start | bytes 196612
  111.1 5.2 %collective-permute-start.4 = (f32[1536]{0:T(1024)S(1)}, f32[1536]{0:T(1024)S(1)}, u32[]{:S(2)}, u32[]{:S(2)}) collective-permute-start(f32[1536]{0:T(1024)S(1)} %add.80), channel_id=1, source_target_pairs={{0,2},{1,3},{2,0},{3,1},{4,6},{5,7},{6,4},{7,5},{8,10},{9,11},{10,... | collective-permute-start | bytes 18440 | tf_op jit(solution)/shard_map/ppermute | solution.py:38
  116.3 9.2 %collective-permute-start.5 = (f32[1536]{0:T(1024)S(1)}, f32[1536]{0:T(1024)S(1)}, u32[]{:S(2)}, u32[]{:S(2)}) collective-permute-start(f32[1536]{0:T(1024)S(1)} %add.81), channel_id=1, source_target_pairs={{0,4},{1,5},{2,6},{3,7},{4,0},{5,1},{6,2},{7,3},{8,12},{9,13},{10,... | collective-permute-start | bytes 18440 | tf_op jit(solution)/shard_map/ppermute | solution.py:38
  125.5 4.5 %collective-permute-start.6 = (f32[1536]{0:T(1024)S(1)}, f32[1536]{0:T(1024)S(1)}, u32[]{:S(2)}, u32[]{:S(2)}) collective-permute-start(f32[1536]{0:T(1024)S(1)} %add.82), channel_id=1, source_target_pairs={{0,8},{1,9},{2,10},{3,11},{4,12},{5,13},{6,14},{7,15},{8,0},{9,1},... | collective-permute-start | bytes 18440 | tf_op jit(solution)/shard_map/ppermute | solution.py:38
  130.1 9.3 %collective-permute-start.7 = (f32[1536]{0:T(1024)S(1)}, f32[1536]{0:T(1024)S(1)}, u32[]{:S(2)}, u32[]{:S(2)}) collective-permute-start(f32[1536]{0:T(1024)S(1)} %add.83), channel_id=1, source_target_pairs={{0,16},{1,17},{2,18},{3,19},{4,20},{5,21},{6,22},{7,23},{8,24},{9,... | collective-permute-start | bytes 18440 | tf_op jit(solution)/shard_map/ppermute | solution.py:38
  135.8 2.4 %copy-start.7 = (bf16[12,128,256]{2,1,0:T(8,128)(2,1)S(1)}, bf16[12,128,256]{2,1,0:T(8,128)(2,1)}, u32[]{:S(2)}) copy-start(bf16[12,128,256]{2,1,0:T(8,128)(2,1)} %fusion.7) | copy-start | bytes 2359300
  135.8 4.2 %copy-start.2 = (f32[12,128,128]{1,2,0:T(8,128)S(1)}, f32[12,128,128]{1,2,0:T(8,128)}, u32[]{:S(2)}) copy-start(f32[12,128,128]{1,2,0:T(8,128)} %fusion.22) | copy-start | bytes 2359300
  140.0 1.6 %copy-start.4 = (f32[12,128,256]{2,1,0:T(8,128)S(1)}, f32[12,128,256]{2,1,0:T(8,128)}, u32[]{:S(2)}) copy-start(f32[12,128,256]{2,1,0:T(8,128)} %fusion.23) | copy-start | bytes 4718596
  142.1 1.7 %copy-start.5 = (f32[12,256,128]{1,2,0:T(8,128)S(1)}, f32[12,256,128]{1,2,0:T(8,128)}, u32[]{:S(2)}) copy-start(f32[12,256,128]{1,2,0:T(8,128)} %fusion.24) | copy-start | bytes 4718596

commit v3 on v2

--- a/solution.py
+++ b/solution.py
@@ -11,17 +11,18 @@
 norm_eps = 1e-05
 
 
-def carried_in(value, axis, backward):
+def carried_in(value, axis, backward, after=None):
     count = lax.axis_size(axis)
-    lanes = value.shape[-1]
-    rows = value.reshape(count, -1, lanes)
+    rows = value.reshape(count, -1)
     parts = lax.all_to_all(rows, axis, 0, 0)
     row = lax.broadcasted_iota(jnp.int32, (count, count), 0)
     col = lax.broadcasted_iota(jnp.int32, (count, count), 1)
-    strict = (row < col) if backward else (row > col)
+    strict = ((row < col) if backward else (row > col)).astype(jnp.float32)
+    if after is not None:
+        strict = strict + 0.0 * after
     shifted = jnp.einsum(
-        "ij,jkl->ikl",
-        strict.astype(jnp.float32),
+        "ij,jk->ik",
+        strict,
         parts,
         precision=lax.Precision.HIGHEST,
         preferred_element_type=jnp.float32,
@@ -83,8 +84,8 @@
     query_parts = jnp.einsum(
         "nchd,nche->nhde", queries, grad_blocks, preferred_element_type=jnp.float32
     )
-    suffix = carried_in(jnp.sum(query_parts, axis=0), "seq", True)
     gain_near = butterfly_sum(butterfly_sum(gain_terms, "dp"), "seq", 1, 4)
+    suffix = carried_in(jnp.sum(query_parts, axis=0), "seq", True, gain_near[0])
     grad_gain = butterfly_sum(gain_near, "seq", 4)
     from_end = lax.cumsum(query_parts, axis=0, reverse=True)
     behind = jnp.concatenate([from_end[1:], query_parts[-1:] * 0.0], axis=0)

time: 146 us -> 150 us (1.027)
  starting transfers between devices: 28.9 us -> 32.5 us
  waiting for transfers between devices: 44.9 us -> 43.3 us
    all_to_all x1, waiting for transfers between devices: 9.85 us -> 1.05 us  [carried_in(): parts = lax.all_to_all(rows, axis, 0, 0)]
    ppermute x8, waiting for transfers between devices: 18.9 us -> 26.1 us  [butterfly_sum(): lax.ppermute(value, axis, [(i, i ^ step) for i in range(count)])]
    all_to_all x0 -> x2, local copies, waits for them, and re-layouts: none -> 3.39 us  [carried_in(): back = lax.all_to_all(shifted, axis, 0, 0)]
    all_to_all x2, starting transfers between devices: 10.3 us -> 13.6 us  [carried_in(): back = lax.all_to_all(shifted, axis, 0, 0)]
    dot_general x2 -> x0, local copies, waits for them, and re-layouts: 2.69 us -> none  [carried_in(): jnp.einsum('ij,jkl->ikl', strict.astype(jnp.float32), parts, precision=la...]
  transfers between devices with their start and end apart: 11 -> 11, of which waited for: 8 -> 9; matrix products, arithmetic and copies ran while one was open for 13% -> 11% of each run, Pallas kernels for 0% -> 0%
where the time goes in v3:
time: 150 us; the launch traced here: 149 us
  waiting for transfers between devices  43.3 us (29%)
  blocking collectives  34 us (23%)
  starting transfers between devices  32.5 us (22%)
  local copies, waits for them, and re-layouts  16 us (11%)
  matrix products  14.6 us (10%)
  other arithmetic  6.82 us (5%)
  between operations  1.56 us (1%)
    all_to_all x1, blocking collectives, carried_in(): parts = lax.all_to_all(rows, axis, 0, 0)  34 us
    ppermute x8, waiting for transfers between devices, butterfly_sum(): lax.ppermute(value, axis, [(i, i ^ step) for i in range(count)])  26.1 us
    all_to_all x2, waiting for transfers between devices, carried_in(): back = lax.all_to_all(shifted, axis, 0, 0)  16.2 us
    ppermute x8, starting transfers between devices, butterfly_sum(): lax.ppermute(value, axis, [(i, i ^ step) for i in range(count)])  13.7 us
    all_to_all x2, starting transfers between devices, carried_in(): back = lax.all_to_all(shifted, axis, 0, 0)  13.6 us
    unnamed x34, local copies, waits for them, and re-layouts  12.1 us
    all_to_all x1, starting transfers between devices, carried_in(): parts = lax.all_to_all(rows, axis, 0, 0)  5.15 us
    all_to_all x2, local copies, waits for them, and re-layouts, carried_in(): back = lax.all_to_all(shifted, axis, 0, 0)  3.39 us
  transfers between devices with their start and end apart: 11, of which 9 were waited for; matrix products, arithmetic and copies ran while one was open for 11% of the time, Pallas kernels for 0%

profile of v3, /device:TPU:16, one launch (start us, length us, event | category | flops | bytes accessed | tf_op | source)
XLA Modules:
  0.0 148.8 jit_solution(8619913771989663752)
XLA Ops:
  2.8 34.0 %all_to_all.42 = f32[32,1,6144]{2,1,0:T(1,128)S(1)} all-to-all(f32[32,1,6144]{2,1,0:T(1,128)S(1)} %bitcast.109), channel_id=1, replica_groups=mesh['dp'=8,'seq'=32] {'seq'}, dimensions={0} | all-to-all | bytes 1572864 | tf_op jit(solution)/shard_map/all_to_all | solution.py:17
  37.6 1.7 %copy.58 = f32[32,1,6144]{2,1,0:T(1,128)} copy(f32[32,1,6144]{2,0,1:T(8,128)S(1)} %convolution_bitcast_fusion) | data formatting | bytes 1572864 | tf_op jit(solution)/shard_map/all_to_all | solution.py:30
  39.3 5.4 %all-to-all-start.1 = ((f32[32,1,6144]{2,1,0:T(1,128)}), f32[32,1,6144]{2,1,0:T(1,128)}, u32[]{:S(2)}, u32[]{:S(2)}) async-start(f32[32,1,6144]{2,1,0:T(1,128)} %copy.58), calls=%async_computation.1 | async-start | bytes 1572864 | tf_op jit(solution)/shard_map/all_to_all | solution.py:30
  44.9 1.7 %copy.59 = bf16[1,256,1536]{1,2,0:T(8,128)(2,1)S(1)} copy(bf16[1,256,1536]{2,1,0:T(8,128)(2,1)} %param.5) | data formatting | bytes 1572864 | tf_op args[0]
  48.5 1.8 %fusion.19 = f32[12,256,128]{1,2,0:T(8,128)} fusion(bf16[12,256,256]{2,1,0:T(8,128)(2,1)S(1)} %select_convert_fusion.1, bf16[256,12,128]{0,2,1:T(8,128)(2,1)S(1)} %bitcast.93), kind=kOutput, calls=%fused_computation.39 | convolution fusion | flops 201326592 | bytes 3932160 | tf_op jit(solution)/shard_map/nhct,nthe->nche/dot_general | solution.py:70
  50.3 16.2 %all-to-all-done.1 = f32[32,1,6144]{2,1,0:T(1,128)} async-done(((f32[32,1,6144]{2,1,0:T(1,128)}), f32[32,1,6144]{2,1,0:T(1,128)}, u32[]{:S(2)}, u32[]{:S(2)}) %all-to-all-start.1) | async-done | bytes 786464 | tf_op jit(solution)/shard_map/all_to_all | solution.py:30
  66.5 1.6 %add_convert_fusion.1 = bf16[12,128,128]{2,1,0:T(8,128)(2,1)S(1)} fusion(f32[12,128,128]{2,1,0:T(8,128)} %bitcast.4, f32[12,128,128]{2,1,0:T(8,128)} %copy-done.4), kind=kLoop, calls=%fused_computation.29 | loop fusion | flops 589824 | bytes 1966080 | tf_op jit(solution)/shard_map/convert_element_type | solution.py:66
  69.8 2.5 %fusion.4 = (bf16[1,256,1536]{1,2,0:T(8,128)(2,1)S(1)}, bf16[1,256,1536]{1,2,0:T(8,128)(2,1)}) fusion(bf16[1,256,1536]{1,2,0:T(8,128)(2,1)} %copy-done.2, f32[12,128,256]{2,1,0:T(8,128)S(1)} %get-tuple-element.25, f32[256]{0:T(256)S(1)} %broadcast_multiply_fusion, f32[1536]{0:T(1024)S(1)} %copy-done.12, f32[256]{0:T(256)S(1)} %add_rsqrt_fusion), kind=kLoop, calls=%fused_computation.10 | loop fusion | flops 3538944 | bytes 3940352 | tf_op jit(solution)/shard_map/convert_element_type | solution.py:83
  73.5 5.1 %all-to-all-start.2 = ((f32[32,1,6144]{2,1,0:T(1,128)}), f32[32,1,6144]{2,1,0:T(1,128)}, u32[]{:S(2)}, u32[]{:S(2)}) async-start(f32[32,1,6144]{2,1,0:T(1,128)} %bitcast.108), calls=%async_computation.2 | async-start | bytes 1572864 | tf_op jit(solution)/shard_map/all_to_all | solution.py:17
  81.2 2.4 %collective-permute-done.1 = f32[1536]{0:T(1024)S(1)} collective-permute-done((f32[1536]{0:T(1024)S(1)}, f32[1536]{0:T(1024)S(1)}, u32[]{:S(2)}, u32[]{:S(2)}) %collective-permute-start.1) | collective-permute-done | bytes 6176 | tf_op jit(solution)/shard_map/ppermute | solution.py:39
  83.9 4.8 %collective-permute-done.2 = f32[1536]{0:T(1024)S(1)} collective-permute-done((f32[1536]{0:T(1024)S(1)}, f32[1536]{0:T(1024)S(1)}, u32[]{:S(2)}, u32[]{:S(2)}) %collective-permute-start.2) | collective-permute-done | bytes 6176 | tf_op jit(solution)/shard_map/ppermute | solution.py:39
  88.8 1.7 %collective-permute-start.3 = (f32[1536]{0:T(1024)S(1)}, f32[1536]{0:T(1024)S(1)}, u32[]{:S(2)}, u32[]{:S(2)}) collective-permute-start(f32[1536]{0:T(1024)S(1)} %add.82), channel_id=1, source_target_pairs={{0,1},{1,0},{2,3},{3,2},{4,5},{5,4},{6,7},{7,6},{8,9},{9,8},{10,11... | collective-permute-start | bytes 18440 | tf_op jit(solution)/shard_map/ppermute | solution.py:39
  90.5 1.9 %collective-permute-done.3 = f32[1536]{0:T(1024)S(1)} collective-permute-done((f32[1536]{0:T(1024)S(1)}, f32[1536]{0:T(1024)S(1)}, u32[]{:S(2)}, u32[]{:S(2)}) %collective-permute-start.3) | collective-permute-done | bytes 6176 | tf_op jit(solution)/shard_map/ppermute | solution.py:39
  92.4 3.6 %collective-permute-start.4 = (f32[1536]{0:T(1024)S(1)}, f32[1536]{0:T(1024)S(1)}, u32[]{:S(2)}, u32[]{:S(2)}) collective-permute-start(f32[1536]{0:T(1024)S(1)} %add.83), channel_id=1, source_target_pairs={{0,2},{1,3},{2,0},{3,1},{4,6},{5,7},{6,4},{7,5},{8,10},{9,11},{10,... | collective-permute-start | bytes 18440 | tf_op jit(solution)/shard_map/ppermute | solution.py:39
  96.0 2.1 %collective-permute-done.4 = f32[1536]{0:T(1024)S(1)} collective-permute-done((f32[1536]{0:T(1024)S(1)}, f32[1536]{0:T(1024)S(1)}, u32[]{:S(2)}, u32[]{:S(2)}) %collective-permute-start.4) | collective-permute-done | bytes 6176 | tf_op jit(solution)/shard_map/ppermute | solution.py:39
  100.3 2.1 %convolution_bitcast_fusion.1 = f32[32,1,6144]{2,0,1:T(8,128)S(1)} fusion(f32[32,1,6144]{2,1,0:T(1,128)} %all-to-all-done.2, f32[]{:T(128)} %bitcast.16), kind=kOutput, calls=%fused_computation.1 | convolution fusion | flops 75500544 | bytes 1572868 | tf_op jit(solution)/shard_map/ij,jk->ik/dot_general | solution.py:23
  102.4 1.7 %copy.71 = f32[32,1,6144]{2,1,0:T(1,128)} copy(f32[32,1,6144]{2,0,1:T(8,128)S(1)} %convolution_bitcast_fusion.1) | data formatting | bytes 1572864 | tf_op jit(solution)/shard_map/all_to_all | solution.py:30
  104.1 8.3 %all-to-all-start.3 = ((f32[32,1,6144]{2,1,0:T(1,128)}), f32[32,1,6144]{2,1,0:T(1,128)}, u32[]{:S(2)}, u32[]{:S(2)}) async-start(f32[32,1,6144]{2,1,0:T(1,128)} %copy.71), calls=%async_computation.3 | async-start | bytes 1572864 | tf_op jit(solution)/shard_map/all_to_all | solution.py:30
  112.4 1.6 %select_convert_fusion = bf16[12,256,256]{2,1,0:T(8,128)(2,1)S(1)} fusion(bf16[256,12,128]{0,2,1:T(8,128)(2,1)S(1)} %bitcast.101, bf16[256,12,128]{0,2,1:T(8,128)(2,1)S(1)} %bitcast.94, pred[256,256]{1,0:T(8,128)(4,1)} %copy-done.11), kind=kOutput, calls=%fused_computation.2 | convolution fusion | flops 202899456 | bytes 3211264 | tf_op jit(solution)/shard_map/nche,nthe->nhct/dot_general | solution.py:93
  115.5 1.7 %collective-permute-start.5 = (f32[1536]{0:T(1024)S(1)}, f32[1536]{0:T(1024)S(1)}, u32[]{:S(2)}, u32[]{:S(2)}) collective-permute-start(f32[1536]{0:T(1024)S(1)} %add.84), channel_id=1, source_target_pairs={{0,4},{1,5},{2,6},{3,7},{4,0},{5,1},{6,2},{7,3},{8,12},{9,13},{10,... | collective-permute-start | bytes 18440 | tf_op jit(solution)/shard_map/ppermute | solution.py:39
  118.8 10.2 %collective-permute-done.5 = f32[1536]{0:T(1024)S(1)} collective-permute-done((f32[1536]{0:T(1024)S(1)}, f32[1536]{0:T(1024)S(1)}, u32[]{:S(2)}, u32[]{:S(2)}) %collective-permute-start.5) | collective-permute-done | bytes 6176 | tf_op jit(solution)/shard_map/ppermute | solution.py:39
  130.2 3.4 %collective-permute-done.6 = f32[1536]{0:T(1024)S(1)} collective-permute-done((f32[1536]{0:T(1024)S(1)}, f32[1536]{0:T(1024)S(1)}, u32[]{:S(2)}, u32[]{:S(2)}) %collective-permute-start.6) | collective-permute-done | bytes 6176 | tf_op jit(solution)/shard_map/ppermute | solution.py:39
  133.6 4.5 %collective-permute-start.7 = (f32[1536]{0:T(1024)S(1)}, f32[1536]{0:T(1024)S(1)}, u32[]{:S(2)}, u32[]{:S(2)}) collective-permute-start(f32[1536]{0:T(1024)S(1)} %add.91), channel_id=1, source_target_pairs={{0,16},{1,17},{2,18},{3,19},{4,20},{5,21},{6,22},{7,23},{8,24},{9,... | collective-permute-start | bytes 18440 | tf_op jit(solution)/shard_map/ppermute | solution.py:39
  139.3 2.4 %copy.75 = bf16[1,256,1536]{2,1,0:T(8,128)(2,1)} copy(bf16[1,256,1536]{1,2,0:T(8,128)(2,1)} %get-tuple-element.23) | data formatting | bytes 1572864
  (65 shorter events, 24.9 us)
Async XLA Ops:
  0.6 1.5 %copy-start.9 = (bf16[1,256,1536]{2,1,0:T(8,128)(2,1)S(1)}, bf16[1,256,1536]{2,1,0:T(8,128)(2,1)}, u32[]{:S(2)}) copy-start(bf16[1,256,1536]{2,1,0:T(8,128)(2,1)} %param.7) | copy-start | bytes 2359300
  2.8 34.8 %copy-start.4 = (f32[12,128,128]{2,1,0:T(8,128)}, f32[12,128,128]{2,1,0:T(8,128)S(1)}, u32[]{:S(2)}) copy-start(f32[12,128,128]{2,1,0:T(8,128)S(1)} %fusion.18) | copy-start | bytes 2359300
  39.3 5.4 %copy-start.10 = (bf16[1,256,1536]{2,1,0:T(8,128)(2,1)S(1)}, bf16[1,256,1536]{2,1,0:T(8,128)(2,1)}, u32[]{:S(2)}) copy-start(bf16[1,256,1536]{2,1,0:T(8,128)(2,1)} %param.9) | copy-start | bytes 2359300
  39.3 27.2 %all-to-all-start.1 = ((f32[32,1,6144]{2,1,0:T(1,128)}), f32[32,1,6144]{2,1,0:T(1,128)}, u32[]{:S(2)}, u32[]{:S(2)}) async-start(f32[32,1,6144]{2,1,0:T(1,128)} %copy.58), calls=%async_computation.1 | async-start | bytes 1572864 | tf_op jit(solution)/shard_map/all_to_all | solution.py:30
  44.9 23.9 %copy-start.2 = (bf16[1,256,1536]{1,2,0:T(8,128)(2,1)}, bf16[1,256,1536]{1,2,0:T(8,128)(2,1)S(1)}, u32[]{:S(2)}) copy-start(bf16[1,256,1536]{1,2,0:T(8,128)(2,1)S(1)} %copy.64) | copy-start | bytes 2359300
  46.7 0.7 copy-start.11
  47.3 1.2 copy-start
  66.5 1.9 %copy-start.7 = (f32[12,256,128]{1,2,0:T(8,128)S(1)}, f32[12,256,128]{1,2,0:T(8,128)}, u32[]{:S(2)}) copy-start(f32[12,256,128]{1,2,0:T(8,128)} %fusion.19) | copy-start | bytes 4718596
  68.4 0.7 copy-start.12
  73.5 26.8 %all-to-all-start.2 = ((f32[32,1,6144]{2,1,0:T(1,128)}), f32[32,1,6144]{2,1,0:T(1,128)}, u32[]{:S(2)}, u32[]{:S(2)}) async-start(f32[32,1,6144]{2,1,0:T(1,128)} %bitcast.108), calls=%async_computation.2 | async-start | bytes 1572864 | tf_op jit(solution)/shard_map/all_to_all | solution.py:17
  78.7 1.3 collective-permute-start
  80.0 3.7 %collective-permute-start.1 = (f32[1536]{0:T(1024)S(1)}, f32[1536]{0:T(1024)S(1)}, u32[]{:S(2)}, u32[]{:S(2)}) collective-permute-start(f32[1536]{0:T(1024)S(1)} %add.80), channel_id=1, source_target_pairs={{0,64},{32,96},{64,0},{96,32},{128,192},{160,224},{192,128},{224,1... | collective-permute-start | bytes 18440 | tf_op jit(solution)/shard_map/ppermute | solution.py:39
  83.6 5.2 %collective-permute-start.2 = (f32[1536]{0:T(1024)S(1)}, f32[1536]{0:T(1024)S(1)}, u32[]{:S(2)}, u32[]{:S(2)}) collective-permute-start(f32[1536]{0:T(1024)S(1)} %add.81), channel_id=1, source_target_pairs={{0,128},{32,160},{64,192},{96,224},{128,0},{160,32},{192,64},{224,... | collective-permute-start | bytes 18440 | tf_op jit(solution)/shard_map/ppermute | solution.py:39
  88.8 3.7 %collective-permute-start.3 = (f32[1536]{0:T(1024)S(1)}, f32[1536]{0:T(1024)S(1)}, u32[]{:S(2)}, u32[]{:S(2)}) collective-permute-start(f32[1536]{0:T(1024)S(1)} %add.82), channel_id=1, source_target_pairs={{0,1},{1,0},{2,3},{3,2},{4,5},{5,4},{6,7},{7,6},{8,9},{9,8},{10,11... | collective-permute-start | bytes 18440 | tf_op jit(solution)/shard_map/ppermute | solution.py:39
  92.4 5.7 %collective-permute-start.4 = (f32[1536]{0:T(1024)S(1)}, f32[1536]{0:T(1024)S(1)}, u32[]{:S(2)}, u32[]{:S(2)}) collective-permute-start(f32[1536]{0:T(1024)S(1)} %add.83), channel_id=1, source_target_pairs={{0,2},{1,3},{2,0},{3,1},{4,6},{5,7},{6,4},{7,5},{8,10},{9,11},{10,... | collective-permute-start | bytes 18440 | tf_op jit(solution)/shard_map/ppermute | solution.py:39
  104.1 39.4 %all-to-all-start.3 = ((f32[32,1,6144]{2,1,0:T(1,128)}), f32[32,1,6144]{2,1,0:T(1,128)}, u32[]{:S(2)}, u32[]{:S(2)}) async-start(f32[32,1,6144]{2,1,0:T(1,128)} %copy.71), calls=%async_computation.3 | async-start | bytes 1572864 | tf_op jit(solution)/shard_map/all_to_all | solution.py:30
  112.4 1.6 %copy-start.1 = (bf16[12,256,256]{2,1,0:T(8,128)(2,1)S(1)}, bf16[12,256,256]{2,1,0:T(8,128)(2,1)}, u32[]{:S(2)}) copy-start(bf16[12,256,256]{2,1,0:T(8,128)(2,1)} %copy-done) | copy-start | bytes 4718596
  115.5 13.5 %collective-permute-start.5 = (f32[1536]{0:T(1024)S(1)}, f32[1536]{0:T(1024)S(1)}, u32[]{:S(2)}, u32[]{:S(2)}) collective-permute-start(f32[1536]{0:T(1024)S(1)} %add.84), channel_id=1, source_target_pairs={{0,4},{1,5},{2,6},{3,7},{4,0},{5,1},{6,2},{7,3},{8,12},{9,13},{10,... | collective-permute-start | bytes 18440 | tf_op jit(solution)/shard_map/ppermute | solution.py:39
  129.1 4.5 %collective-permute-start.6 = (f32[1536]{0:T(1024)S(1)}, f32[1536]{0:T(1024)S(1)}, u32[]{:S(2)}, u32[]{:S(2)}) collective-permute-start(f32[1536]{0:T(1024)S(1)} %add.90), channel_id=1, source_target_pairs={{0,8},{1,9},{2,10},{3,11},{4,12},{5,13},{6,14},{7,15},{8,0},{9,1},... | collective-permute-start | bytes 18440 | tf_op jit(solution)/shard_map/ppermute | solution.py:39
  133.6 9.3 %collective-permute-start.7 = (f32[1536]{0:T(1024)S(1)}, f32[1536]{0:T(1024)S(1)}, u32[]{:S(2)}, u32[]{:S(2)}) collective-permute-start(f32[1536]{0:T(1024)S(1)} %add.91), channel_id=1, source_target_pairs={{0,16},{1,17},{2,18},{3,19},{4,20},{5,21},{6,22},{7,23},{8,24},{9,... | collective-permute-start | bytes 18440 | tf_op jit(solution)/shard_map/ppermute | solution.py:39
  139.3 2.4 %copy-start.8 = (bf16[12,128,256]{2,1,0:T(8,128)(2,1)S(1)}, bf16[12,128,256]{2,1,0:T(8,128)(2,1)}, u32[]{:S(2)}) copy-start(bf16[12,128,256]{2,1,0:T(8,128)(2,1)} %fusion.7) | copy-start | bytes 2359300
  139.3 4.2 %copy-start.3 = (f32[12,128,128]{1,2,0:T(8,128)S(1)}, f32[12,128,128]{1,2,0:T(8,128)}, u32[]{:S(2)}) copy-start(f32[12,128,128]{1,2,0:T(8,128)} %fusion.21) | copy-start | bytes 2359300
  143.5 1.6 %copy-start.5 = (f32[12,128,256]{2,1,0:T(8,128)S(1)}, f32[12,128,256]{2,1,0:T(8,128)}, u32[]{:S(2)}) copy-start(f32[12,128,256]{2,1,0:T(8,128)} %fusion.22) | copy-start | bytes 4718596
  145.6 1.7 %copy-start.6 = (f32[12,256,128]{1,2,0:T(8,128)S(1)}, f32[12,256,128]{1,2,0:T(8,128)}, u32[]{:S(2)}) copy-start(f32[12,256,128]{1,2,0:T(8,128)} %fusion.23) | copy-start | bytes 4718596

commit v4 on v2

--- a/solution.py
+++ b/solution.py
@@ -84,8 +84,8 @@
         "nchd,nche->nhde", queries, grad_blocks, preferred_element_type=jnp.float32
     )
     suffix = carried_in(jnp.sum(query_parts, axis=0), "seq", True)
-    gain_near = butterfly_sum(butterfly_sum(gain_terms, "dp"), "seq", 1, 4)
-    grad_gain = butterfly_sum(gain_near, "seq", 4)
+    gain_dp = butterfly_sum(gain_terms, "dp")
+    grad_gain = jnp.sum(lax.all_gather(gain_dp, "seq"), axis=0)
     from_end = lax.cumsum(query_parts, axis=0, reverse=True)
     behind = jnp.concatenate([from_end[1:], query_parts[-1:] * 0.0], axis=0)
     suffix_states = (suffix[None] + behind).astype(jnp.bfloat16)

time: 146 us -> 181 us (1.24)
  blocking collectives: 34 us -> 83.6 us
  starting transfers between devices: 28.9 us -> 17 us
  waiting for transfers between devices: 44.9 us -> 39.5 us
    all_gather x0 -> x1, blocking collectives: none -> 49.6 us  [local(): grad_gain = jnp.sum(lax.all_gather(gain_dp, 'seq'), axis=0)]
    ppermute x8 -> x3, waiting for transfers between devices: 18.9 us -> 1.74 us  [butterfly_sum(): lax.ppermute(value, axis, [(i, i ^ step) for i in range(count)])]
    ppermute x8 -> x3, starting transfers between devices: 13.5 us -> 1.71 us  [butterfly_sum(): lax.ppermute(value, axis, [(i, i ^ step) for i in range(count)])]
    all_to_all x1, waiting for transfers between devices: 9.85 us -> 21.5 us  [carried_in(): parts = lax.all_to_all(rows, axis, 0, 0)]
    unnamed x34 -> x35, local copies, waits for them, and re-layouts: 12.1 us -> 12.8 us
  transfers between devices with their start and end apart: 11 -> 6, of which waited for: 8 -> 3; matrix products, arithmetic and copies ran while one was open for 13% -> 10% of each run, Pallas kernels for 0% -> 0%
where the time goes in v4:
time: 181 us; the launch traced here: 179 us
  blocking collectives  83.6 us (46%)
  waiting for transfers between devices  39.5 us (22%)
  starting transfers between devices  17 us (9%)
  local copies, waits for them, and re-layouts  15.5 us (9%)
  matrix products  15.4 us (9%)
  other arithmetic  6.93 us (4%)
    all_gather x1, blocking collectives, local(): grad_gain = jnp.sum(lax.all_gather(gain_dp, 'seq'), axis=0)  49.6 us
    all_to_all x1, blocking collectives, carried_in(): parts = lax.all_to_all(rows, axis, 0, 0)  34 us
    all_to_all x1, waiting for transfers between devices, carried_in(): parts = lax.all_to_all(rows, axis, 0, 0)  21.5 us
    all_to_all x2, waiting for transfers between devices, carried_in(): back = lax.all_to_all(shifted, axis, 0, 0)  16.2 us
    unnamed x35, local copies, waits for them, and re-layouts  12.8 us
    all_to_all x2, starting transfers between devices, carried_in(): back = lax.all_to_all(shifted, axis, 0, 0)  10.2 us
    all_to_all x1, starting transfers between devices, carried_in(): parts = lax.all_to_all(rows, axis, 0, 0)  5.15 us
  transfers between devices with their start and end apart: 6, of which 3 were waited for; matrix products, arithmetic and copies ran while one was open for 10% of the time, Pallas kernels for 0%

profile of v4, /device:TPU:16, one launch (start us, length us, event | category | flops | bytes accessed | tf_op | source)
XLA Modules:
  0.0 178.8 jit_solution(9276836461856815858)
XLA Ops:
  0.6 1.5 copy.60
  2.8 34.0 %all_to_all.20 = f32[32,48,128]{2,1,0:T(8,128)S(1)} all-to-all(f32[32,48,128]{2,1,0:T(8,128)S(1)} %bitcast.104), channel_id=1, replica_groups=mesh['dp'=8,'seq'=32] {'seq'}, dimensions={0} | all-to-all | bytes 1572864 | tf_op jit(solution)/shard_map/all_to_all | solution.py:18
  37.6 1.3 copy.64
  38.9 5.3 %all-to-all-start.1 = ((f32[32,48,128]{2,1,0:T(8,128)}), f32[32,48,128]{2,1,0:T(8,128)}, u32[]{:S(2)}, u32[]{:S(2)}) async-start(f32[32,48,128]{2,1,0:T(8,128)} %copy.64), calls=%async_computation.1 | async-start | bytes 1572864 | tf_op jit(solution)/shard_map/all_to_all | solution.py:29
  44.5 1.7 copy.65
  48.0 1.8 %fusion.20 = f32[12,256,128]{1,2,0:T(8,128)} fusion(bf16[12,256,256]{2,1,0:T(8,128)(2,1)S(1)} %select_convert_fusion.1, bf16[256,12,128]{0,2,1:T(8,128)(2,1)S(1)} %bitcast.88), kind=kOutput, calls=%fused_computation.36 | convolution fusion | flops 201326592 | bytes 3932160 | tf_op jit(solution)/shard_map/nhct,nthe->nche/dot_general | solution.py:69
  49.8 16.2 %all-to-all-done.1 = f32[32,48,128]{2,1,0:T(8,128)} async-done(((f32[32,48,128]{2,1,0:T(8,128)}), f32[32,48,128]{2,1,0:T(8,128)}, u32[]{:S(2)}, u32[]{:S(2)}) %all-to-all-start.1) | async-done | bytes 786464 | tf_op jit(solution)/shard_map/all_to_all | solution.py:29
  66.0 1.6 add_convert_fusion.1
  69.3 2.5 %fusion.4 = (bf16[1,256,1536]{1,2,0:T(8,128)(2,1)S(1)}, bf16[1,256,1536]{1,2,0:T(8,128)(2,1)}) fusion(bf16[1,256,1536]{1,2,0:T(8,128)(2,1)} %copy-done.2, f32[12,128,256]{2,1,0:T(8,128)S(1)} %get-tuple-element.25, f32[256]{0:T(256)S(1)} %broadcast_multiply_fusion, f32[1536]{0:T(1024)S(1)} %copy-done.12, f32[256]{0:T(256)S(1)} %add_rsqrt_fusion), kind=kLoop, calls=%fused_computation.8 | loop fusion | flops 3538944 | bytes 3940352 | tf_op jit(solution)/shard_map/convert_element_type | solution.py:82
  73.1 5.1 %all-to-all-start.2 = ((f32[32,48,128]{2,1,0:T(8,128)}), f32[32,48,128]{2,1,0:T(8,128)}, u32[]{:S(2)}, u32[]{:S(2)}) async-start(f32[32,48,128]{2,1,0:T(8,128)} %bitcast.103), calls=%async_computation.2 | async-start | bytes 1572864 | tf_op jit(solution)/shard_map/all_to_all | solution.py:18
  78.3 21.5 %all-to-all-done.2 = f32[32,48,128]{2,1,0:T(8,128)} async-done(((f32[32,48,128]{2,1,0:T(8,128)}), f32[32,48,128]{2,1,0:T(8,128)}, u32[]{:S(2)}, u32[]{:S(2)}) %all-to-all-start.2) | async-done | bytes 786464 | tf_op jit(solution)/shard_map/all_to_all | solution.py:18
  99.9 1.9 %fusion.11 = f32[32,48,128]{2,0,1:T(8,128)S(1)} fusion(f32[32,48,128]{2,1,0:T(8,128)} %all-to-all-done.2), kind=kOutput, calls=%fused_computation.23 | convolution fusion | flops 75498496 | bytes 1572864 | tf_op jit(solution)/shard_map/ij,jkl->ikl/dot_general | solution.py:22
  101.8 1.4 copy.76
  103.2 4.9 %all-to-all-start.3 = ((f32[32,48,128]{2,1,0:T(8,128)}), f32[32,48,128]{2,1,0:T(8,128)}, u32[]{:S(2)}, u32[]{:S(2)}) async-start(f32[32,48,128]{2,1,0:T(8,128)} %copy.76), calls=%async_computation.3 | async-start | bytes 1572864 | tf_op jit(solution)/shard_map/all_to_all | solution.py:29
  108.1 1.6 select_convert_fusion
  109.7 1.5 fusion.23
  111.2 1.6 fusion.24
  112.8 1.3 collective-permute-start.1
  114.7 1.7 collective-permute-done.1
  118.0 2.4 %copy.80 = bf16[1,256,1536]{2,1,0:T(8,128)(2,1)} copy(bf16[1,256,1536]{1,2,0:T(8,128)(2,1)} %get-tuple-element.23) | data formatting | bytes 1572864
  121.6 49.6 %all-gather.1 = f32[32,1,1536]{2,1,0:T(1,128)S(1)} all-gather(f32[1,1,1536]{2,1,0:T(1,128)S(1)} %reshape.329), channel_id=2, replica_groups=mesh['dp'=8,'seq'=32] {'seq'}, dimensions={0}, use_global_device_ids=true | all-gather | bytes 202752 | tf_op jit(solution)/shard_map/all_gather | solution.py:88
  171.9 1.3 fusion.10
  173.6 1.3 add_convert_fusion
  174.9 2.4 %copy.83 = bf16[1,256,1536]{2,1,0:T(8,128)(2,1)} copy(bf16[1,256,1536]{1,2,0:T(8,128)(2,1)} %bitcast.107) | data formatting | bytes 1572864
  (52 shorter events, 12.5 us)
Async XLA Ops:
  0.6 1.5 copy-start.9
  2.8 34.8 %copy-start.4 = (f32[12,128,128]{2,1,0:T(8,128)}, f32[12,128,128]{2,1,0:T(8,128)S(1)}, u32[]{:S(2)}) copy-start(f32[12,128,128]{2,1,0:T(8,128)S(1)} %fusion.19) | copy-start | bytes 2359300
  37.6 6.6 %copy-start.10 = (bf16[1,256,1536]{2,1,0:T(8,128)(2,1)S(1)}, bf16[1,256,1536]{2,1,0:T(8,128)(2,1)}, u32[]{:S(2)}) copy-start(bf16[1,256,1536]{2,1,0:T(8,128)(2,1)} %param.9) | copy-start | bytes 2359300
  38.9 27.1 %all-to-all-start.1 = ((f32[32,48,128]{2,1,0:T(8,128)}), f32[32,48,128]{2,1,0:T(8,128)}, u32[]{:S(2)}, u32[]{:S(2)}) async-start(f32[32,48,128]{2,1,0:T(8,128)} %copy.64), calls=%async_computation.1 | async-start | bytes 1572864 | tf_op jit(solution)/shard_map/all_to_all | solution.py:29
  44.5 23.9 %copy-start.2 = (bf16[1,256,1536]{1,2,0:T(8,128)(2,1)}, bf16[1,256,1536]{1,2,0:T(8,128)(2,1)S(1)}, u32[]{:S(2)}) copy-start(bf16[1,256,1536]{1,2,0:T(8,128)(2,1)S(1)} %copy.70) | copy-start | bytes 2359300
  46.2 0.7 copy-start.11
  46.9 1.2 copy-start
  66.0 1.9 %copy-start.7 = (f32[12,256,128]{1,2,0:T(8,128)S(1)}, f32[12,256,128]{1,2,0:T(8,128)}, u32[]{:S(2)}) copy-start(f32[12,256,128]{1,2,0:T(8,128)} %fusion.20) | copy-start | bytes 4718596
  67.9 0.7 copy-start.12
  73.1 26.8 %all-to-all-start.2 = ((f32[32,48,128]{2,1,0:T(8,128)}), f32[32,48,128]{2,1,0:T(8,128)}, u32[]{:S(2)}, u32[]{:S(2)}) async-start(f32[32,48,128]{2,1,0:T(8,128)} %bitcast.103), calls=%async_computation.2 | async-start | bytes 1572864 | tf_op jit(solution)/shard_map/all_to_all | solution.py:18
  78.2 34.5 %collective-permute-start = (f32[1536]{0:T(1024)S(1)}, f32[1536]{0:T(1024)S(1)}, u32[]{:S(2)}, u32[]{:S(2)}) collective-permute-start(f32[1536]{0:T(1024)S(1)} %get-tuple-element.20), channel_id=1, source_target_pairs={{0,32},{32,0},{64,96},{96,64},{128,160},{160,128},{192,224},{224,1... | collective-permute-start | bytes 18440 | tf_op jit(solution)/shard_map/ppermute | solution.py:38
  103.2 68.8 %all-to-all-start.3 = ((f32[32,48,128]{2,1,0:T(8,128)}), f32[32,48,128]{2,1,0:T(8,128)}, u32[]{:S(2)}, u32[]{:S(2)}) async-start(f32[32,48,128]{2,1,0:T(8,128)} %copy.76), calls=%async_computation.3 | async-start | bytes 1572864 | tf_op jit(solution)/shard_map/all_to_all | solution.py:29
  108.1 1.6 copy-start.1
  112.8 3.7 %collective-permute-start.1 = (f32[1536]{0:T(1024)S(1)}, f32[1536]{0:T(1024)S(1)}, u32[]{:S(2)}, u32[]{:S(2)}) collective-permute-start(f32[1536]{0:T(1024)S(1)} %add.62), channel_id=1, source_target_pairs={{0,64},{32,96},{64,0},{96,32},{128,192},{160,224},{192,128},{224,1... | collective-permute-start | bytes 18440 | tf_op jit(solution)/shard_map/ppermute | solution.py:38
  116.5 5.2 %collective-permute-start.2 = (f32[1536]{0:T(1024)S(1)}, f32[1536]{0:T(1024)S(1)}, u32[]{:S(2)}, u32[]{:S(2)}) collective-permute-start(f32[1536]{0:T(1024)S(1)} %add.63), channel_id=1, source_target_pairs={{0,128},{32,160},{64,192},{96,224},{128,0},{160,32},{192,64},{224,... | collective-permute-start | bytes 18440 | tf_op jit(solution)/shard_map/ppermute | solution.py:38
  118.0 2.4 %copy-start.8 = (bf16[12,128,256]{2,1,0:T(8,128)(2,1)S(1)}, bf16[12,128,256]{2,1,0:T(8,128)(2,1)}, u32[]{:S(2)}) copy-start(bf16[12,128,256]{2,1,0:T(8,128)(2,1)} %fusion.7) | copy-start | bytes 2359300
  118.0 53.9 %copy-start.3 = (f32[12,128,128]{1,2,0:T(8,128)S(1)}, f32[12,128,128]{1,2,0:T(8,128)}, u32[]{:S(2)}) copy-start(f32[12,128,128]{1,2,0:T(8,128)} %fusion.22) | copy-start | bytes 2359300
  171.9 1.6 copy-start.6
  174.9 2.4 %copy-start.5 = (f32[12,256,128]{1,2,0:T(8,128)S(1)}, f32[12,256,128]{1,2,0:T(8,128)}, u32[]{:S(2)}) copy-start(f32[12,256,128]{1,2,0:T(8,128)} %fusion.24) | copy-start | bytes 4718596

commit v5 on v4

--- a/solution.py
+++ b/solution.py
@@ -6,6 +6,7 @@
 HEADS = 12
 HEAD_DIM = 128
 BLOCK = 256
+GAIN_PAD = 16384
 
 
 norm_eps = 1e-05
@@ -28,16 +29,6 @@
     )
     back = lax.all_to_all(shifted, axis, 0, 0)
     return back.reshape(value.shape)
-
-
-def butterfly_sum(value, axis, first=1, last=None):
-    count = lax.axis_size(axis)
-    last = count if last is None else last
-    step = first
-    while step < last:
-        value = value + lax.ppermute(value, axis, [(i, i ^ step) for i in range(count)])
-        step *= 2
-    return value
 
 
 def lower_mask(length):
@@ -84,8 +75,8 @@
         "nchd,nche->nhde", queries, grad_blocks, preferred_element_type=jnp.float32
     )
     suffix = carried_in(jnp.sum(query_parts, axis=0), "seq", True)
-    gain_dp = butterfly_sum(gain_terms, "dp")
-    grad_gain = jnp.sum(lax.all_gather(gain_dp, "seq"), axis=0)
+
+    grad_gain = lax.psum(jnp.pad(gain_terms, (0, GAIN_PAD - features)), ("dp", "seq"))[:features]
     from_end = lax.cumsum(query_parts, axis=0, reverse=True)
     behind = jnp.concatenate([from_end[1:], query_parts[-1:] * 0.0], axis=0)
     suffix_states = (suffix[None] + behind).astype(jnp.bfloat16)

time: 181 us -> 352 us (1.94)
  waiting for transfers between devices: 39.5 us -> 248 us
  blocking collectives: 83.6 us -> 34 us
  between operations: 0.89 us -> 14.3 us
    psum x0 -> x1, waiting for transfers between devices: none -> 211 us  [local(): lax.psum(jnp.pad(gain_terms, (0, GAIN_PAD - features)), ('dp', 'seq'))]
    all_gather x1 -> x0, blocking collectives: 49.6 us -> none  [local(): grad_gain = jnp.sum(lax.all_gather(gain_dp, 'seq'), axis=0)]
    unnamed x35 -> x34, local copies, waits for them, and re-layouts: 12.8 us -> 12.1 us
  transfers between devices with their start and end apart: 6 -> 4, of which waited for: 3 -> 3; matrix products, arithmetic and copies ran while one was open for 10% -> 6% of each run, Pallas kernels for 0% -> 0%
where the time goes in v5:
time: 352 us; the launch traced here: 349 us
  waiting for transfers between devices  248 us (70%)
  blocking collectives  34 us (10%)
  local copies, waits for them, and re-layouts  16.7 us (5%)
  starting transfers between devices  15.7 us (4%)
  matrix products  14.5 us (4%)
  between operations  14.3 us (4%)
  other arithmetic  6.2 us (2%)
    psum x1, waiting for transfers between devices, local(): lax.psum(jnp.pad(gain_terms, (0, GAIN_PAD - features)), ('dp', 'seq'))  211 us
    all_to_all x1, blocking collectives, carried_in(): parts = lax.all_to_all(rows, axis, 0, 0)  34 us
    all_to_all x1, waiting for transfers between devices, carried_in(): parts = lax.all_to_all(rows, axis, 0, 0)  20.9 us
    all_to_all x2, waiting for transfers between devices, carried_in(): back = lax.all_to_all(shifted, axis, 0, 0)  16.2 us
    unnamed x34, local copies, waits for them, and re-layouts  12.1 us
    all_to_all x2, starting transfers between devices, carried_in(): back = lax.all_to_all(shifted, axis, 0, 0)  10.5 us
  transfers between devices with their start and end apart: 4, of which 3 were waited for; matrix products, arithmetic and copies ran while one was open for 6% of the time, Pallas kernels for 0%

profile of v5, /device:TPU:16, one launch (start us, length us, event | category | flops | bytes accessed | tf_op | source)
XLA Modules:
  0.0 349.4 jit_solution(11559505907553414886)
XLA Ops:
  7.2 1.5 copy.60
  9.3 34.0 %all_to_all.20 = f32[32,48,128]{2,1,0:T(8,128)S(1)} all-to-all(f32[32,48,128]{2,1,0:T(8,128)S(1)} %bitcast.104), channel_id=1, replica_groups=mesh['dp'=8,'seq'=32] {'seq'}, dimensions={0} | all-to-all | bytes 1572864 | tf_op jit(solution)/shard_map/all_to_all | solution.py:19
  44.1 1.3 copy.64
  45.4 5.4 %all-to-all-start.1 = ((f32[32,48,128]{2,1,0:T(8,128)}), f32[32,48,128]{2,1,0:T(8,128)}, u32[]{:S(2)}, u32[]{:S(2)}) async-start(f32[32,48,128]{2,1,0:T(8,128)} %copy.64), calls=%async_computation.1 | async-start | bytes 1572864 | tf_op jit(solution)/shard_map/all_to_all | solution.py:30
  51.1 1.7 copy.65
  54.7 1.8 fusion.20
  56.5 16.2 %all-to-all-done.1 = f32[32,48,128]{2,1,0:T(8,128)} async-done(((f32[32,48,128]{2,1,0:T(8,128)}), f32[32,48,128]{2,1,0:T(8,128)}, u32[]{:S(2)}, u32[]{:S(2)}) %all-to-all-start.1) | async-done | bytes 786464 | tf_op jit(solution)/shard_map/all_to_all | solution.py:30
  72.7 1.6 add_convert_fusion.1
  76.0 2.5 fusion.4
  78.5 1.3 fusion.22
  79.7 5.2 %all-to-all-start.2 = ((f32[32,48,128]{2,1,0:T(8,128)}), f32[32,48,128]{2,1,0:T(8,128)}, u32[]{:S(2)}, u32[]{:S(2)}) async-start(f32[32,48,128]{2,1,0:T(8,128)} %bitcast.103), calls=%async_computation.2 | async-start | bytes 1572864 | tf_op jit(solution)/shard_map/all_to_all | solution.py:19
  85.6 20.9 %all-to-all-done.2 = f32[32,48,128]{2,1,0:T(8,128)} async-done(((f32[32,48,128]{2,1,0:T(8,128)}), f32[32,48,128]{2,1,0:T(8,128)}, u32[]{:S(2)}, u32[]{:S(2)}) %all-to-all-start.2) | async-done | bytes 786464 | tf_op jit(solution)/shard_map/all_to_all | solution.py:19
  106.5 1.9 fusion.11
  108.4 1.4 copy.76
  109.8 5.1 %all-to-all-start.3 = ((f32[32,48,128]{2,1,0:T(8,128)}), f32[32,48,128]{2,1,0:T(8,128)}, u32[]{:S(2)}, u32[]{:S(2)}) async-start(f32[32,48,128]{2,1,0:T(8,128)} %copy.76), calls=%async_computation.3 | async-start | bytes 1572864 | tf_op jit(solution)/shard_map/all_to_all | solution.py:30
  114.9 1.6 select_convert_fusion
  116.5 1.5 fusion.23
  118.1 1.6 fusion.24
  120.3 1.2 fusion.7
  121.5 2.4 copy.80
  125.1 210.9 %all-reduce.3.cloned.1.call-done = f32[16384]{0:T(1024)} async-done(((f32[16384]{0:T(1024)}), f32[16384]{0:T(1024)}) %all-reduce.3.cloned.1.call-update) | async-done | bytes 65552 | tf_op jit(solution)/shard_map/psum | solution.py:79
  336.0 1.3 slice.4
  337.3 1.4 fusion.10
  339.3 1.2 copy.83
  (45 shorter events, 10.5 us)
Async XLA Ops:
  7.2 1.5 copy-start.9
  9.3 34.8 %copy-start.4 = (f32[12,128,128]{2,1,0:T(8,128)}, f32[12,128,128]{2,1,0:T(8,128)S(1)}, u32[]{:S(2)}) copy-start(f32[12,128,128]{2,1,0:T(8,128)S(1)} %fusion.19) | copy-start | bytes 2359300
  45.4 5.4 %copy-start.10 = (bf16[1,256,1536]{2,1,0:T(8,128)(2,1)S(1)}, bf16[1,256,1536]{2,1,0:T(8,128)(2,1)}, u32[]{:S(2)}) copy-start(bf16[1,256,1536]{2,1,0:T(8,128)(2,1)} %param.9) | copy-start | bytes 2359300
  45.4 27.2 %all-to-all-start.1 = ((f32[32,48,128]{2,1,0:T(8,128)}), f32[32,48,128]{2,1,0:T(8,128)}, u32[]{:S(2)}, u32[]{:S(2)}) async-start(f32[32,48,128]{2,1,0:T(8,128)} %copy.64), calls=%async_computation.1 | async-start | bytes 1572864 | tf_op jit(solution)/shard_map/all_to_all | solution.py:30
  51.1 23.9 %copy-start.2 = (bf16[1,256,1536]{1,2,0:T(8,128)(2,1)}, bf16[1,256,1536]{1,2,0:T(8,128)(2,1)S(1)}, u32[]{:S(2)}) copy-start(bf16[1,256,1536]{1,2,0:T(8,128)(2,1)S(1)} %copy.70) | copy-start | bytes 2359300
  52.9 0.7 copy-start.11
  53.5 1.2 copy-start
  72.7 1.9 copy-start.7
  74.5 0.7 copy-start.12
  79.7 26.8 %all-to-all-start.2 = ((f32[32,48,128]{2,1,0:T(8,128)}), f32[32,48,128]{2,1,0:T(8,128)}, u32[]{:S(2)}, u32[]{:S(2)}) async-start(f32[32,48,128]{2,1,0:T(8,128)} %bitcast.103), calls=%async_computation.2 | async-start | bytes 1572864 | tf_op jit(solution)/shard_map/all_to_all | solution.py:19
  84.9 251.1 %all-reduce.3.cloned.1.call-start = ((), (), s32[]{:S(2)}) async-start(), calls=%async_computation.4 | async-start | bytes 131072 | tf_op jit(solution)/shard_map/psum | solution.py:79
  109.8 227.4 %all-to-all-start.3 = ((f32[32,48,128]{2,1,0:T(8,128)}), f32[32,48,128]{2,1,0:T(8,128)}, u32[]{:S(2)}, u32[]{:S(2)}) async-start(f32[32,48,128]{2,1,0:T(8,128)} %copy.76), calls=%async_computation.3 | async-start | bytes 1572864 | tf_op jit(solution)/shard_map/all_to_all | solution.py:30
  114.9 1.6 copy-start.1
  121.5 2.4 copy-start.8
  121.5 215.7 %copy-start.3 = (f32[12,128,128]{1,2,0:T(8,128)S(1)}, f32[12,128,128]{1,2,0:T(8,128)}, u32[]{:S(2)}) copy-start(f32[12,128,128]{1,2,0:T(8,128)} %fusion.22) | copy-start | bytes 2359300
  337.3 1.6 copy-start.6
  339.3 1.7 copy-start.5
Sparse Core Ops, SparseCore 0:
  91.2 244.6 all-reduce.2

commit v6 on v3

--- a/solution.py
+++ b/solution.py
@@ -13,7 +13,8 @@
 
 def carried_in(value, axis, backward, after=None):
     count = lax.axis_size(axis)
-    rows = value.reshape(count, -1)
+    lanes = value.shape[-1]
+    rows = value.reshape(count, -1, lanes)
     parts = lax.all_to_all(rows, axis, 0, 0)
     row = lax.broadcasted_iota(jnp.int32, (count, count), 0)
     col = lax.broadcasted_iota(jnp.int32, (count, count), 1)
@@ -21,7 +22,7 @@
     if after is not None:
         strict = strict + 0.0 * after
     shifted = jnp.einsum(
-        "ij,jk->ik",
+        "ij,jkl->ikl",
         strict,
         parts,
         precision=lax.Precision.HIGHEST,
@@ -47,7 +48,7 @@
     return row_index >= col_index
 
 
-def local(query_rows, key_rows, value_rows, norm_gain, grad_output):
+def local_body(query_rows, key_rows, value_rows, norm_gain, grad_output):
     tokens = query_rows.shape[1]
     features = query_rows.shape[2]
     blocks = tokens // BLOCK
@@ -84,9 +85,9 @@
     query_parts = jnp.einsum(
         "nchd,nche->nhde", queries, grad_blocks, preferred_element_type=jnp.float32
     )
-    gain_near = butterfly_sum(butterfly_sum(gain_terms, "dp"), "seq", 1, 4)
-    suffix = carried_in(jnp.sum(query_parts, axis=0), "seq", True, gain_near[0])
-    grad_gain = butterfly_sum(gain_near, "seq", 4)
+    gain_dp = butterfly_sum(gain_terms, "dp")
+    suffix = carried_in(jnp.sum(query_parts, axis=0), "seq", True, gain_dp[0])
+    grad_gain = butterfly_sum(gain_dp, "seq")
     from_end = lax.cumsum(query_parts, axis=0, reverse=True)
     behind = jnp.concatenate([from_end[1:], query_parts[-1:] * 0.0], axis=0)
     suffix_states = (suffix[None] + behind).astype(jnp.bfloat16)
@@ -131,7 +132,7 @@
         P("dp", "seq", None),
     )
     return jax.shard_map(
-        local,
+        local_body,
         mesh=mesh,
         in_specs=placed,
         out_specs=(

time: 150 us -> 146 us (0.973)
  starting transfers between devices: 32.5 us -> 28.9 us
    all_to_all x1, waiting for transfers between devices: 1.05 us -> 8.69 us  [carried_in(): parts = lax.all_to_all(rows, axis, 0, 0)]
    ppermute x8, waiting for transfers between devices: 26.1 us -> 18.9 us  [butterfly_sum(): lax.ppermute(value, axis, [(i, i ^ step) for i in range(count)])]
    all_to_all x2 -> x0, local copies, waits for them, and re-layouts: 3.39 us -> none  [carried_in(): back = lax.all_to_all(shifted, axis, 0, 0)]
    all_to_all x2, starting transfers between devices: 13.6 us -> 10.3 us  [carried_in(): back = lax.all_to_all(shifted, axis, 0, 0)]
    dot_general x0 -> x2, local copies, waits for them, and re-layouts: none -> 2.69 us  [carried_in(): jnp.einsum('ij,jkl->ikl', strict, parts, precision=lax.Precision.HIGHEST,...]
  transfers between devices with their start and end apart: 11 -> 11, of which waited for: 9 -> 8; matrix products, arithmetic and copies ran while one was open for 11% -> 13% of each run, Pallas kernels for 0% -> 0%
where the time goes in v6:
time: 146 us; the launch traced here: 145 us
  waiting for transfers between devices  43.8 us (30%)
  blocking collectives  34 us (23%)
  starting transfers between devices  28.9 us (20%)
  local copies, waits for them, and re-layouts  15.3 us (10%)
  matrix products  15.1 us (10%)
  other arithmetic  6.82 us (5%)
  between operations  1.55 us (1%)
    all_to_all x1, blocking collectives, carried_in(): parts = lax.all_to_all(rows, axis, 0, 0)  34 us
    ppermute x8, waiting for transfers between devices, butterfly_sum(): lax.ppermute(value, axis, [(i, i ^ step) for i in range(count)])  18.9 us
    all_to_all x2, waiting for transfers between devices, carried_in(): back = lax.all_to_all(shifted, axis, 0, 0)  16.2 us
    ppermute x8, starting transfers between devices, butterfly_sum(): lax.ppermute(value, axis, [(i, i ^ step) for i in range(count)])  13.5 us
    unnamed x34, local copies, waits for them, and re-layouts  12.1 us
    all_to_all x2, starting transfers between devices, carried_in(): back = lax.all_to_all(shifted, axis, 0, 0)  10.3 us
    all_to_all x1, waiting for transfers between devices, carried_in(): parts = lax.all_to_all(rows, axis, 0, 0)  8.69 us
    all_to_all x1, starting transfers between devices, carried_in(): parts = lax.all_to_all(rows, axis, 0, 0)  5.14 us
  transfers between devices with their start and end apart: 11, of which 8 were waited for; matrix products, arithmetic and copies ran while one was open for 13% of the time, Pallas kernels for 0%

profile of v6, /device:TPU:16, one launch (start us, length us, event | category | flops | bytes accessed | tf_op | source)
XLA Modules:
  0.0 145.5 jit_solution(13076239780083069935)
XLA Ops:
  0.6 1.5 %copy.60 = bf16[1,256,1536]{1,2,0:T(8,128)(2,1)S(1)} copy(bf16[1,256,1536]{2,1,0:T(8,128)(2,1)} %param.6) | data formatting | bytes 1572864 | tf_op args[1]
  2.8 34.0 %all_to_all.20 = f32[32,48,128]{2,1,0:T(8,128)S(1)} all-to-all(f32[32,48,128]{2,1,0:T(8,128)S(1)} %bitcast.105), channel_id=1, replica_groups=mesh['dp'=8,'seq'=32] {'seq'}, dimensions={0} | all-to-all | bytes 1572864 | tf_op jit(solution)/shard_map/all_to_all | solution.py:18
  38.9 5.4 %all-to-all-start.1 = ((f32[32,48,128]{2,1,0:T(8,128)}), f32[32,48,128]{2,1,0:T(8,128)}, u32[]{:S(2)}, u32[]{:S(2)}) async-start(f32[32,48,128]{2,1,0:T(8,128)} %copy.64), calls=%async_computation.1 | async-start | bytes 1572864 | tf_op jit(solution)/shard_map/all_to_all | solution.py:31
  44.6 1.7 %copy.65 = bf16[1,256,1536]{1,2,0:T(8,128)(2,1)S(1)} copy(bf16[1,256,1536]{2,1,0:T(8,128)(2,1)} %param.5) | data formatting | bytes 1572864 | tf_op args[0]
  48.2 1.8 %fusion.22 = f32[12,256,128]{1,2,0:T(8,128)} fusion(bf16[12,256,256]{2,1,0:T(8,128)(2,1)S(1)} %select_convert_fusion.1, bf16[256,12,128]{0,2,1:T(8,128)(2,1)S(1)} %bitcast.89), kind=kOutput, calls=%fused_computation.39 | convolution fusion | flops 201326592 | bytes 3932160 | tf_op jit(solution)/shard_map/nhct,nthe->nche/dot_general | solution.py:71
  49.9 16.2 %all-to-all-done.1 = f32[32,48,128]{2,1,0:T(8,128)} async-done(((f32[32,48,128]{2,1,0:T(8,128)}), f32[32,48,128]{2,1,0:T(8,128)}, u32[]{:S(2)}, u32[]{:S(2)}) %all-to-all-start.1) | async-done | bytes 786464 | tf_op jit(solution)/shard_map/all_to_all | solution.py:31
  66.1 1.6 %add_convert_fusion.1 = bf16[12,128,128]{2,1,0:T(8,128)(2,1)S(1)} fusion(f32[12,128,128]{2,1,0:T(8,128)} %bitcast.4, f32[12,128,128]{2,1,0:T(8,128)} %copy-done.3), kind=kLoop, calls=%fused_computation.27 | loop fusion | flops 589824 | bytes 1966080 | tf_op jit(solution)/shard_map/convert_element_type | solution.py:67
  69.5 2.5 %fusion.4 = (bf16[1,256,1536]{1,2,0:T(8,128)(2,1)S(1)}, bf16[1,256,1536]{1,2,0:T(8,128)(2,1)}) fusion(bf16[1,256,1536]{1,2,0:T(8,128)(2,1)} %copy-done.1, f32[12,128,256]{2,1,0:T(8,128)S(1)} %get-tuple-element.25, f32[256]{0:T(256)S(1)} %broadcast_multiply_fusion, f32[1536]{0:T(1024)S(1)} %copy-done.12, f32[256]{0:T(256)S(1)} %add_rsqrt_fusion), kind=kLoop, calls=%fused_computation.8 | loop fusion | flops 3538944 | bytes 3940352 | tf_op jit(solution)/shard_map/convert_element_type | solution.py:84
  73.2 5.1 %all-to-all-start.2 = ((f32[32,48,128]{2,1,0:T(8,128)}), f32[32,48,128]{2,1,0:T(8,128)}, u32[]{:S(2)}, u32[]{:S(2)}) async-start(f32[32,48,128]{2,1,0:T(8,128)} %bitcast.104), calls=%async_computation.2 | async-start | bytes 1572864 | tf_op jit(solution)/shard_map/all_to_all | solution.py:18
  80.9 2.4 %collective-permute-done.1 = f32[1536]{0:T(1024)S(1)} collective-permute-done((f32[1536]{0:T(1024)S(1)}, f32[1536]{0:T(1024)S(1)}, u32[]{:S(2)}, u32[]{:S(2)}) %collective-permute-start.1) | collective-permute-done | bytes 6176 | tf_op jit(solution)/shard_map/ppermute | solution.py:40
  83.6 4.8 %collective-permute-done.2 = f32[1536]{0:T(1024)S(1)} collective-permute-done((f32[1536]{0:T(1024)S(1)}, f32[1536]{0:T(1024)S(1)}, u32[]{:S(2)}, u32[]{:S(2)}) %collective-permute-start.2) | collective-permute-done | bytes 6176 | tf_op jit(solution)/shard_map/ppermute | solution.py:40
  88.9 1.7 %collective-permute-start.3 = (f32[1536]{0:T(1024)S(1)}, f32[1536]{0:T(1024)S(1)}, u32[]{:S(2)}, u32[]{:S(2)}) collective-permute-start(f32[1536]{0:T(1024)S(1)} %add.82), channel_id=1, source_target_pairs={{0,1},{1,0},{2,3},{3,2},{4,5},{5,4},{6,7},{7,6},{8,9},{9,8},{10,11... | collective-permute-start | bytes 18440 | tf_op jit(solution)/shard_map/ppermute | solution.py:40
  91.3 8.7 %all-to-all-done.2 = f32[32,48,128]{2,1,0:T(8,128)} async-done(((f32[32,48,128]{2,1,0:T(8,128)}), f32[32,48,128]{2,1,0:T(8,128)}, u32[]{:S(2)}, u32[]{:S(2)}) %all-to-all-start.2) | async-done | bytes 786464 | tf_op jit(solution)/shard_map/all_to_all | solution.py:18
  100.0 2.1 %fusion.11 = f32[32,48,128]{2,0,1:T(8,128)S(1)} fusion(f32[32,48,128]{2,1,0:T(8,128)} %all-to-all-done.2, f32[]{:T(128)} %bitcast.16), kind=kOutput, calls=%fused_computation.23 | convolution fusion | flops 75500544 | bytes 1572868 | tf_op jit(solution)/shard_map/ij,jkl->ikl/dot_general | solution.py:24
  102.1 1.4 copy.76
  103.4 4.9 %all-to-all-start.3 = ((f32[32,48,128]{2,1,0:T(8,128)}), f32[32,48,128]{2,1,0:T(8,128)}, u32[]{:S(2)}, u32[]{:S(2)}) async-start(f32[32,48,128]{2,1,0:T(8,128)} %copy.76), calls=%async_computation.3 | async-start | bytes 1572864 | tf_op jit(solution)/shard_map/all_to_all | solution.py:31
  108.4 3.0 %fusion.25 = f32[12,128,256]{2,1,0:T(8,128)} fusion(bf16[256,12,128]{0,2,1:T(8,128)(2,1)S(1)} %bitcast.97, bf16[12,256,256]{2,1,0:T(8,128)(2,1)} %copy-done), kind=kOutput, calls=%fused_computation.42 | convolution fusion | flops 201326592 | bytes 3932160 | tf_op jit(solution)/shard_map/nhct,nche->nthe/dot_general | solution.py:113
  111.3 3.2 %collective-permute-start.4 = (f32[1536]{0:T(1024)S(1)}, f32[1536]{0:T(1024)S(1)}, u32[]{:S(2)}, u32[]{:S(2)}) collective-permute-start(f32[1536]{0:T(1024)S(1)} %add.88), channel_id=1, source_target_pairs={{0,2},{1,3},{2,0},{3,1},{4,6},{5,7},{6,4},{7,5},{8,10},{9,11},{10,... | collective-permute-start | bytes 18440 | tf_op jit(solution)/shard_map/ppermute | solution.py:40
  116.5 1.8 %collective-permute-start.5 = (f32[1536]{0:T(1024)S(1)}, f32[1536]{0:T(1024)S(1)}, u32[]{:S(2)}, u32[]{:S(2)}) collective-permute-start(f32[1536]{0:T(1024)S(1)} %add.89), channel_id=1, source_target_pairs={{0,4},{1,5},{2,6},{3,7},{4,0},{5,1},{6,2},{7,3},{8,12},{9,13},{10,... | collective-permute-start | bytes 18440 | tf_op jit(solution)/shard_map/ppermute | solution.py:40
  118.3 1.6 %fusion.26 = f32[12,256,128]{1,2,0:T(8,128)} fusion(bf16[256,12,128]{0,2,1:T(8,128)(2,1)S(1)} %bitcast.103, bf16[12,256,256]{2,1,0:T(8,128)(2,1)S(1)} %select_convert_fusion), kind=kOutput, calls=%fused_computation.43 | convolution fusion | flops 201326592 | bytes 3932160 | tf_op jit(solution)/shard_map/nhct,nchd->nthd/dot_general | solution.py:107
  119.9 5.8 %collective-permute-done.5 = f32[1536]{0:T(1024)S(1)} collective-permute-done((f32[1536]{0:T(1024)S(1)}, f32[1536]{0:T(1024)S(1)}, u32[]{:S(2)}, u32[]{:S(2)}) %collective-permute-start.5) | collective-permute-done | bytes 6176 | tf_op jit(solution)/shard_map/ppermute | solution.py:40
  126.9 3.4 %collective-permute-done.6 = f32[1536]{0:T(1024)S(1)} collective-permute-done((f32[1536]{0:T(1024)S(1)}, f32[1536]{0:T(1024)S(1)}, u32[]{:S(2)}, u32[]{:S(2)}) %collective-permute-start.6) | collective-permute-done | bytes 6176 | tf_op jit(solution)/shard_map/ppermute | solution.py:40
  130.3 4.5 %collective-permute-start.7 = (f32[1536]{0:T(1024)S(1)}, f32[1536]{0:T(1024)S(1)}, u32[]{:S(2)}, u32[]{:S(2)}) collective-permute-start(f32[1536]{0:T(1024)S(1)} %add.91), channel_id=1, source_target_pairs={{0,16},{1,17},{2,18},{3,19},{4,20},{5,21},{6,22},{7,23},{8,24},{9,... | collective-permute-start | bytes 18440 | tf_op jit(solution)/shard_map/ppermute | solution.py:40
  136.0 2.4 %copy.80 = bf16[1,256,1536]{2,1,0:T(8,128)(2,1)} copy(bf16[1,256,1536]{1,2,0:T(8,128)(2,1)} %get-tuple-element.23) | data formatting | bytes 1572864
  (65 shorter events, 22.6 us)
Async XLA Ops:
  0.6 1.5 %copy-start.8 = (bf16[1,256,1536]{2,1,0:T(8,128)(2,1)S(1)}, bf16[1,256,1536]{2,1,0:T(8,128)(2,1)}, u32[]{:S(2)}) copy-start(bf16[1,256,1536]{2,1,0:T(8,128)(2,1)} %param.7) | copy-start | bytes 2359300
  2.8 34.8 %copy-start.3 = (f32[12,128,128]{2,1,0:T(8,128)}, f32[12,128,128]{2,1,0:T(8,128)S(1)}, u32[]{:S(2)}) copy-start(f32[12,128,128]{2,1,0:T(8,128)S(1)} %fusion.21) | copy-start | bytes 2359300
  38.9 5.4 %copy-start.9 = (bf16[1,256,1536]{2,1,0:T(8,128)(2,1)S(1)}, bf16[1,256,1536]{2,1,0:T(8,128)(2,1)}, u32[]{:S(2)}) copy-start(bf16[1,256,1536]{2,1,0:T(8,128)(2,1)} %param.9) | copy-start | bytes 2359300
  38.9 27.2 %all-to-all-start.1 = ((f32[32,48,128]{2,1,0:T(8,128)}), f32[32,48,128]{2,1,0:T(8,128)}, u32[]{:S(2)}, u32[]{:S(2)}) async-start(f32[32,48,128]{2,1,0:T(8,128)} %copy.64), calls=%async_computation.1 | async-start | bytes 1572864 | tf_op jit(solution)/shard_map/all_to_all | solution.py:31
  44.6 23.9 %copy-start.1 = (bf16[1,256,1536]{1,2,0:T(8,128)(2,1)}, bf16[1,256,1536]{1,2,0:T(8,128)(2,1)S(1)}, u32[]{:S(2)}) copy-start(bf16[1,256,1536]{1,2,0:T(8,128)(2,1)S(1)} %copy.70) | copy-start | bytes 2359300
  46.3 0.7 copy-start.10
  47.0 1.2 copy-start
  66.1 1.9 %copy-start.6 = (f32[12,256,128]{1,2,0:T(8,128)S(1)}, f32[12,256,128]{1,2,0:T(8,128)}, u32[]{:S(2)}) copy-start(f32[12,256,128]{1,2,0:T(8,128)} %fusion.22) | copy-start | bytes 4718596
  68.0 0.7 copy-start.12
  73.2 26.8 %all-to-all-start.2 = ((f32[32,48,128]{2,1,0:T(8,128)}), f32[32,48,128]{2,1,0:T(8,128)}, u32[]{:S(2)}, u32[]{:S(2)}) async-start(f32[32,48,128]{2,1,0:T(8,128)} %bitcast.104), calls=%async_computation.2 | async-start | bytes 1572864 | tf_op jit(solution)/shard_map/all_to_all | solution.py:18
  78.3 1.3 collective-permute-start
  79.6 3.7 %collective-permute-start.1 = (f32[1536]{0:T(1024)S(1)}, f32[1536]{0:T(1024)S(1)}, u32[]{:S(2)}, u32[]{:S(2)}) collective-permute-start(f32[1536]{0:T(1024)S(1)} %add.80), channel_id=1, source_target_pairs={{0,64},{32,96},{64,0},{96,32},{128,192},{160,224},{192,128},{224,1... | collective-permute-start | bytes 18440 | tf_op jit(solution)/shard_map/ppermute | solution.py:40
  83.3 5.2 %collective-permute-start.2 = (f32[1536]{0:T(1024)S(1)}, f32[1536]{0:T(1024)S(1)}, u32[]{:S(2)}, u32[]{:S(2)}) collective-permute-start(f32[1536]{0:T(1024)S(1)} %add.81), channel_id=1, source_target_pairs={{0,128},{32,160},{64,192},{96,224},{128,0},{160,32},{192,64},{224,... | collective-permute-start | bytes 18440 | tf_op jit(solution)/shard_map/ppermute | solution.py:40
  88.9 22.4 %collective-permute-start.3 = (f32[1536]{0:T(1024)S(1)}, f32[1536]{0:T(1024)S(1)}, u32[]{:S(2)}, u32[]{:S(2)}) collective-permute-start(f32[1536]{0:T(1024)S(1)} %add.82), channel_id=1, source_target_pairs={{0,1},{1,0},{2,3},{3,2},{4,5},{5,4},{6,7},{7,6},{8,9},{9,8},{10,11... | collective-permute-start | bytes 18440 | tf_op jit(solution)/shard_map/ppermute | solution.py:40
  103.4 36.8 %all-to-all-start.3 = ((f32[32,48,128]{2,1,0:T(8,128)}), f32[32,48,128]{2,1,0:T(8,128)}, u32[]{:S(2)}, u32[]{:S(2)}) async-start(f32[32,48,128]{2,1,0:T(8,128)} %copy.76), calls=%async_computation.3 | async-start | bytes 1572864 | tf_op jit(solution)/shard_map/all_to_all | solution.py:31
  108.4 6.2 %copy-start.11 = (pred[256,256]{1,0:T(8,128)(4,1)S(1)}, pred[256,256]{1,0:T(8,128)(4,1)}, u32[]{:S(2)}) copy-start(pred[256,256]{1,0:T(8,128)(4,1)} %copy-done.10) | copy-start | bytes 196612
  111.3 5.2 %collective-permute-start.4 = (f32[1536]{0:T(1024)S(1)}, f32[1536]{0:T(1024)S(1)}, u32[]{:S(2)}, u32[]{:S(2)}) collective-permute-start(f32[1536]{0:T(1024)S(1)} %add.88), channel_id=1, source_target_pairs={{0,2},{1,3},{2,0},{3,1},{4,6},{5,7},{6,4},{7,5},{8,10},{9,11},{10,... | collective-permute-start | bytes 18440 | tf_op jit(solution)/shard_map/ppermute | solution.py:40
  116.5 9.2 %collective-permute-start.5 = (f32[1536]{0:T(1024)S(1)}, f32[1536]{0:T(1024)S(1)}, u32[]{:S(2)}, u32[]{:S(2)}) collective-permute-start(f32[1536]{0:T(1024)S(1)} %add.89), channel_id=1, source_target_pairs={{0,4},{1,5},{2,6},{3,7},{4,0},{5,1},{6,2},{7,3},{8,12},{9,13},{10,... | collective-permute-start | bytes 18440 | tf_op jit(solution)/shard_map/ppermute | solution.py:40
  125.7 4.5 %collective-permute-start.6 = (f32[1536]{0:T(1024)S(1)}, f32[1536]{0:T(1024)S(1)}, u32[]{:S(2)}, u32[]{:S(2)}) collective-permute-start(f32[1536]{0:T(1024)S(1)} %add.90), channel_id=1, source_target_pairs={{0,8},{1,9},{2,10},{3,11},{4,12},{5,13},{6,14},{7,15},{8,0},{9,1},... | collective-permute-start | bytes 18440 | tf_op jit(solution)/shard_map/ppermute | solution.py:40
  130.3 9.3 %collective-permute-start.7 = (f32[1536]{0:T(1024)S(1)}, f32[1536]{0:T(1024)S(1)}, u32[]{:S(2)}, u32[]{:S(2)}) collective-permute-start(f32[1536]{0:T(1024)S(1)} %add.91), channel_id=1, source_target_pairs={{0,16},{1,17},{2,18},{3,19},{4,20},{5,21},{6,22},{7,23},{8,24},{9,... | collective-permute-start | bytes 18440 | tf_op jit(solution)/shard_map/ppermute | solution.py:40
  136.0 2.4 %copy-start.7 = (bf16[12,128,256]{2,1,0:T(8,128)(2,1)S(1)}, bf16[12,128,256]{2,1,0:T(8,128)(2,1)}, u32[]{:S(2)}) copy-start(bf16[12,128,256]{2,1,0:T(8,128)(2,1)} %fusion.7) | copy-start | bytes 2359300
  136.0 4.2 %copy-start.2 = (f32[12,128,128]{1,2,0:T(8,128)S(1)}, f32[12,128,128]{1,2,0:T(8,128)}, u32[]{:S(2)}) copy-start(f32[12,128,128]{1,2,0:T(8,128)} %fusion.24) | copy-start | bytes 2359300
  140.2 1.6 %copy-start.4 = (f32[12,128,256]{2,1,0:T(8,128)S(1)}, f32[12,128,256]{2,1,0:T(8,128)}, u32[]{:S(2)}) copy-start(f32[12,128,256]{2,1,0:T(8,128)} %fusion.25) | copy-start | bytes 4718596
  142.3 1.7 %copy-start.5 = (f32[12,256,128]{1,2,0:T(8,128)S(1)}, f32[12,256,128]{1,2,0:T(8,128)}, u32[]{:S(2)}) copy-start(f32[12,256,128]{1,2,0:T(8,128)} %fusion.26) | copy-start | bytes 4718596

commit v7 on v6

--- a/solution.py
+++ b/solution.py
@@ -32,13 +32,19 @@
     return back.reshape(value.shape)
 
 
-def butterfly_sum(value, axis, first=1, last=None):
+def butterfly_sum(value, axis, radices):
     count = lax.axis_size(axis)
-    last = count if last is None else last
-    step = first
-    while step < last:
-        value = value + lax.ppermute(value, axis, [(i, i ^ step) for i in range(count)])
-        step *= 2
+    step = 1
+    for radix in radices:
+        vals = [value] + [
+            lax.ppermute(value, axis, [(i, i ^ (k * step)) for i in range(count)])
+            for k in range(1, radix)
+        ]
+        while len(vals) > 1:
+            vals = [vals[m] + vals[m + 1] for m in range(0, len(vals), 2)]
+        value = vals[0]
+        step *= radix
+    assert step == count
     return value
 
 
@@ -85,9 +91,9 @@
     query_parts = jnp.einsum(
         "nchd,nche->nhde", queries, grad_blocks, preferred_element_type=jnp.float32
     )
-    gain_dp = butterfly_sum(gain_terms, "dp")
+    gain_dp = butterfly_sum(gain_terms, "dp", (8,))
     suffix = carried_in(jnp.sum(query_parts, axis=0), "seq", True, gain_dp[0])
-    grad_gain = butterfly_sum(gain_dp, "seq")
+    grad_gain = butterfly_sum(gain_dp, "seq", (4, 8))
     from_end = lax.cumsum(query_parts, axis=0, reverse=True)
     behind = jnp.concatenate([from_end[1:], query_parts[-1:] * 0.0], axis=0)
     suffix_states = (suffix[None] + behind).astype(jnp.bfloat16)

time: 146 us -> 149 us (1.021)
  waiting for transfers between devices: 43.8 us -> 28.2 us
  starting transfers between devices: 28.9 us -> 41.8 us
  matrix products: 15.1 us -> 17.8 us
  local copies, waits for them, and re-layouts: 15.3 us -> 17.1 us
    ppermute x8 -> x17, waiting for transfers between devices: 18.9 us -> 2.58 us  [butterfly_sum(): lax.ppermute(value, axis, [(i, i ^ k * step) for i in range(count)])]
    ppermute x8 -> x17, starting transfers between devices: 13.5 us -> 26.3 us  [butterfly_sum(): lax.ppermute(value, axis, [(i, i ^ k * step) for i in range(count)])]
    unnamed x34 -> x36, local copies, waits for them, and re-layouts: 12.1 us -> 13.8 us
  transfers between devices with their start and end apart: 11 -> 20, of which waited for: 8 -> 3; matrix products, arithmetic and copies ran while one was open for 13% -> 12% of each run, Pallas kernels for 0% -> 0%
where the time goes in v7:
time: 149 us; the launch traced here: 148 us
  starting transfers between devices  41.8 us (28%)
  blocking collectives  34 us (23%)
  waiting for transfers between devices  28.2 us (19%)
  matrix products  17.8 us (12%)
  local copies, waits for them, and re-layouts  17.1 us (11%)
  other arithmetic  7.58 us (5%)
  between operations  1.59 us (1%)
    all_to_all x1, blocking collectives, carried_in(): parts = lax.all_to_all(rows, axis, 0, 0)  34 us
    ppermute x17, starting transfers between devices, butterfly_sum(): lax.ppermute(value, axis, [(i, i ^ k * step) for i in range(count)])  26.3 us
    all_to_all x2, waiting for transfers between devices, carried_in(): back = lax.all_to_all(shifted, axis, 0, 0)  16.1 us
    unnamed x36, local copies, waits for them, and re-layouts  13.8 us
    all_to_all x2, starting transfers between devices, carried_in(): back = lax.all_to_all(shifted, axis, 0, 0)  10.3 us
    all_to_all x1, waiting for transfers between devices, carried_in(): parts = lax.all_to_all(rows, axis, 0, 0)  9.48 us
    all_to_all x1, starting transfers between devices, carried_in(): parts = lax.all_to_all(rows, axis, 0, 0)  5.14 us
    dot_general x1, matrix products, local_body(): jnp.einsum('nhct,nche->nthe', weights, grad_blocks, preferred_element_typ...  2.98 us
  transfers between devices with their start and end apart: 20, of which 3 were waited for; matrix products, arithmetic and copies ran while one was open for 12% of the time, Pallas kernels for 0%

profile of v7, /device:TPU:16, one launch (start us, length us, event | category | flops | bytes accessed | tf_op | source)
XLA Modules:
  0.0 148.0 jit_solution(6536228671278665711)
XLA Ops:
  2.8 34.0 %all_to_all.20 = f32[32,48,128]{2,1,0:T(8,128)S(1)} all-to-all(f32[32,48,128]{2,1,0:T(8,128)S(1)} %bitcast.105), channel_id=1, replica_groups=mesh['dp'=8,'seq'=32] {'seq'}, dimensions={0} | all-to-all | bytes 1572864 | tf_op jit(solution)/shard_map/all_to_all | solution.py:18
  38.9 5.4 %all-to-all-start.1 = ((f32[32,48,128]{2,1,0:T(8,128)}), f32[32,48,128]{2,1,0:T(8,128)}, u32[]{:S(2)}, u32[]{:S(2)}) async-start(f32[32,48,128]{2,1,0:T(8,128)} %copy.64), calls=%async_computation.1 | async-start | bytes 1572864 | tf_op jit(solution)/shard_map/all_to_all | solution.py:31
  44.6 1.7 %copy.65 = bf16[1,256,1536]{1,2,0:T(8,128)(2,1)S(1)} copy(bf16[1,256,1536]{2,1,0:T(8,128)(2,1)} %param.5) | data formatting | bytes 1572864 | tf_op args[0]
  48.1 1.8 %fusion.22 = f32[12,256,128]{1,2,0:T(8,128)} fusion(bf16[12,256,256]{2,1,0:T(8,128)(2,1)S(1)} %select_convert_fusion.1, bf16[256,12,128]{0,2,1:T(8,128)(2,1)S(1)} %bitcast.89), kind=kOutput, calls=%fused_computation.42 | convolution fusion | flops 201326592 | bytes 3932160 | tf_op jit(solution)/shard_map/nhct,nthe->nche/dot_general | solution.py:77
  50.0 16.1 %all-to-all-done.1 = f32[32,48,128]{2,1,0:T(8,128)} async-done(((f32[32,48,128]{2,1,0:T(8,128)}), f32[32,48,128]{2,1,0:T(8,128)}, u32[]{:S(2)}, u32[]{:S(2)}) %all-to-all-start.1) | async-done | bytes 786464 | tf_op jit(solution)/shard_map/all_to_all | solution.py:31
  66.1 1.6 %add_convert_fusion.1 = bf16[12,128,128]{2,1,0:T(8,128)(2,1)S(1)} fusion(f32[12,128,128]{2,1,0:T(8,128)} %bitcast.4, f32[12,128,128]{2,1,0:T(8,128)} %copy-done.3), kind=kLoop, calls=%fused_computation.27 | loop fusion | flops 589824 | bytes 1966080 | tf_op jit(solution)/shard_map/convert_element_type | solution.py:73
  69.5 2.5 %fusion.4 = (bf16[1,256,1536]{1,2,0:T(8,128)(2,1)S(1)}, bf16[1,256,1536]{1,2,0:T(8,128)(2,1)}) fusion(bf16[1,256,1536]{1,2,0:T(8,128)(2,1)} %copy-done.1, f32[12,128,256]{2,1,0:T(8,128)S(1)} %get-tuple-element.25, f32[256]{0:T(256)S(1)} %broadcast_multiply_fusion, f32[1536]{0:T(1024)S(1)} %copy-done.11, f32[256]{0:T(256)S(1)} %add_rsqrt_fusion), kind=kLoop, calls=%fused_computation.8 | loop fusion | flops 3538944 | bytes 3940352 | tf_op jit(solution)/shard_map/convert_element_type | solution.py:90
  73.2 5.1 %all-to-all-start.2 = ((f32[32,48,128]{2,1,0:T(8,128)}), f32[32,48,128]{2,1,0:T(8,128)}, u32[]{:S(2)}, u32[]{:S(2)}) async-start(f32[32,48,128]{2,1,0:T(8,128)} %bitcast.104), calls=%async_computation.2 | async-start | bytes 1572864 | tf_op jit(solution)/shard_map/all_to_all | solution.py:18
  79.0 2.5 %collective-permute-start.4 = (f32[1536]{0:T(1024)S(1)}, f32[1536]{0:T(1024)S(1)}, u32[]{:S(2)}, u32[]{:S(2)}) collective-permute-start(f32[1536]{0:T(1024)S(1)} %get-tuple-element.20), channel_id=1, source_target_pairs={{0,160},{32,128},{64,224},{96,192},{128,32},{160,0},{192,96},{224,... | collective-permute-start | bytes 18440 | tf_op jit(solution)/shard_map/ppermute | solution.py:40
  81.5 1.9 %collective-permute-start.3 = (f32[1536]{0:T(1024)S(1)}, f32[1536]{0:T(1024)S(1)}, u32[]{:S(2)}, u32[]{:S(2)}) collective-permute-start(f32[1536]{0:T(1024)S(1)} %get-tuple-element.20), channel_id=1, source_target_pairs={{0,128},{32,160},{64,192},{96,224},{128,0},{160,32},{192,64},{224,... | collective-permute-start | bytes 18440 | tf_op jit(solution)/shard_map/ppermute | solution.py:40
  83.5 2.4 %collective-permute-start.1 = (f32[1536]{0:T(1024)S(1)}, f32[1536]{0:T(1024)S(1)}, u32[]{:S(2)}, u32[]{:S(2)}) collective-permute-start(f32[1536]{0:T(1024)S(1)} %get-tuple-element.20), channel_id=1, source_target_pairs={{0,64},{32,96},{64,0},{96,32},{128,192},{160,224},{192,128},{224,1... | collective-permute-start | bytes 18440 | tf_op jit(solution)/shard_map/ppermute | solution.py:40
  86.3 3.0 %fusion.25 = f32[12,128,256]{2,1,0:T(8,128)} fusion(bf16[256,12,128]{0,2,1:T(8,128)(2,1)S(1)} %bitcast.97, bf16[12,256,256]{2,1,0:T(8,128)(2,1)} %copy-done), kind=kOutput, calls=%fused_computation.45 | convolution fusion | flops 201326592 | bytes 3932160 | tf_op jit(solution)/shard_map/nhct,nche->nthe/dot_general | solution.py:119
  90.5 9.5 %all-to-all-done.2 = f32[32,48,128]{2,1,0:T(8,128)} async-done(((f32[32,48,128]{2,1,0:T(8,128)}), f32[32,48,128]{2,1,0:T(8,128)}, u32[]{:S(2)}, u32[]{:S(2)}) %all-to-all-start.2) | async-done | bytes 786464 | tf_op jit(solution)/shard_map/all_to_all | solution.py:18
  100.0 2.1 %fusion.11 = f32[32,48,128]{2,0,1:T(8,128)S(1)} fusion(f32[32,48,128]{2,1,0:T(8,128)} %all-to-all-done.2, f32[]{:T(128)} %bitcast.16), kind=kOutput, calls=%fused_computation.23 | convolution fusion | flops 75500544 | bytes 1572868 | tf_op jit(solution)/shard_map/ij,jkl->ikl/dot_general | solution.py:24
  103.4 4.9 %all-to-all-start.3 = ((f32[32,48,128]{2,1,0:T(8,128)}), f32[32,48,128]{2,1,0:T(8,128)}, u32[]{:S(2)}, u32[]{:S(2)}) async-start(f32[32,48,128]{2,1,0:T(8,128)} %copy.76), calls=%async_computation.3 | async-start | bytes 1572864 | tf_op jit(solution)/shard_map/all_to_all | solution.py:31
  109.8 3.0 %collective-permute-start.9 = (f32[1536]{0:T(1024)S(1)}, f32[1536]{0:T(1024)S(1)}, u32[]{:S(2)}, u32[]{:S(2)}) collective-permute-start(f32[1536]{0:T(1024)S(1)} %add_add_fusion.2), channel_id=1, source_target_pairs={{0,3},{1,2},{2,1},{3,0},{4,7},{5,6},{6,5},{7,4},{8,11},{9,10},{10,... | collective-permute-start | bytes 18440 | tf_op jit(solution)/shard_map/ppermute | solution.py:40
  115.6 2.5 %collective-permute-done.8 = f32[1536]{0:T(1024)S(1)} collective-permute-done((f32[1536]{0:T(1024)S(1)}, f32[1536]{0:T(1024)S(1)}, u32[]{:S(2)}, u32[]{:S(2)}) %collective-permute-start.8) | collective-permute-done | bytes 6176 | tf_op jit(solution)/shard_map/ppermute | solution.py:40
  118.1 2.9 %collective-permute-start.16 = (f32[1536]{0:T(1024)S(1)}, f32[1536]{0:T(1024)S(1)}, u32[]{:S(2)}, u32[]{:S(2)}) collective-permute-start(f32[1536]{0:T(1024)S(1)} %add_add_fusion.1), channel_id=1, source_target_pairs={{0,28},{1,29},{2,30},{3,31},{4,24},{5,25},{6,26},{7,27},{8,20},{9,... | collective-permute-start | bytes 18440 | tf_op jit(solution)/shard_map/ppermute | solution.py:40
  121.1 2.1 %collective-permute-start.15 = (f32[1536]{0:T(1024)S(1)}, f32[1536]{0:T(1024)S(1)}, u32[]{:S(2)}, u32[]{:S(2)}) collective-permute-start(f32[1536]{0:T(1024)S(1)} %add_add_fusion.1), channel_id=1, source_target_pairs={{0,24},{1,25},{2,26},{3,27},{4,28},{5,29},{6,30},{7,31},{8,16},{9,... | collective-permute-start | bytes 18440 | tf_op jit(solution)/shard_map/ppermute | solution.py:40
  123.8 3.7 %collective-permute-start.14 = (f32[1536]{0:T(1024)S(1)}, f32[1536]{0:T(1024)}, u32[]{:S(2)}, u32[]{:S(2)}) collective-permute-start(f32[1536]{0:T(1024)S(1)} %add_add_fusion.1), channel_id=1, source_target_pairs={{0,20},{1,21},{2,22},{3,23},{4,16},{5,17},{6,18},{7,19},{8,28},{9,... | collective-permute-start | bytes 18440 | tf_op jit(solution)/shard_map/ppermute | solution.py:40
  128.6 3.1 %collective-permute-start.12 = (f32[1536]{0:T(1024)S(1)}, f32[1536]{0:T(1024)}, u32[]{:S(2)}, u32[]{:S(2)}) collective-permute-start(f32[1536]{0:T(1024)S(1)} %add_add_fusion.1), channel_id=1, source_target_pairs={{0,12},{1,13},{2,14},{3,15},{4,8},{5,9},{6,10},{7,11},{8,4},{9,5},... | collective-permute-start | bytes 18440 | tf_op jit(solution)/shard_map/ppermute | solution.py:40
  135.4 2.3 %copy.81 = bf16[1,256,1536]{2,1,0:T(8,128)(2,1)} copy(bf16[1,256,1536]{1,2,0:T(8,128)(2,1)} %bitcast.106) | data formatting | bytes 1572864
  142.0 2.4 %copy.83 = bf16[1,256,1536]{2,1,0:T(8,128)(2,1)} copy(bf16[1,256,1536]{1,2,0:T(8,128)(2,1)} %bitcast.108) | data formatting | bytes 1572864
  145.7 2.3 %copy.82 = bf16[1,256,1536]{2,1,0:T(8,128)(2,1)} copy(bf16[1,256,1536]{1,2,0:T(8,128)(2,1)} %bitcast.107) | data formatting | bytes 1572864
  (80 shorter events, 27.4 us)
Async XLA Ops:
  2.8 34.8 %copy-start.3 = (f32[12,128,128]{2,1,0:T(8,128)}, f32[12,128,128]{2,1,0:T(8,128)S(1)}, u32[]{:S(2)}) copy-start(f32[12,128,128]{2,1,0:T(8,128)S(1)} %fusion.21) | copy-start | bytes 2359300
  38.9 5.4 %copy-start.9 = (bf16[1,256,1536]{2,1,0:T(8,128)(2,1)S(1)}, bf16[1,256,1536]{2,1,0:T(8,128)(2,1)}, u32[]{:S(2)}) copy-start(bf16[1,256,1536]{2,1,0:T(8,128)(2,1)} %param.9) | copy-start | bytes 2359300
  38.9 27.2 %all-to-all-start.1 = ((f32[32,48,128]{2,1,0:T(8,128)}), f32[32,48,128]{2,1,0:T(8,128)}, u32[]{:S(2)}, u32[]{:S(2)}) async-start(f32[32,48,128]{2,1,0:T(8,128)} %copy.64), calls=%async_computation.1 | async-start | bytes 1572864 | tf_op jit(solution)/shard_map/all_to_all | solution.py:31
  44.6 23.9 %copy-start.1 = (bf16[1,256,1536]{1,2,0:T(8,128)(2,1)}, bf16[1,256,1536]{1,2,0:T(8,128)(2,1)S(1)}, u32[]{:S(2)}) copy-start(bf16[1,256,1536]{1,2,0:T(8,128)(2,1)S(1)} %copy.70) | copy-start | bytes 2359300
  73.2 26.8 %all-to-all-start.2 = ((f32[32,48,128]{2,1,0:T(8,128)}), f32[32,48,128]{2,1,0:T(8,128)}, u32[]{:S(2)}, u32[]{:S(2)}) async-start(f32[32,48,128]{2,1,0:T(8,128)} %bitcast.104), calls=%async_computation.2 | async-start | bytes 1572864 | tf_op jit(solution)/shard_map/all_to_all | solution.py:18
  78.3 5.2 %collective-permute-start.6 = (f32[1536]{0:T(1024)S(1)}, f32[1536]{0:T(1024)S(1)}, u32[]{:S(2)}, u32[]{:S(2)}) collective-permute-start(f32[1536]{0:T(1024)S(1)} %get-tuple-element.20), channel_id=1, source_target_pairs={{0,224},{32,192},{64,160},{96,128},{128,96},{160,64},{192,32},{224... | collective-permute-start | bytes 18440 | tf_op jit(solution)/shard_map/ppermute | solution.py:40
  78.4 7.5 %collective-permute-start.5 = (f32[1536]{0:T(1024)S(1)}, f32[1536]{0:T(1024)S(1)}, u32[]{:S(2)}, u32[]{:S(2)}) collective-permute-start(f32[1536]{0:T(1024)S(1)} %get-tuple-element.20), channel_id=1, source_target_pairs={{0,192},{32,224},{64,128},{96,160},{128,64},{160,96},{192,0},{224,... | collective-permute-start | bytes 18440 | tf_op jit(solution)/shard_map/ppermute | solution.py:40
  79.0 10.3 %collective-permute-start.4 = (f32[1536]{0:T(1024)S(1)}, f32[1536]{0:T(1024)S(1)}, u32[]{:S(2)}, u32[]{:S(2)}) collective-permute-start(f32[1536]{0:T(1024)S(1)} %get-tuple-element.20), channel_id=1, source_target_pairs={{0,160},{32,128},{64,224},{96,192},{128,32},{160,0},{192,96},{224,... | collective-permute-start | bytes 18440 | tf_op jit(solution)/shard_map/ppermute | solution.py:40
  81.5 7.8 %collective-permute-start.3 = (f32[1536]{0:T(1024)S(1)}, f32[1536]{0:T(1024)S(1)}, u32[]{:S(2)}, u32[]{:S(2)}) collective-permute-start(f32[1536]{0:T(1024)S(1)} %get-tuple-element.20), channel_id=1, source_target_pairs={{0,128},{32,160},{64,192},{96,224},{128,0},{160,32},{192,64},{224,... | collective-permute-start | bytes 18440 | tf_op jit(solution)/shard_map/ppermute | solution.py:40
  83.4 5.9 %collective-permute-start.2 = (f32[1536]{0:T(1024)S(1)}, f32[1536]{0:T(1024)S(1)}, u32[]{:S(2)}, u32[]{:S(2)}) collective-permute-start(f32[1536]{0:T(1024)S(1)} %get-tuple-element.20), channel_id=1, source_target_pairs={{0,96},{32,64},{64,32},{96,0},{128,224},{160,192},{192,160},{224,1... | collective-permute-start | bytes 18440 | tf_op jit(solution)/shard_map/ppermute | solution.py:40
  83.5 5.8 %collective-permute-start.1 = (f32[1536]{0:T(1024)S(1)}, f32[1536]{0:T(1024)S(1)}, u32[]{:S(2)}, u32[]{:S(2)}) collective-permute-start(f32[1536]{0:T(1024)S(1)} %get-tuple-element.20), channel_id=1, source_target_pairs={{0,64},{32,96},{64,0},{96,32},{128,192},{160,224},{192,128},{224,1... | collective-permute-start | bytes 18440 | tf_op jit(solution)/shard_map/ppermute | solution.py:40
  85.9 3.4 %collective-permute-start = (f32[1536]{0:T(1024)S(1)}, f32[1536]{0:T(1024)S(1)}, u32[]{:S(2)}, u32[]{:S(2)}) collective-permute-start(f32[1536]{0:T(1024)S(1)} %get-tuple-element.20), channel_id=1, source_target_pairs={{0,32},{32,0},{64,96},{96,64},{128,160},{160,128},{192,224},{224,1... | collective-permute-start | bytes 18440 | tf_op jit(solution)/shard_map/ppermute | solution.py:40
  103.4 35.6 %all-to-all-start.3 = ((f32[32,48,128]{2,1,0:T(8,128)}), f32[32,48,128]{2,1,0:T(8,128)}, u32[]{:S(2)}, u32[]{:S(2)}) async-start(f32[32,48,128]{2,1,0:T(8,128)} %copy.76), calls=%async_computation.3 | async-start | bytes 1572864 | tf_op jit(solution)/shard_map/all_to_all | solution.py:31
  109.8 5.7 %collective-permute-start.9 = (f32[1536]{0:T(1024)S(1)}, f32[1536]{0:T(1024)S(1)}, u32[]{:S(2)}, u32[]{:S(2)}) collective-permute-start(f32[1536]{0:T(1024)S(1)} %add_add_fusion.2), channel_id=1, source_target_pairs={{0,3},{1,2},{2,1},{3,0},{4,7},{5,6},{6,5},{7,4},{8,11},{9,10},{10,... | collective-permute-start | bytes 18440 | tf_op jit(solution)/shard_map/ppermute | solution.py:40
  112.9 5.2 %collective-permute-start.8 = (f32[1536]{0:T(1024)S(1)}, f32[1536]{0:T(1024)S(1)}, u32[]{:S(2)}, u32[]{:S(2)}) collective-permute-start(f32[1536]{0:T(1024)S(1)} %add_add_fusion.2), channel_id=1, source_target_pairs={{0,2},{1,3},{2,0},{3,1},{4,6},{5,7},{6,4},{7,5},{8,10},{9,11},{10,... | collective-permute-start | bytes 18440 | tf_op jit(solution)/shard_map/ppermute | solution.py:40
  113.7 4.4 %collective-permute-start.7 = (f32[1536]{0:T(1024)S(1)}, f32[1536]{0:T(1024)S(1)}, u32[]{:S(2)}, u32[]{:S(2)}) collective-permute-start(f32[1536]{0:T(1024)S(1)} %add_add_fusion.2), channel_id=1, source_target_pairs={{0,1},{1,0},{2,3},{3,2},{4,5},{5,4},{6,7},{7,6},{8,9},{9,8},{10,11... | collective-permute-start | bytes 18440 | tf_op jit(solution)/shard_map/ppermute | solution.py:40
  118.1 13.5 %collective-permute-start.16 = (f32[1536]{0:T(1024)S(1)}, f32[1536]{0:T(1024)S(1)}, u32[]{:S(2)}, u32[]{:S(2)}) collective-permute-start(f32[1536]{0:T(1024)S(1)} %add_add_fusion.1), channel_id=1, source_target_pairs={{0,28},{1,29},{2,30},{3,31},{4,24},{5,25},{6,26},{7,27},{8,20},{9,... | collective-permute-start | bytes 18440 | tf_op jit(solution)/shard_map/ppermute | solution.py:40
  121.1 10.8 %collective-permute-start.15 = (f32[1536]{0:T(1024)S(1)}, f32[1536]{0:T(1024)S(1)}, u32[]{:S(2)}, u32[]{:S(2)}) collective-permute-start(f32[1536]{0:T(1024)S(1)} %add_add_fusion.1), channel_id=1, source_target_pairs={{0,24},{1,25},{2,26},{3,27},{4,28},{5,29},{6,30},{7,31},{8,16},{9,... | collective-permute-start | bytes 18440 | tf_op jit(solution)/shard_map/ppermute | solution.py:40
  123.8 10.4 %copy-start.7 = (bf16[1,256,1536]{1,2,0:T(8,128)(2,1)S(1)}, bf16[1,256,1536]{1,2,0:T(8,128)(2,1)}, u32[]{:S(2)}) copy-start(bf16[1,256,1536]{1,2,0:T(8,128)(2,1)} %get-tuple-element.23) | copy-start | bytes 2359300
  123.8 13.8 %collective-permute-start.14 = (f32[1536]{0:T(1024)S(1)}, f32[1536]{0:T(1024)}, u32[]{:S(2)}, u32[]{:S(2)}) collective-permute-start(f32[1536]{0:T(1024)S(1)} %add_add_fusion.1), channel_id=1, source_target_pairs={{0,20},{1,21},{2,22},{3,23},{4,16},{5,17},{6,18},{7,19},{8,28},{9,... | collective-permute-start | bytes 18440 | tf_op jit(solution)/shard_map/ppermute | solution.py:40
  127.6 10.1 %collective-permute-start.13 = (f32[1536]{0:T(1024)S(1)}, f32[1536]{0:T(1024)}, u32[]{:S(2)}, u32[]{:S(2)}) collective-permute-start(f32[1536]{0:T(1024)S(1)} %add_add_fusion.1), channel_id=1, source_target_pairs={{0,16},{1,17},{2,18},{3,19},{4,20},{5,21},{6,22},{7,23},{8,24},{9,... | collective-permute-start | bytes 18440 | tf_op jit(solution)/shard_map/ppermute | solution.py:40
  128.6 9.1 %collective-permute-start.12 = (f32[1536]{0:T(1024)S(1)}, f32[1536]{0:T(1024)}, u32[]{:S(2)}, u32[]{:S(2)}) collective-permute-start(f32[1536]{0:T(1024)S(1)} %add_add_fusion.1), channel_id=1, source_target_pairs={{0,12},{1,13},{2,14},{3,15},{4,8},{5,9},{6,10},{7,11},{8,4},{9,5},... | collective-permute-start | bytes 18440 | tf_op jit(solution)/shard_map/ppermute | solution.py:40
  131.7 6.0 %collective-permute-start.11 = (f32[1536]{0:T(1024)S(1)}, f32[1536]{0:T(1024)}, u32[]{:S(2)}, u32[]{:S(2)}) collective-permute-start(f32[1536]{0:T(1024)S(1)} %add_add_fusion.1), channel_id=1, source_target_pairs={{0,8},{1,9},{2,10},{3,11},{4,12},{5,13},{6,14},{7,15},{8,0},{9,1},... | collective-permute-start | bytes 18440 | tf_op jit(solution)/shard_map/ppermute | solution.py:40
  131.9 5.8 %collective-permute-start.10 = (f32[1536]{0:T(1024)S(1)}, f32[1536]{0:T(1024)}, u32[]{:S(2)}, u32[]{:S(2)}) collective-permute-start(f32[1536]{0:T(1024)S(1)} %add_add_fusion.1), channel_id=1, source_target_pairs={{0,4},{1,5},{2,6},{3,7},{4,0},{5,1},{6,2},{7,3},{8,12},{9,13},{10,... | collective-permute-start | bytes 18440 | tf_op jit(solution)/shard_map/ppermute | solution.py:40
  (10 other events, 20.6 us)

commit v8 on v7

--- a/solution.py
+++ b/solution.py
@@ -32,19 +32,20 @@
     return back.reshape(value.shape)
 
 
-def butterfly_sum(value, axis, radices):
+def butterfly_sum(value, axis, step=1, stop=None):
     count = lax.axis_size(axis)
-    step = 1
-    for radix in radices:
-        vals = [value] + [
+    stop = count if stop is None else stop
+    while step < stop:
+        radix = 4 if step * 4 <= count else 2
+        got = [
             lax.ppermute(value, axis, [(i, i ^ (k * step)) for i in range(count)])
             for k in range(1, radix)
         ]
-        while len(vals) > 1:
-            vals = [vals[m] + vals[m + 1] for m in range(0, len(vals), 2)]
-        value = vals[0]
+        if radix == 4:
+            value = (value + got[0]) + (got[1] + got[2])
+        else:
+            value = value + got[0]
         step *= radix
-    assert step == count
     return value
 
 
@@ -91,9 +92,9 @@
     query_parts = jnp.einsum(
         "nchd,nche->nhde", queries, grad_blocks, preferred_element_type=jnp.float32
     )
-    gain_dp = butterfly_sum(gain_terms, "dp", (8,))
-    suffix = carried_in(jnp.sum(query_parts, axis=0), "seq", True, gain_dp[0])
-    grad_gain = butterfly_sum(gain_dp, "seq", (4, 8))
+    gain_near = butterfly_sum(butterfly_sum(gain_terms, "dp"), "seq", 1, 4)
+    suffix = carried_in(jnp.sum(query_parts, axis=0), "seq", True, gain_near[0])
+    grad_gain = butterfly_sum(gain_near, "seq", 4)
     from_end = lax.cumsum(query_parts, axis=0, reverse=True)
     behind = jnp.concatenate([from_end[1:], query_parts[-1:] * 0.0], axis=0)
     suffix_states = (suffix[None] + behind).astype(jnp.bfloat16)

time: 149 us -> 143 us (0.960)
  starting transfers between devices: 41.8 us -> 31 us
  waiting for transfers between devices: 28.2 us -> 38.7 us
  matrix products: 17.8 us -> 14.7 us
  local copies, waits for them, and re-layouts: 17.1 us -> 15.3 us
    ppermute x17 -> x11, waiting for transfers between devices: 2.58 us -> 19.5 us  [butterfly_sum(): lax.ppermute(value, axis, [(i, i ^ k * step) for i in range(count)])]
    ppermute x17 -> x11, starting transfers between devices: 26.3 us -> 15.1 us  [butterfly_sum(): lax.ppermute(value, axis, [(i, i ^ k * step) for i in range(count)])]
    all_to_all x1, waiting for transfers between devices: 9.48 us -> 3.06 us  [carried_in(): parts = lax.all_to_all(rows, axis, 0, 0)]
    unnamed x36 -> x34, local copies, waits for them, and re-layouts: 13.8 us -> 12.1 us
  transfers between devices with their start and end apart: 20 -> 14, of which waited for: 3 -> 9; matrix products, arithmetic and copies ran while one was open for 12% -> 11% of each run, Pallas kernels for 0% -> 0%
where the time goes in v8:
time: 143 us; the launch traced here: 142 us
  waiting for transfers between devices  38.7 us (27%)
  blocking collectives  34 us (24%)
  starting transfers between devices  31 us (22%)
  local copies, waits for them, and re-layouts  15.3 us (11%)
  matrix products  14.7 us (10%)
  other arithmetic  6.81 us (5%)
  between operations  1.56 us (1%)
    all_to_all x1, blocking collectives, carried_in(): parts = lax.all_to_all(rows, axis, 0, 0)  34 us
    ppermute x11, waiting for transfers between devices, butterfly_sum(): lax.ppermute(value, axis, [(i, i ^ k * step) for i in range(count)])  19.5 us
    all_to_all x2, waiting for transfers between devices, carried_in(): back = lax.all_to_all(shifted, axis, 0, 0)  16.2 us
    ppermute x11, starting transfers between devices, butterfly_sum(): lax.ppermute(value, axis, [(i, i ^ k * step) for i in range(count)])  15.1 us
    unnamed x34, local copies, waits for them, and re-layouts  12.1 us
    all_to_all x2, starting transfers between devices, carried_in(): back = lax.all_to_all(shifted, axis, 0, 0)  10.7 us
    all_to_all x1, starting transfers between devices, carried_in(): parts = lax.all_to_all(rows, axis, 0, 0)  5.14 us
    all_to_all x1, waiting for transfers between devices, carried_in(): parts = lax.all_to_all(rows, axis, 0, 0)  3.06 us
  transfers between devices with their start and end apart: 14, of which 9 were waited for; matrix products, arithmetic and copies ran while one was open for 11% of the time, Pallas kernels for 0%

profile of v8, /device:TPU:16, one launch (start us, length us, event | category | flops | bytes accessed | tf_op | source)
XLA Modules:
  0.0 142.1 jit_solution(15312713776517699362)
XLA Ops:
  0.6 1.5 %copy.60 = bf16[1,256,1536]{1,2,0:T(8,128)(2,1)S(1)} copy(bf16[1,256,1536]{2,1,0:T(8,128)(2,1)} %param.6) | data formatting | bytes 1572864 | tf_op args[1]
  2.8 34.0 %all_to_all.20 = f32[32,48,128]{2,1,0:T(8,128)S(1)} all-to-all(f32[32,48,128]{2,1,0:T(8,128)S(1)} %bitcast.105), channel_id=1, replica_groups=mesh['dp'=8,'seq'=32] {'seq'}, dimensions={0} | all-to-all | bytes 1572864 | tf_op jit(solution)/shard_map/all_to_all | solution.py:18
  38.9 5.4 %all-to-all-start.1 = ((f32[32,48,128]{2,1,0:T(8,128)}), f32[32,48,128]{2,1,0:T(8,128)}, u32[]{:S(2)}, u32[]{:S(2)}) async-start(f32[32,48,128]{2,1,0:T(8,128)} %copy.64), calls=%async_computation.1 | async-start | bytes 1572864 | tf_op jit(solution)/shard_map/all_to_all | solution.py:31
  44.6 1.7 %copy.65 = bf16[1,256,1536]{1,2,0:T(8,128)(2,1)S(1)} copy(bf16[1,256,1536]{2,1,0:T(8,128)(2,1)} %param.5) | data formatting | bytes 1572864 | tf_op args[0]
  48.1 1.8 %fusion.22 = f32[12,256,128]{1,2,0:T(8,128)} fusion(bf16[12,256,256]{2,1,0:T(8,128)(2,1)S(1)} %select_convert_fusion.1, bf16[256,12,128]{0,2,1:T(8,128)(2,1)S(1)} %bitcast.89), kind=kOutput, calls=%fused_computation.42 | convolution fusion | flops 201326592 | bytes 3932160 | tf_op jit(solution)/shard_map/nhct,nthe->nche/dot_general | solution.py:78
  49.9 16.2 %all-to-all-done.1 = f32[32,48,128]{2,1,0:T(8,128)} async-done(((f32[32,48,128]{2,1,0:T(8,128)}), f32[32,48,128]{2,1,0:T(8,128)}, u32[]{:S(2)}, u32[]{:S(2)}) %all-to-all-start.1) | async-done | bytes 786464 | tf_op jit(solution)/shard_map/all_to_all | solution.py:31
  66.1 1.6 %add_convert_fusion.1 = bf16[12,128,128]{2,1,0:T(8,128)(2,1)S(1)} fusion(f32[12,128,128]{2,1,0:T(8,128)} %bitcast.4, f32[12,128,128]{2,1,0:T(8,128)} %copy-done.4), kind=kLoop, calls=%fused_computation.27 | loop fusion | flops 589824 | bytes 1966080 | tf_op jit(solution)/shard_map/convert_element_type | solution.py:74
  69.5 2.5 %fusion.4 = (bf16[1,256,1536]{1,2,0:T(8,128)(2,1)S(1)}, bf16[1,256,1536]{1,2,0:T(8,128)(2,1)}) fusion(bf16[1,256,1536]{1,2,0:T(8,128)(2,1)} %copy-done.2, f32[12,128,256]{2,1,0:T(8,128)S(1)} %get-tuple-element.25, f32[256]{0:T(256)S(1)} %broadcast_multiply_fusion, f32[1536]{0:T(1024)S(1)} %copy-done.12, f32[256]{0:T(256)S(1)} %add_rsqrt_fusion), kind=kLoop, calls=%fused_computation.8 | loop fusion | flops 3538944 | bytes 3940352 | tf_op jit(solution)/shard_map/convert_element_type | solution.py:91
  73.2 5.1 %all-to-all-start.2 = ((f32[32,48,128]{2,1,0:T(8,128)}), f32[32,48,128]{2,1,0:T(8,128)}, u32[]{:S(2)}, u32[]{:S(2)}) async-start(f32[32,48,128]{2,1,0:T(8,128)} %bitcast.104), calls=%async_computation.2 | async-start | bytes 1572864 | tf_op jit(solution)/shard_map/all_to_all | solution.py:18
  78.4 1.4 collective-permute-start.1
  82.6 4.8 %collective-permute-done.3 = f32[1536]{0:T(1024)S(1)} collective-permute-done((f32[1536]{0:T(1024)S(1)}, f32[1536]{0:T(1024)S(1)}, u32[]{:S(2)}, u32[]{:S(2)}) %collective-permute-start.3) | collective-permute-done | bytes 6176 | tf_op jit(solution)/shard_map/ppermute | solution.py:41
  87.4 2.9 %collective-permute-start.6 = (f32[1536]{0:T(1024)S(1)}, f32[1536]{0:T(1024)S(1)}, u32[]{:S(2)}, u32[]{:S(2)}) collective-permute-start(f32[1536]{0:T(1024)S(1)} %add.92), channel_id=1, source_target_pairs={{0,3},{1,2},{2,1},{3,0},{4,7},{5,6},{6,5},{7,4},{8,11},{9,10},{10,... | collective-permute-start | bytes 18440 | tf_op jit(solution)/shard_map/ppermute | solution.py:41
  92.3 3.4 %collective-permute-done.5 = f32[1536]{0:T(1024)S(1)} collective-permute-done((f32[1536]{0:T(1024)S(1)}, f32[1536]{0:T(1024)S(1)}, u32[]{:S(2)}, u32[]{:S(2)}) %collective-permute-start.5) | collective-permute-done | bytes 6176 | tf_op jit(solution)/shard_map/ppermute | solution.py:41
  96.9 3.1 %all-to-all-done.2 = f32[32,48,128]{2,1,0:T(8,128)} async-done(((f32[32,48,128]{2,1,0:T(8,128)}), f32[32,48,128]{2,1,0:T(8,128)}, u32[]{:S(2)}, u32[]{:S(2)}) %all-to-all-start.2) | async-done | bytes 786464 | tf_op jit(solution)/shard_map/all_to_all | solution.py:18
  100.0 2.1 %fusion.11 = f32[32,48,128]{2,0,1:T(8,128)S(1)} fusion(f32[32,48,128]{2,1,0:T(8,128)} %all-to-all-done.2, f32[]{:T(128)} %bitcast.16), kind=kOutput, calls=%fused_computation.23 | convolution fusion | flops 75500544 | bytes 1572868 | tf_op jit(solution)/shard_map/ij,jkl->ikl/dot_general | solution.py:24
  102.1 1.4 copy.76
  103.4 5.3 %all-to-all-start.3 = ((f32[32,48,128]{2,1,0:T(8,128)}), f32[32,48,128]{2,1,0:T(8,128)}, u32[]{:S(2)}, u32[]{:S(2)}) async-start(f32[32,48,128]{2,1,0:T(8,128)} %copy.76), calls=%async_computation.3 | async-start | bytes 1572864 | tf_op jit(solution)/shard_map/all_to_all | solution.py:31
  108.8 1.6 %select_convert_fusion = bf16[12,256,256]{2,1,0:T(8,128)(2,1)S(1)} fusion(bf16[256,12,128]{0,2,1:T(8,128)(2,1)S(1)} %bitcast.97, bf16[256,12,128]{0,2,1:T(8,128)(2,1)S(1)} %bitcast.90, pred[256,256]{1,0:T(8,128)(4,1)} %copy-done.11), kind=kOutput, calls=%fused_computation | convolution fusion | flops 202899456 | bytes 3211264 | tf_op jit(solution)/shard_map/nche,nthe->nhct/dot_general | solution.py:101
  110.4 1.5 %fusion.25 = f32[12,128,256]{2,1,0:T(8,128)} fusion(bf16[256,12,128]{0,2,1:T(8,128)(2,1)S(1)} %bitcast.98, bf16[12,256,256]{2,1,0:T(8,128)(2,1)S(1)} %copy-done.1), kind=kOutput, calls=%fused_computation.45 | convolution fusion | flops 201326592 | bytes 3932160 | tf_op jit(solution)/shard_map/nhct,nche->nthe/dot_general | solution.py:120
  111.9 1.6 %fusion.26 = f32[12,256,128]{1,2,0:T(8,128)} fusion(bf16[256,12,128]{0,2,1:T(8,128)(2,1)S(1)} %bitcast.103, bf16[12,256,256]{2,1,0:T(8,128)(2,1)S(1)} %select_convert_fusion), kind=kOutput, calls=%fused_computation.46 | convolution fusion | flops 201326592 | bytes 3932160 | tf_op jit(solution)/shard_map/nhct,nchd->nthd/dot_general | solution.py:114
  113.5 3.5 %collective-permute-start.9 = (f32[1536]{0:T(1024)S(1)}, f32[1536]{0:T(1024)S(1)}, u32[]{:S(2)}, u32[]{:S(2)}) collective-permute-start(f32[1536]{0:T(1024)S(1)} %add_add_fusion.1), channel_id=1, source_target_pairs={{0,12},{1,13},{2,14},{3,15},{4,8},{5,9},{6,10},{7,11},{8,4},{9,5},... | collective-permute-start | bytes 18440 | tf_op jit(solution)/shard_map/ppermute | solution.py:41
  118.5 8.4 %collective-permute-done.9 = f32[1536]{0:T(1024)S(1)} collective-permute-done((f32[1536]{0:T(1024)S(1)}, f32[1536]{0:T(1024)S(1)}, u32[]{:S(2)}, u32[]{:S(2)}) %collective-permute-start.9) | collective-permute-done | bytes 6176 | tf_op jit(solution)/shard_map/ppermute | solution.py:41
  127.1 4.3 %collective-permute-start.10 = (f32[1536]{0:T(1024)S(1)}, f32[1536]{0:T(1024)S(1)}, u32[]{:S(2)}, u32[]{:S(2)}) collective-permute-start(f32[1536]{0:T(1024)S(1)} %add_add_fusion), channel_id=1, source_target_pairs={{0,16},{1,17},{2,18},{3,19},{4,20},{5,21},{6,22},{7,23},{8,24},{9,... | collective-permute-start | bytes 18440 | tf_op jit(solution)/shard_map/ppermute | solution.py:41
  132.6 2.4 %copy.80 = bf16[1,256,1536]{2,1,0:T(8,128)(2,1)} copy(bf16[1,256,1536]{1,2,0:T(8,128)(2,1)} %get-tuple-element.23) | data formatting | bytes 1572864
  (68 shorter events, 23.2 us)
Async XLA Ops:
  0.6 1.5 %copy-start.9 = (bf16[1,256,1536]{2,1,0:T(8,128)(2,1)S(1)}, bf16[1,256,1536]{2,1,0:T(8,128)(2,1)}, u32[]{:S(2)}) copy-start(bf16[1,256,1536]{2,1,0:T(8,128)(2,1)} %param.7) | copy-start | bytes 2359300
  2.8 34.8 %copy-start.4 = (f32[12,128,128]{2,1,0:T(8,128)}, f32[12,128,128]{2,1,0:T(8,128)S(1)}, u32[]{:S(2)}) copy-start(f32[12,128,128]{2,1,0:T(8,128)S(1)} %fusion.21) | copy-start | bytes 2359300
  38.9 5.4 %copy-start.10 = (bf16[1,256,1536]{2,1,0:T(8,128)(2,1)S(1)}, bf16[1,256,1536]{2,1,0:T(8,128)(2,1)}, u32[]{:S(2)}) copy-start(bf16[1,256,1536]{2,1,0:T(8,128)(2,1)} %param.9) | copy-start | bytes 2359300
  38.9 27.2 %all-to-all-start.1 = ((f32[32,48,128]{2,1,0:T(8,128)}), f32[32,48,128]{2,1,0:T(8,128)}, u32[]{:S(2)}, u32[]{:S(2)}) async-start(f32[32,48,128]{2,1,0:T(8,128)} %copy.64), calls=%async_computation.1 | async-start | bytes 1572864 | tf_op jit(solution)/shard_map/all_to_all | solution.py:31
  44.6 23.9 %copy-start.2 = (bf16[1,256,1536]{1,2,0:T(8,128)(2,1)}, bf16[1,256,1536]{1,2,0:T(8,128)(2,1)S(1)}, u32[]{:S(2)}) copy-start(bf16[1,256,1536]{1,2,0:T(8,128)(2,1)S(1)} %copy.70) | copy-start | bytes 2359300
  66.1 1.9 %copy-start.7 = (f32[12,256,128]{1,2,0:T(8,128)S(1)}, f32[12,256,128]{1,2,0:T(8,128)}, u32[]{:S(2)}) copy-start(f32[12,256,128]{1,2,0:T(8,128)} %fusion.22) | copy-start | bytes 4718596
  73.2 26.8 %all-to-all-start.2 = ((f32[32,48,128]{2,1,0:T(8,128)}), f32[32,48,128]{2,1,0:T(8,128)}, u32[]{:S(2)}, u32[]{:S(2)}) async-start(f32[32,48,128]{2,1,0:T(8,128)} %bitcast.104), calls=%async_computation.2 | async-start | bytes 1572864 | tf_op jit(solution)/shard_map/all_to_all | solution.py:18
  78.3 3.2 %collective-permute-start.2 = (f32[1536]{0:T(1024)S(1)}, f32[1536]{0:T(1024)S(1)}, u32[]{:S(2)}, u32[]{:S(2)}) collective-permute-start(f32[1536]{0:T(1024)S(1)} %get-tuple-element.20), channel_id=1, source_target_pairs={{0,96},{32,64},{64,32},{96,0},{128,224},{160,192},{192,160},{224,1... | collective-permute-start | bytes 18440 | tf_op jit(solution)/shard_map/ppermute | solution.py:41
  78.4 3.7 %collective-permute-start.1 = (f32[1536]{0:T(1024)S(1)}, f32[1536]{0:T(1024)S(1)}, u32[]{:S(2)}, u32[]{:S(2)}) collective-permute-start(f32[1536]{0:T(1024)S(1)} %get-tuple-element.20), channel_id=1, source_target_pairs={{0,64},{32,96},{64,0},{96,32},{128,192},{160,224},{192,128},{224,1... | collective-permute-start | bytes 18440 | tf_op jit(solution)/shard_map/ppermute | solution.py:41
  79.8 2.4 %collective-permute-start = (f32[1536]{0:T(1024)S(1)}, f32[1536]{0:T(1024)S(1)}, u32[]{:S(2)}, u32[]{:S(2)}) collective-permute-start(f32[1536]{0:T(1024)S(1)} %get-tuple-element.20), channel_id=1, source_target_pairs={{0,32},{32,0},{64,96},{96,64},{128,160},{160,128},{192,224},{224,1... | collective-permute-start | bytes 18440 | tf_op jit(solution)/shard_map/ppermute | solution.py:41
  82.2 5.2 %collective-permute-start.3 = (f32[1536]{0:T(1024)S(1)}, f32[1536]{0:T(1024)S(1)}, u32[]{:S(2)}, u32[]{:S(2)}) collective-permute-start(f32[1536]{0:T(1024)S(1)} %add_add_fusion.2), channel_id=1, source_target_pairs={{0,128},{32,160},{64,192},{96,224},{128,0},{160,32},{192,64},{224,... | collective-permute-start | bytes 18440 | tf_op jit(solution)/shard_map/ppermute | solution.py:41
  87.4 4.9 %collective-permute-start.6 = (f32[1536]{0:T(1024)S(1)}, f32[1536]{0:T(1024)S(1)}, u32[]{:S(2)}, u32[]{:S(2)}) collective-permute-start(f32[1536]{0:T(1024)S(1)} %add.92), channel_id=1, source_target_pairs={{0,3},{1,2},{2,1},{3,0},{4,7},{5,6},{6,5},{7,4},{8,11},{9,10},{10,... | collective-permute-start | bytes 18440 | tf_op jit(solution)/shard_map/ppermute | solution.py:41
  90.4 5.4 %collective-permute-start.5 = (f32[1536]{0:T(1024)S(1)}, f32[1536]{0:T(1024)S(1)}, u32[]{:S(2)}, u32[]{:S(2)}) collective-permute-start(f32[1536]{0:T(1024)S(1)} %add.92), channel_id=1, source_target_pairs={{0,2},{1,3},{2,0},{3,1},{4,6},{5,7},{6,4},{7,5},{8,10},{9,11},{10,... | collective-permute-start | bytes 18440 | tf_op jit(solution)/shard_map/ppermute | solution.py:41
  91.2 4.5 %collective-permute-start.4 = (f32[1536]{0:T(1024)S(1)}, f32[1536]{0:T(1024)S(1)}, u32[]{:S(2)}, u32[]{:S(2)}) collective-permute-start(f32[1536]{0:T(1024)S(1)} %add.92), channel_id=1, source_target_pairs={{0,1},{1,0},{2,3},{3,2},{4,5},{5,4},{6,7},{7,6},{8,9},{9,8},{10,11... | collective-permute-start | bytes 18440 | tf_op jit(solution)/shard_map/ppermute | solution.py:41
  103.4 33.4 %all-to-all-start.3 = ((f32[32,48,128]{2,1,0:T(8,128)}), f32[32,48,128]{2,1,0:T(8,128)}, u32[]{:S(2)}, u32[]{:S(2)}) async-start(f32[32,48,128]{2,1,0:T(8,128)} %copy.76), calls=%async_computation.3 | async-start | bytes 1572864 | tf_op jit(solution)/shard_map/all_to_all | solution.py:31
  108.8 1.6 %copy-start.1 = (bf16[12,256,256]{2,1,0:T(8,128)(2,1)S(1)}, bf16[12,256,256]{2,1,0:T(8,128)(2,1)}, u32[]{:S(2)}) copy-start(bf16[12,256,256]{2,1,0:T(8,128)(2,1)} %copy-done) | copy-start | bytes 4718596
  113.5 13.4 %collective-permute-start.9 = (f32[1536]{0:T(1024)S(1)}, f32[1536]{0:T(1024)S(1)}, u32[]{:S(2)}, u32[]{:S(2)}) collective-permute-start(f32[1536]{0:T(1024)S(1)} %add_add_fusion.1), channel_id=1, source_target_pairs={{0,12},{1,13},{2,14},{3,15},{4,8},{5,9},{6,10},{7,11},{8,4},{9,5},... | collective-permute-start | bytes 18440 | tf_op jit(solution)/shard_map/ppermute | solution.py:41
  117.0 10.1 %collective-permute-start.8 = (f32[1536]{0:T(1024)S(1)}, f32[1536]{0:T(1024)S(1)}, u32[]{:S(2)}, u32[]{:S(2)}) collective-permute-start(f32[1536]{0:T(1024)S(1)} %add_add_fusion.1), channel_id=1, source_target_pairs={{0,8},{1,9},{2,10},{3,11},{4,12},{5,13},{6,14},{7,15},{8,0},{9,1},... | collective-permute-start | bytes 18440 | tf_op jit(solution)/shard_map/ppermute | solution.py:41
  117.0 10.1 %collective-permute-start.7 = (f32[1536]{0:T(1024)S(1)}, f32[1536]{0:T(1024)S(1)}, u32[]{:S(2)}, u32[]{:S(2)}) collective-permute-start(f32[1536]{0:T(1024)S(1)} %add_add_fusion.1), channel_id=1, source_target_pairs={{0,4},{1,5},{2,6},{3,7},{4,0},{5,1},{6,2},{7,3},{8,12},{9,13},{10,... | collective-permute-start | bytes 18440 | tf_op jit(solution)/shard_map/ppermute | solution.py:41
  127.1 9.1 %collective-permute-start.10 = (f32[1536]{0:T(1024)S(1)}, f32[1536]{0:T(1024)S(1)}, u32[]{:S(2)}, u32[]{:S(2)}) collective-permute-start(f32[1536]{0:T(1024)S(1)} %add_add_fusion), channel_id=1, source_target_pairs={{0,16},{1,17},{2,18},{3,19},{4,20},{5,21},{6,22},{7,23},{8,24},{9,... | collective-permute-start | bytes 18440 | tf_op jit(solution)/shard_map/ppermute | solution.py:41
  132.6 2.4 %copy-start.8 = (bf16[12,128,256]{2,1,0:T(8,128)(2,1)S(1)}, bf16[12,128,256]{2,1,0:T(8,128)(2,1)}, u32[]{:S(2)}) copy-start(bf16[12,128,256]{2,1,0:T(8,128)(2,1)} %fusion.7) | copy-start | bytes 2359300
  132.6 4.2 %copy-start.3 = (f32[12,128,128]{1,2,0:T(8,128)S(1)}, f32[12,128,128]{1,2,0:T(8,128)}, u32[]{:S(2)}) copy-start(f32[12,128,128]{1,2,0:T(8,128)} %fusion.24) | copy-start | bytes 2359300
  136.8 1.6 %copy-start.6 = (f32[12,128,256]{2,1,0:T(8,128)S(1)}, f32[12,128,256]{2,1,0:T(8,128)}, u32[]{:S(2)}) copy-start(f32[12,128,256]{2,1,0:T(8,128)} %fusion.25) | copy-start | bytes 4718596
  138.9 1.7 %copy-start.5 = (f32[12,256,128]{1,2,0:T(8,128)S(1)}, f32[12,256,128]{1,2,0:T(8,128)}, u32[]{:S(2)}) copy-start(f32[12,256,128]{1,2,0:T(8,128)} %fusion.26) | copy-start | bytes 4718596
  (3 other events, 2.5 us)

commit v9 on v8

--- a/solution.py
+++ b/solution.py
@@ -32,10 +32,10 @@
     return back.reshape(value.shape)
 
 
-def butterfly_sum(value, axis, step=1, stop=None):
+def butterfly_sum(value, axis):
     count = lax.axis_size(axis)
-    stop = count if stop is None else stop
-    while step < stop:
+    step = 1
+    while step < count:
         radix = 4 if step * 4 <= count else 2
         got = [
             lax.ppermute(value, axis, [(i, i ^ (k * step)) for i in range(count)])
@@ -92,9 +92,9 @@
     query_parts = jnp.einsum(
         "nchd,nche->nhde", queries, grad_blocks, preferred_element_type=jnp.float32
     )
-    gain_near = butterfly_sum(butterfly_sum(gain_terms, "dp"), "seq", 1, 4)
-    suffix = carried_in(jnp.sum(query_parts, axis=0), "seq", True, gain_near[0])
-    grad_gain = butterfly_sum(gain_near, "seq", 4)
+    gain_dp = butterfly_sum(gain_terms, "dp")
+    suffix = carried_in(jnp.sum(query_parts, axis=0), "seq", True, gain_dp[0])
+    grad_gain = butterfly_sum(gain_dp, "seq")
     from_end = lax.cumsum(query_parts, axis=0, reverse=True)
     behind = jnp.concatenate([from_end[1:], query_parts[-1:] * 0.0], axis=0)
     suffix_states = (suffix[None] + behind).astype(jnp.bfloat16)
@@ -108,18 +108,20 @@
     grad_query = grad_query + jnp.einsum(
         "nhct,nthd->nchd", grad_weights, key_blocks, preferred_element_type=jnp.float32
     )
+    key_local = jnp.einsum(
+        "nhct,nchd->nthd", grad_weights, queries, preferred_element_type=jnp.float32
+    )
+    value_local = jnp.einsum(
+        "nhct,nche->nthe", weights, grad_blocks, preferred_element_type=jnp.float32
+    )
     grad_key = jnp.einsum(
         "nche,nhde->nchd", value_blocks, suffix_states, preferred_element_type=jnp.float32
     )
-    grad_key = grad_key + jnp.einsum(
-        "nhct,nchd->nthd", grad_weights, queries, preferred_element_type=jnp.float32
-    )
+    grad_key = grad_key + key_local
     grad_value = jnp.einsum(
         "nchd,nhde->nche", key_blocks, suffix_states, preferred_element_type=jnp.float32
     )
-    grad_value = grad_value + jnp.einsum(
-        "nhct,nche->nthe", weights, grad_blocks, preferred_element_type=jnp.float32
-    )
+    grad_value = grad_value + value_local
     out_shape = (1, tokens, features)
     return (
         attended,

time: 143 us -> 142 us (level)
  waiting for transfers between devices: 38.7 us -> 36.8 us
    ppermute x11, waiting for transfers between devices: 19.5 us -> 9.23 us  [butterfly_sum(): lax.ppermute(value, axis, [(i, i ^ k * step) for i in range(count)])]
    all_to_all x1, waiting for transfers between devices: 3.06 us -> 11.4 us  [carried_in(): parts = lax.all_to_all(rows, axis, 0, 0)]
    unnamed x34 -> x32, local copies, waits for them, and re-layouts: 12.1 us -> 12.1 us
  transfers between devices with their start and end apart: 14 -> 14, of which waited for: 9 -> 8; matrix products, arithmetic and copies ran while one was open for 11% -> 12% of each run, Pallas kernels for 0% -> 0%
where the time goes in v9:
time: 142 us; the launch traced here: 141 us
  waiting for transfers between devices  36.8 us (26%)
  blocking collectives  34 us (24%)
  starting transfers between devices  31.1 us (22%)
  matrix products  15.9 us (11%)
  local copies, waits for them, and re-layouts  15.3 us (11%)
  other arithmetic  6.82 us (5%)
  between operations  1.55 us (1%)
    all_to_all x1, blocking collectives, carried_in(): parts = lax.all_to_all(rows, axis, 0, 0)  34 us
    all_to_all x2, waiting for transfers between devices, carried_in(): back = lax.all_to_all(shifted, axis, 0, 0)  16.2 us
    ppermute x11, starting transfers between devices, butterfly_sum(): lax.ppermute(value, axis, [(i, i ^ k * step) for i in range(count)])  15.5 us
    unnamed x32, local copies, waits for them, and re-layouts  12.1 us
    all_to_all x1, waiting for transfers between devices, carried_in(): parts = lax.all_to_all(rows, axis, 0, 0)  11.4 us
    all_to_all x2, starting transfers between devices, carried_in(): back = lax.all_to_all(shifted, axis, 0, 0)  10.5 us
    ppermute x11, waiting for transfers between devices, butterfly_sum(): lax.ppermute(value, axis, [(i, i ^ k * step) for i in range(count)])  9.23 us
    all_to_all x1, starting transfers between devices, carried_in(): parts = lax.all_to_all(rows, axis, 0, 0)  5.14 us
  transfers between devices with their start and end apart: 14, of which 8 were waited for; matrix products, arithmetic and copies ran while one was open for 12% of the time, Pallas kernels for 0%

profile of v9, /device:TPU:16, one launch (start us, length us, event | category | flops | bytes accessed | tf_op | source)
XLA Modules:
  0.0 141.5 jit_solution(10535958473844103807)
XLA Ops:
  0.6 1.5 %copy.60 = bf16[1,256,1536]{1,2,0:T(8,128)(2,1)S(1)} copy(bf16[1,256,1536]{2,1,0:T(8,128)(2,1)} %param.6) | data formatting | bytes 1572864 | tf_op args[1]
  2.8 34.0 %all_to_all.20 = f32[32,48,128]{2,1,0:T(8,128)S(1)} all-to-all(f32[32,48,128]{2,1,0:T(8,128)S(1)} %bitcast.105), channel_id=1, replica_groups=mesh['dp'=8,'seq'=32] {'seq'}, dimensions={0} | all-to-all | bytes 1572864 | tf_op jit(solution)/shard_map/all_to_all | solution.py:18
  38.9 5.4 %all-to-all-start.1 = ((f32[32,48,128]{2,1,0:T(8,128)}), f32[32,48,128]{2,1,0:T(8,128)}, u32[]{:S(2)}, u32[]{:S(2)}) async-start(f32[32,48,128]{2,1,0:T(8,128)} %copy.64), calls=%async_computation.1 | async-start | bytes 1572864 | tf_op jit(solution)/shard_map/all_to_all | solution.py:31
  44.6 1.7 %copy.65 = bf16[1,256,1536]{1,2,0:T(8,128)(2,1)S(1)} copy(bf16[1,256,1536]{2,1,0:T(8,128)(2,1)} %param.5) | data formatting | bytes 1572864 | tf_op args[0]
  48.1 1.8 %fusion.22 = f32[12,256,128]{1,2,0:T(8,128)} fusion(bf16[12,256,256]{2,1,0:T(8,128)(2,1)S(1)} %select_convert_fusion.1, bf16[256,12,128]{0,2,1:T(8,128)(2,1)S(1)} %bitcast.89), kind=kOutput, calls=%fused_computation.42 | convolution fusion | flops 201326592 | bytes 3932160 | tf_op jit(solution)/shard_map/nhct,nthe->nche/dot_general | solution.py:78
  49.9 16.2 %all-to-all-done.1 = f32[32,48,128]{2,1,0:T(8,128)} async-done(((f32[32,48,128]{2,1,0:T(8,128)}), f32[32,48,128]{2,1,0:T(8,128)}, u32[]{:S(2)}, u32[]{:S(2)}) %all-to-all-start.1) | async-done | bytes 786464 | tf_op jit(solution)/shard_map/all_to_all | solution.py:31
  66.1 1.6 %add_convert_fusion.1 = bf16[12,128,128]{2,1,0:T(8,128)(2,1)S(1)} fusion(f32[12,128,128]{2,1,0:T(8,128)} %bitcast.4, f32[12,128,128]{2,1,0:T(8,128)} %copy-done.3), kind=kLoop, calls=%fused_computation.27 | loop fusion | flops 589824 | bytes 1966080 | tf_op jit(solution)/shard_map/convert_element_type | solution.py:74
  69.5 2.5 %fusion.4 = (bf16[1,256,1536]{1,2,0:T(8,128)(2,1)S(1)}, bf16[1,256,1536]{1,2,0:T(8,128)(2,1)}) fusion(bf16[1,256,1536]{1,2,0:T(8,128)(2,1)} %copy-done.1, f32[12,128,256]{2,1,0:T(8,128)S(1)} %get-tuple-element.25, f32[256]{0:T(256)S(1)} %broadcast_multiply_fusion, f32[1536]{0:T(1024)S(1)} %copy-done.11, f32[256]{0:T(256)S(1)} %add_rsqrt_fusion), kind=kLoop, calls=%fused_computation.8 | loop fusion | flops 3538944 | bytes 3940352 | tf_op jit(solution)/shard_map/convert_element_type | solution.py:91
  73.2 5.1 %all-to-all-start.2 = ((f32[32,48,128]{2,1,0:T(8,128)}), f32[32,48,128]{2,1,0:T(8,128)}, u32[]{:S(2)}, u32[]{:S(2)}) async-start(f32[32,48,128]{2,1,0:T(8,128)} %bitcast.104), calls=%async_computation.2 | async-start | bytes 1572864 | tf_op jit(solution)/shard_map/all_to_all | solution.py:18
  78.4 1.4 collective-permute-start.1
  82.6 2.9 %fusion.25 = f32[12,128,256]{2,1,0:T(8,128)} fusion(bf16[256,12,128]{0,2,1:T(8,128)(2,1)S(1)} %bitcast.97, bf16[12,256,256]{2,1,0:T(8,128)(2,1)} %copy-done), kind=kOutput, calls=%fused_computation.45 | convolution fusion | flops 201326592 | bytes 3932160 | tf_op jit(solution)/shard_map/nhct,nche->nthe/dot_general | solution.py:114
  85.6 1.9 %collective-permute-done.3 = f32[1536]{0:T(1024)S(1)} collective-permute-done((f32[1536]{0:T(1024)S(1)}, f32[1536]{0:T(1024)S(1)}, u32[]{:S(2)}, u32[]{:S(2)}) %collective-permute-start.3) | collective-permute-done | bytes 6176 | tf_op jit(solution)/shard_map/ppermute | solution.py:41
  88.6 11.4 %all-to-all-done.2 = f32[32,48,128]{2,1,0:T(8,128)} async-done(((f32[32,48,128]{2,1,0:T(8,128)}), f32[32,48,128]{2,1,0:T(8,128)}, u32[]{:S(2)}, u32[]{:S(2)}) %all-to-all-start.2) | async-done | bytes 786464 | tf_op jit(solution)/shard_map/all_to_all | solution.py:18
  100.0 2.1 %fusion.11 = f32[32,48,128]{2,0,1:T(8,128)S(1)} fusion(f32[32,48,128]{2,1,0:T(8,128)} %all-to-all-done.2, f32[]{:T(128)} %bitcast.16), kind=kOutput, calls=%fused_computation.23 | convolution fusion | flops 75500544 | bytes 1572868 | tf_op jit(solution)/shard_map/ij,jkl->ikl/dot_general | solution.py:24
  102.1 1.4 copy.76
  103.4 5.1 %all-to-all-start.3 = ((f32[32,48,128]{2,1,0:T(8,128)}), f32[32,48,128]{2,1,0:T(8,128)}, u32[]{:S(2)}, u32[]{:S(2)}) async-start(f32[32,48,128]{2,1,0:T(8,128)} %copy.76), calls=%async_computation.3 | async-start | bytes 1572864 | tf_op jit(solution)/shard_map/all_to_all | solution.py:31
  108.5 1.5 %select_convert_fusion = bf16[12,256,256]{2,1,0:T(8,128)(2,1)S(1)} fusion(bf16[256,12,128]{0,2,1:T(8,128)(2,1)S(1)} %bitcast.98, bf16[256,12,128]{0,2,1:T(8,128)(2,1)S(1)} %bitcast.90, pred[256,256]{1,0:T(8,128)(4,1)} %copy-done.10), kind=kOutput, calls=%fused_computation | convolution fusion | flops 202899456 | bytes 3211264 | tf_op jit(solution)/shard_map/nche,nthe->nhct/dot_general | solution.py:101
  110.0 2.9 %collective-permute-start.6 = (f32[1536]{0:T(1024)S(1)}, f32[1536]{0:T(1024)S(1)}, u32[]{:S(2)}, u32[]{:S(2)}) collective-permute-start(f32[1536]{0:T(1024)S(1)} %add.92), channel_id=1, source_target_pairs={{0,3},{1,2},{2,1},{3,0},{4,7},{5,6},{6,5},{7,4},{8,11},{9,10},{10,... | collective-permute-start | bytes 18440 | tf_op jit(solution)/shard_map/ppermute | solution.py:41
  114.2 1.5 %fusion.26 = f32[12,256,128]{1,2,0:T(8,128)} fusion(bf16[256,12,128]{0,2,1:T(8,128)(2,1)S(1)} %bitcast.103, bf16[12,256,256]{2,1,0:T(8,128)(2,1)S(1)} %select_convert_fusion), kind=kOutput, calls=%fused_computation.46 | convolution fusion | flops 201326592 | bytes 3932160 | tf_op jit(solution)/shard_map/nhct,nchd->nthd/dot_general | solution.py:111
  115.7 2.4 %collective-permute-done.5 = f32[1536]{0:T(1024)S(1)} collective-permute-done((f32[1536]{0:T(1024)S(1)}, f32[1536]{0:T(1024)S(1)}, u32[]{:S(2)}, u32[]{:S(2)}) %collective-permute-start.5) | collective-permute-done | bytes 6176 | tf_op jit(solution)/shard_map/ppermute | solution.py:41
  118.1 3.6 %collective-permute-start.9 = (f32[1536]{0:T(1024)S(1)}, f32[1536]{0:T(1024)S(1)}, u32[]{:S(2)}, u32[]{:S(2)}) collective-permute-start(f32[1536]{0:T(1024)S(1)} %add_add_fusion.1), channel_id=1, source_target_pairs={{0,12},{1,13},{2,14},{3,15},{4,8},{5,9},{6,10},{7,11},{8,4},{9,5},... | collective-permute-start | bytes 18440 | tf_op jit(solution)/shard_map/ppermute | solution.py:41
  123.2 2.9 %collective-permute-done.9 = f32[1536]{0:T(1024)S(1)} collective-permute-done((f32[1536]{0:T(1024)S(1)}, f32[1536]{0:T(1024)S(1)}, u32[]{:S(2)}, u32[]{:S(2)}) %collective-permute-start.9) | collective-permute-done | bytes 6176 | tf_op jit(solution)/shard_map/ppermute | solution.py:41
  126.3 4.5 %collective-permute-start.10 = (f32[1536]{0:T(1024)S(1)}, f32[1536]{0:T(1024)S(1)}, u32[]{:S(2)}, u32[]{:S(2)}) collective-permute-start(f32[1536]{0:T(1024)S(1)} %add_add_fusion), channel_id=1, source_target_pairs={{0,16},{1,17},{2,18},{3,19},{4,20},{5,21},{6,22},{7,23},{8,24},{9,... | collective-permute-start | bytes 18440 | tf_op jit(solution)/shard_map/ppermute | solution.py:41
  132.0 2.4 %copy.80 = bf16[1,256,1536]{2,1,0:T(8,128)(2,1)} copy(bf16[1,256,1536]{1,2,0:T(8,128)(2,1)} %get-tuple-element.23) | data formatting | bytes 1572864
  (66 shorter events, 22.5 us)
Async XLA Ops:
  0.6 1.5 %copy-start.8 = (bf16[1,256,1536]{2,1,0:T(8,128)(2,1)S(1)}, bf16[1,256,1536]{2,1,0:T(8,128)(2,1)}, u32[]{:S(2)}) copy-start(bf16[1,256,1536]{2,1,0:T(8,128)(2,1)} %param.7) | copy-start | bytes 2359300
  2.8 34.8 %copy-start.3 = (f32[12,128,128]{2,1,0:T(8,128)}, f32[12,128,128]{2,1,0:T(8,128)S(1)}, u32[]{:S(2)}) copy-start(f32[12,128,128]{2,1,0:T(8,128)S(1)} %fusion.21) | copy-start | bytes 2359300
  38.9 5.4 %copy-start.9 = (bf16[1,256,1536]{2,1,0:T(8,128)(2,1)S(1)}, bf16[1,256,1536]{2,1,0:T(8,128)(2,1)}, u32[]{:S(2)}) copy-start(bf16[1,256,1536]{2,1,0:T(8,128)(2,1)} %param.9) | copy-start | bytes 2359300
  38.9 27.2 %all-to-all-start.1 = ((f32[32,48,128]{2,1,0:T(8,128)}), f32[32,48,128]{2,1,0:T(8,128)}, u32[]{:S(2)}, u32[]{:S(2)}) async-start(f32[32,48,128]{2,1,0:T(8,128)} %copy.64), calls=%async_computation.1 | async-start | bytes 1572864 | tf_op jit(solution)/shard_map/all_to_all | solution.py:31
  44.6 23.9 %copy-start.1 = (bf16[1,256,1536]{1,2,0:T(8,128)(2,1)}, bf16[1,256,1536]{1,2,0:T(8,128)(2,1)S(1)}, u32[]{:S(2)}) copy-start(bf16[1,256,1536]{1,2,0:T(8,128)(2,1)S(1)} %copy.70) | copy-start | bytes 2359300
  47.0 1.1 copy-start
  66.1 1.9 %copy-start.6 = (f32[12,256,128]{1,2,0:T(8,128)S(1)}, f32[12,256,128]{1,2,0:T(8,128)}, u32[]{:S(2)}) copy-start(f32[12,256,128]{1,2,0:T(8,128)} %fusion.22) | copy-start | bytes 4718596
  73.2 26.8 %all-to-all-start.2 = ((f32[32,48,128]{2,1,0:T(8,128)}), f32[32,48,128]{2,1,0:T(8,128)}, u32[]{:S(2)}, u32[]{:S(2)}) async-start(f32[32,48,128]{2,1,0:T(8,128)} %bitcast.104), calls=%async_computation.2 | async-start | bytes 1572864 | tf_op jit(solution)/shard_map/all_to_all | solution.py:18
  78.3 3.2 %collective-permute-start.2 = (f32[1536]{0:T(1024)S(1)}, f32[1536]{0:T(1024)S(1)}, u32[]{:S(2)}, u32[]{:S(2)}) collective-permute-start(f32[1536]{0:T(1024)S(1)} %get-tuple-element.20), channel_id=1, source_target_pairs={{0,96},{32,64},{64,32},{96,0},{128,224},{160,192},{192,160},{224,1... | collective-permute-start | bytes 18440 | tf_op jit(solution)/shard_map/ppermute | solution.py:41
  78.4 3.7 %collective-permute-start.1 = (f32[1536]{0:T(1024)S(1)}, f32[1536]{0:T(1024)S(1)}, u32[]{:S(2)}, u32[]{:S(2)}) collective-permute-start(f32[1536]{0:T(1024)S(1)} %get-tuple-element.20), channel_id=1, source_target_pairs={{0,64},{32,96},{64,0},{96,32},{128,192},{160,224},{192,128},{224,1... | collective-permute-start | bytes 18440 | tf_op jit(solution)/shard_map/ppermute | solution.py:41
  79.8 2.4 %collective-permute-start = (f32[1536]{0:T(1024)S(1)}, f32[1536]{0:T(1024)S(1)}, u32[]{:S(2)}, u32[]{:S(2)}) collective-permute-start(f32[1536]{0:T(1024)S(1)} %get-tuple-element.20), channel_id=1, source_target_pairs={{0,32},{32,0},{64,96},{96,64},{128,160},{160,128},{192,224},{224,1... | collective-permute-start | bytes 18440 | tf_op jit(solution)/shard_map/ppermute | solution.py:41
  82.2 5.2 %collective-permute-start.3 = (f32[1536]{0:T(1024)S(1)}, f32[1536]{0:T(1024)S(1)}, u32[]{:S(2)}, u32[]{:S(2)}) collective-permute-start(f32[1536]{0:T(1024)S(1)} %add_add_fusion.2), channel_id=1, source_target_pairs={{0,128},{32,160},{64,192},{96,224},{128,0},{160,32},{192,64},{224,... | collective-permute-start | bytes 18440 | tf_op jit(solution)/shard_map/ppermute | solution.py:41
  103.4 32.8 %all-to-all-start.3 = ((f32[32,48,128]{2,1,0:T(8,128)}), f32[32,48,128]{2,1,0:T(8,128)}, u32[]{:S(2)}, u32[]{:S(2)}) async-start(f32[32,48,128]{2,1,0:T(8,128)} %copy.76), calls=%async_computation.3 | async-start | bytes 1572864 | tf_op jit(solution)/shard_map/all_to_all | solution.py:31
  110.0 5.7 %collective-permute-start.6 = (f32[1536]{0:T(1024)S(1)}, f32[1536]{0:T(1024)S(1)}, u32[]{:S(2)}, u32[]{:S(2)}) collective-permute-start(f32[1536]{0:T(1024)S(1)} %add.92), channel_id=1, source_target_pairs={{0,3},{1,2},{2,1},{3,0},{4,7},{5,6},{6,5},{7,4},{8,11},{9,10},{10,... | collective-permute-start | bytes 18440 | tf_op jit(solution)/shard_map/ppermute | solution.py:41
  112.9 5.2 %collective-permute-start.5 = (f32[1536]{0:T(1024)S(1)}, f32[1536]{0:T(1024)S(1)}, u32[]{:S(2)}, u32[]{:S(2)}) collective-permute-start(f32[1536]{0:T(1024)S(1)} %add.92), channel_id=1, source_target_pairs={{0,2},{1,3},{2,0},{3,1},{4,6},{5,7},{6,4},{7,5},{8,10},{9,11},{10,... | collective-permute-start | bytes 18440 | tf_op jit(solution)/shard_map/ppermute | solution.py:41
  113.7 4.4 %collective-permute-start.4 = (f32[1536]{0:T(1024)S(1)}, f32[1536]{0:T(1024)S(1)}, u32[]{:S(2)}, u32[]{:S(2)}) collective-permute-start(f32[1536]{0:T(1024)S(1)} %add.92), channel_id=1, source_target_pairs={{0,1},{1,0},{2,3},{3,2},{4,5},{5,4},{6,7},{7,6},{8,9},{9,8},{10,11... | collective-permute-start | bytes 18440 | tf_op jit(solution)/shard_map/ppermute | solution.py:41
  118.1 8.0 %collective-permute-start.9 = (f32[1536]{0:T(1024)S(1)}, f32[1536]{0:T(1024)S(1)}, u32[]{:S(2)}, u32[]{:S(2)}) collective-permute-start(f32[1536]{0:T(1024)S(1)} %add_add_fusion.1), channel_id=1, source_target_pairs={{0,12},{1,13},{2,14},{3,15},{4,8},{5,9},{6,10},{7,11},{8,4},{9,5},... | collective-permute-start | bytes 18440 | tf_op jit(solution)/shard_map/ppermute | solution.py:41
  121.7 4.6 %collective-permute-start.8 = (f32[1536]{0:T(1024)S(1)}, f32[1536]{0:T(1024)S(1)}, u32[]{:S(2)}, u32[]{:S(2)}) collective-permute-start(f32[1536]{0:T(1024)S(1)} %add_add_fusion.1), channel_id=1, source_target_pairs={{0,8},{1,9},{2,10},{3,11},{4,12},{5,13},{6,14},{7,15},{8,0},{9,1},... | collective-permute-start | bytes 18440 | tf_op jit(solution)/shard_map/ppermute | solution.py:41
  121.7 4.6 %collective-permute-start.7 = (f32[1536]{0:T(1024)S(1)}, f32[1536]{0:T(1024)S(1)}, u32[]{:S(2)}, u32[]{:S(2)}) collective-permute-start(f32[1536]{0:T(1024)S(1)} %add_add_fusion.1), channel_id=1, source_target_pairs={{0,4},{1,5},{2,6},{3,7},{4,0},{5,1},{6,2},{7,3},{8,12},{9,13},{10,... | collective-permute-start | bytes 18440 | tf_op jit(solution)/shard_map/ppermute | solution.py:41
  126.3 9.3 %collective-permute-start.10 = (f32[1536]{0:T(1024)S(1)}, f32[1536]{0:T(1024)S(1)}, u32[]{:S(2)}, u32[]{:S(2)}) collective-permute-start(f32[1536]{0:T(1024)S(1)} %add_add_fusion), channel_id=1, source_target_pairs={{0,16},{1,17},{2,18},{3,19},{4,20},{5,21},{6,22},{7,23},{8,24},{9,... | collective-permute-start | bytes 18440 | tf_op jit(solution)/shard_map/ppermute | solution.py:41
  132.0 2.4 %copy-start.7 = (bf16[12,128,256]{2,1,0:T(8,128)(2,1)S(1)}, bf16[12,128,256]{2,1,0:T(8,128)(2,1)}, u32[]{:S(2)}) copy-start(bf16[12,128,256]{2,1,0:T(8,128)(2,1)} %fusion.7) | copy-start | bytes 2359300
  132.0 4.2 %copy-start.2 = (f32[12,128,128]{1,2,0:T(8,128)S(1)}, f32[12,128,128]{1,2,0:T(8,128)}, u32[]{:S(2)}) copy-start(f32[12,128,128]{1,2,0:T(8,128)} %fusion.24) | copy-start | bytes 2359300
  136.2 1.6 %copy-start.4 = (f32[12,128,256]{2,1,0:T(8,128)S(1)}, f32[12,128,256]{2,1,0:T(8,128)}, u32[]{:S(2)}) copy-start(f32[12,128,256]{2,1,0:T(8,128)} %fusion.25) | copy-start | bytes 4718596
  138.3 1.7 %copy-start.5 = (f32[12,256,128]{1,2,0:T(8,128)S(1)}, f32[12,256,128]{1,2,0:T(8,128)}, u32[]{:S(2)}) copy-start(f32[12,256,128]{1,2,0:T(8,128)} %fusion.26) | copy-start | bytes 4718596
  (2 other events, 1.4 us)

commit v10 on v8

--- a/solution.py
+++ b/solution.py
@@ -32,11 +32,14 @@
     return back.reshape(value.shape)
 
 
-def butterfly_sum(value, axis, step=1, stop=None):
+def butterfly_sum(value, axis, rounds=None):
     count = lax.axis_size(axis)
-    stop = count if stop is None else stop
-    while step < stop:
-        radix = 4 if step * 4 <= count else 2
+    if rounds is None:
+        rounds, step = [], 1
+        while step < count:
+            rounds.append((step, 4 if step * 4 <= count else 2))
+            step *= rounds[-1][1]
+    for step, radix in rounds:
         got = [
             lax.ppermute(value, axis, [(i, i ^ (k * step)) for i in range(count)])
             for k in range(1, radix)
@@ -45,7 +48,6 @@
             value = (value + got[0]) + (got[1] + got[2])
         else:
             value = value + got[0]
-        step *= radix
     return value
 
 
@@ -92,9 +94,9 @@
     query_parts = jnp.einsum(
         "nchd,nche->nhde", queries, grad_blocks, preferred_element_type=jnp.float32
     )
-    gain_near = butterfly_sum(butterfly_sum(gain_terms, "dp"), "seq", 1, 4)
-    suffix = carried_in(jnp.sum(query_parts, axis=0), "seq", True, gain_near[0])
-    grad_gain = butterfly_sum(gain_near, "seq", 4)
+    gain_dp = butterfly_sum(gain_terms, "dp", ((1, 2), (2, 4)))
+    suffix = carried_in(jnp.sum(query_parts, axis=0), "seq", True, gain_dp[0])
+    grad_gain = butterfly_sum(gain_dp, "seq")
     from_end = lax.cumsum(query_parts, axis=0, reverse=True)
     behind = jnp.concatenate([from_end[1:], query_parts[-1:] * 0.0], axis=0)
     suffix_states = (suffix[None] + behind).astype(jnp.bfloat16)

time: 143 us -> 142 us (level)
  waiting for transfers between devices: 38.7 us -> 35 us
  starting transfers between devices: 31 us -> 32.9 us
    ppermute x11, waiting for transfers between devices: 19.5 us -> 6.63 us  [butterfly_sum(): lax.ppermute(value, axis, [(i, i ^ k * step) for i in range(count)])]
    all_to_all x1, waiting for transfers between devices: 3.06 us -> 12.2 us  [carried_in(): parts = lax.all_to_all(rows, axis, 0, 0)]
    ppermute x11, starting transfers between devices: 15.1 us -> 17.3 us  [butterfly_sum(): lax.ppermute(value, axis, [(i, i ^ k * step) for i in range(count)])]
    unnamed x34 -> x32, local copies, waits for them, and re-layouts: 12.1 us -> 12.1 us
  transfers between devices with their start and end apart: 14 -> 14, of which waited for: 9 -> 6; matrix products, arithmetic and copies ran while one was open for 11% -> 12% of each run, Pallas kernels for 0% -> 0%
where the time goes in v10:
time: 142 us; the launch traced here: 141 us
  waiting for transfers between devices  35 us (25%)
  blocking collectives  34 us (24%)
  starting transfers between devices  32.9 us (23%)
  matrix products  15.9 us (11%)
  local copies, waits for them, and re-layouts  15.3 us (11%)
  other arithmetic  6.82 us (5%)
  between operations  1.55 us (1%)
    all_to_all x1, blocking collectives, carried_in(): parts = lax.all_to_all(rows, axis, 0, 0)  34 us
    ppermute x11, starting transfers between devices, butterfly_sum(): lax.ppermute(value, axis, [(i, i ^ k * step) for i in range(count)])  17.3 us
    all_to_all x2, waiting for transfers between devices, carried_in(): back = lax.all_to_all(shifted, axis, 0, 0)  16.2 us
    all_to_all x1, waiting for transfers between devices, carried_in(): parts = lax.all_to_all(rows, axis, 0, 0)  12.2 us
    unnamed x32, local copies, waits for them, and re-layouts  12.1 us
    all_to_all x2, starting transfers between devices, carried_in(): back = lax.all_to_all(shifted, axis, 0, 0)  10.5 us
    ppermute x11, waiting for transfers between devices, butterfly_sum(): lax.ppermute(value, axis, [(i, i ^ k * step) for i in range(count)])  6.63 us
    all_to_all x1, starting transfers between devices, carried_in(): parts = lax.all_to_all(rows, axis, 0, 0)  5.14 us
  transfers between devices with their start and end apart: 14, of which 6 were waited for; matrix products, arithmetic and copies ran while one was open for 12% of the time, Pallas kernels for 0%

profile of v10, /device:TPU:16, one launch (start us, length us, event | category | flops | bytes accessed | tf_op | source)
XLA Modules:
  0.0 141.5 jit_solution(5884182470804986298)
XLA Ops:
  0.6 1.5 %copy.60 = bf16[1,256,1536]{1,2,0:T(8,128)(2,1)S(1)} copy(bf16[1,256,1536]{2,1,0:T(8,128)(2,1)} %param.6) | data formatting | bytes 1572864 | tf_op args[1]
  2.8 34.0 %all_to_all.20 = f32[32,48,128]{2,1,0:T(8,128)S(1)} all-to-all(f32[32,48,128]{2,1,0:T(8,128)S(1)} %bitcast.105), channel_id=1, replica_groups=mesh['dp'=8,'seq'=32] {'seq'}, dimensions={0} | all-to-all | bytes 1572864 | tf_op jit(solution)/shard_map/all_to_all | solution.py:18
  38.9 5.4 %all-to-all-start.1 = ((f32[32,48,128]{2,1,0:T(8,128)}), f32[32,48,128]{2,1,0:T(8,128)}, u32[]{:S(2)}, u32[]{:S(2)}) async-start(f32[32,48,128]{2,1,0:T(8,128)} %copy.64), calls=%async_computation.1 | async-start | bytes 1572864 | tf_op jit(solution)/shard_map/all_to_all | solution.py:31
  44.6 1.7 %copy.65 = bf16[1,256,1536]{1,2,0:T(8,128)(2,1)S(1)} copy(bf16[1,256,1536]{2,1,0:T(8,128)(2,1)} %param.5) | data formatting | bytes 1572864 | tf_op args[0]
  48.1 1.8 %fusion.22 = f32[12,256,128]{1,2,0:T(8,128)} fusion(bf16[12,256,256]{2,1,0:T(8,128)(2,1)S(1)} %select_convert_fusion.1, bf16[256,12,128]{0,2,1:T(8,128)(2,1)S(1)} %bitcast.89), kind=kOutput, calls=%fused_computation.42 | convolution fusion | flops 201326592 | bytes 3932160 | tf_op jit(solution)/shard_map/nhct,nthe->nche/dot_general | solution.py:80
  49.9 16.2 %all-to-all-done.1 = f32[32,48,128]{2,1,0:T(8,128)} async-done(((f32[32,48,128]{2,1,0:T(8,128)}), f32[32,48,128]{2,1,0:T(8,128)}, u32[]{:S(2)}, u32[]{:S(2)}) %all-to-all-start.1) | async-done | bytes 786464 | tf_op jit(solution)/shard_map/all_to_all | solution.py:31
  66.1 1.6 %add_convert_fusion.1 = bf16[12,128,128]{2,1,0:T(8,128)(2,1)S(1)} fusion(f32[12,128,128]{2,1,0:T(8,128)} %bitcast.4, f32[12,128,128]{2,1,0:T(8,128)} %copy-done.3), kind=kLoop, calls=%fused_computation.27 | loop fusion | flops 589824 | bytes 1966080 | tf_op jit(solution)/shard_map/convert_element_type | solution.py:76
  69.5 2.5 %fusion.4 = (bf16[1,256,1536]{1,2,0:T(8,128)(2,1)S(1)}, bf16[1,256,1536]{1,2,0:T(8,128)(2,1)}) fusion(bf16[1,256,1536]{1,2,0:T(8,128)(2,1)} %copy-done.1, f32[12,128,256]{2,1,0:T(8,128)S(1)} %get-tuple-element.25, f32[256]{0:T(256)S(1)} %broadcast_multiply_fusion, f32[1536]{0:T(1024)S(1)} %copy-done.11, f32[256]{0:T(256)S(1)} %add_rsqrt_fusion), kind=kLoop, calls=%fused_computation.8 | loop fusion | flops 3538944 | bytes 3940352 | tf_op jit(solution)/shard_map/convert_element_type | solution.py:93
  73.2 5.1 %all-to-all-start.2 = ((f32[32,48,128]{2,1,0:T(8,128)}), f32[32,48,128]{2,1,0:T(8,128)}, u32[]{:S(2)}, u32[]{:S(2)}) async-start(f32[32,48,128]{2,1,0:T(8,128)} %bitcast.104), calls=%async_computation.2 | async-start | bytes 1572864 | tf_op jit(solution)/shard_map/all_to_all | solution.py:18
  80.1 2.9 %collective-permute-start.2 = (f32[1536]{0:T(1024)S(1)}, f32[1536]{0:T(1024)S(1)}, u32[]{:S(2)}, u32[]{:S(2)}) collective-permute-start(f32[1536]{0:T(1024)S(1)} %add.89), channel_id=1, source_target_pairs={{0,128},{32,160},{64,192},{96,224},{128,0},{160,32},{192,64},{224,... | collective-permute-start | bytes 18440 | tf_op jit(solution)/shard_map/ppermute | solution.py:44
  83.7 2.9 %fusion.25 = f32[12,128,256]{2,1,0:T(8,128)} fusion(bf16[256,12,128]{0,2,1:T(8,128)(2,1)S(1)} %bitcast.97, bf16[12,256,256]{2,1,0:T(8,128)(2,1)} %copy-done), kind=kOutput, calls=%fused_computation.45 | convolution fusion | flops 201326592 | bytes 3932160 | tf_op jit(solution)/shard_map/nhct,nche->nthe/dot_general | solution.py:122
  87.8 12.2 %all-to-all-done.2 = f32[32,48,128]{2,1,0:T(8,128)} async-done(((f32[32,48,128]{2,1,0:T(8,128)}), f32[32,48,128]{2,1,0:T(8,128)}, u32[]{:S(2)}, u32[]{:S(2)}) %all-to-all-start.2) | async-done | bytes 786464 | tf_op jit(solution)/shard_map/all_to_all | solution.py:18
  100.0 2.1 %fusion.11 = f32[32,48,128]{2,0,1:T(8,128)S(1)} fusion(f32[32,48,128]{2,1,0:T(8,128)} %all-to-all-done.2, f32[]{:T(128)} %bitcast.16), kind=kOutput, calls=%fused_computation.23 | convolution fusion | flops 75500544 | bytes 1572868 | tf_op jit(solution)/shard_map/ij,jkl->ikl/dot_general | solution.py:24
  102.1 1.4 copy.76
  103.4 5.1 %all-to-all-start.3 = ((f32[32,48,128]{2,1,0:T(8,128)}), f32[32,48,128]{2,1,0:T(8,128)}, u32[]{:S(2)}, u32[]{:S(2)}) async-start(f32[32,48,128]{2,1,0:T(8,128)} %copy.76), calls=%async_computation.3 | async-start | bytes 1572864 | tf_op jit(solution)/shard_map/all_to_all | solution.py:31
  108.5 1.5 %select_convert_fusion = bf16[12,256,256]{2,1,0:T(8,128)(2,1)S(1)} fusion(bf16[256,12,128]{0,2,1:T(8,128)(2,1)S(1)} %bitcast.98, bf16[256,12,128]{0,2,1:T(8,128)(2,1)S(1)} %bitcast.90, pred[256,256]{1,0:T(8,128)(4,1)} %copy-done.10), kind=kOutput, calls=%fused_computation | convolution fusion | flops 202899456 | bytes 3211264 | tf_op jit(solution)/shard_map/nche,nthe->nhct/dot_general | solution.py:103
  110.0 2.9 %collective-permute-start.6 = (f32[1536]{0:T(1024)S(1)}, f32[1536]{0:T(1024)S(1)}, u32[]{:S(2)}, u32[]{:S(2)}) collective-permute-start(f32[1536]{0:T(1024)S(1)} %add_add_fusion.2), channel_id=1, source_target_pairs={{0,3},{1,2},{2,1},{3,0},{4,7},{5,6},{6,5},{7,4},{8,11},{9,10},{10,... | collective-permute-start | bytes 18440 | tf_op jit(solution)/shard_map/ppermute | solution.py:44
  114.2 1.5 %fusion.26 = f32[12,256,128]{1,2,0:T(8,128)} fusion(bf16[256,12,128]{0,2,1:T(8,128)(2,1)S(1)} %bitcast.103, bf16[12,256,256]{2,1,0:T(8,128)(2,1)S(1)} %select_convert_fusion), kind=kOutput, calls=%fused_computation.46 | convolution fusion | flops 201326592 | bytes 3932160 | tf_op jit(solution)/shard_map/nhct,nchd->nthd/dot_general | solution.py:116
  115.7 2.4 %collective-permute-done.5 = f32[1536]{0:T(1024)S(1)} collective-permute-done((f32[1536]{0:T(1024)S(1)}, f32[1536]{0:T(1024)S(1)}, u32[]{:S(2)}, u32[]{:S(2)}) %collective-permute-start.5) | collective-permute-done | bytes 6176 | tf_op jit(solution)/shard_map/ppermute | solution.py:44
  118.1 3.6 %collective-permute-start.9 = (f32[1536]{0:T(1024)S(1)}, f32[1536]{0:T(1024)S(1)}, u32[]{:S(2)}, u32[]{:S(2)}) collective-permute-start(f32[1536]{0:T(1024)S(1)} %add_add_fusion.1), channel_id=1, source_target_pairs={{0,12},{1,13},{2,14},{3,15},{4,8},{5,9},{6,10},{7,11},{8,4},{9,5},... | collective-permute-start | bytes 18440 | tf_op jit(solution)/shard_map/ppermute | solution.py:44
  123.2 2.9 %collective-permute-done.9 = f32[1536]{0:T(1024)S(1)} collective-permute-done((f32[1536]{0:T(1024)S(1)}, f32[1536]{0:T(1024)S(1)}, u32[]{:S(2)}, u32[]{:S(2)}) %collective-permute-start.9) | collective-permute-done | bytes 6176 | tf_op jit(solution)/shard_map/ppermute | solution.py:44
  126.3 4.5 %collective-permute-start.10 = (f32[1536]{0:T(1024)S(1)}, f32[1536]{0:T(1024)S(1)}, u32[]{:S(2)}, u32[]{:S(2)}) collective-permute-start(f32[1536]{0:T(1024)S(1)} %add_add_fusion), channel_id=1, source_target_pairs={{0,16},{1,17},{2,18},{3,19},{4,20},{5,21},{6,22},{7,23},{8,24},{9,... | collective-permute-start | bytes 18440 | tf_op jit(solution)/shard_map/ppermute | solution.py:44
  132.0 2.4 %copy.80 = bf16[1,256,1536]{2,1,0:T(8,128)(2,1)} copy(bf16[1,256,1536]{1,2,0:T(8,128)(2,1)} %get-tuple-element.23) | data formatting | bytes 1572864
  136.2 1.4 fusion.10
  (66 shorter events, 20.7 us)
Async XLA Ops:
  0.6 1.5 %copy-start.8 = (bf16[1,256,1536]{2,1,0:T(8,128)(2,1)S(1)}, bf16[1,256,1536]{2,1,0:T(8,128)(2,1)}, u32[]{:S(2)}) copy-start(bf16[1,256,1536]{2,1,0:T(8,128)(2,1)} %param.7) | copy-start | bytes 2359300
  2.8 34.8 %copy-start.3 = (f32[12,128,128]{2,1,0:T(8,128)}, f32[12,128,128]{2,1,0:T(8,128)S(1)}, u32[]{:S(2)}) copy-start(f32[12,128,128]{2,1,0:T(8,128)S(1)} %fusion.21) | copy-start | bytes 2359300
  38.9 5.4 %copy-start.9 = (bf16[1,256,1536]{2,1,0:T(8,128)(2,1)S(1)}, bf16[1,256,1536]{2,1,0:T(8,128)(2,1)}, u32[]{:S(2)}) copy-start(bf16[1,256,1536]{2,1,0:T(8,128)(2,1)} %param.9) | copy-start | bytes 2359300
  38.9 27.2 %all-to-all-start.1 = ((f32[32,48,128]{2,1,0:T(8,128)}), f32[32,48,128]{2,1,0:T(8,128)}, u32[]{:S(2)}, u32[]{:S(2)}) async-start(f32[32,48,128]{2,1,0:T(8,128)} %copy.64), calls=%async_computation.1 | async-start | bytes 1572864 | tf_op jit(solution)/shard_map/all_to_all | solution.py:31
  44.6 23.9 %copy-start.1 = (bf16[1,256,1536]{1,2,0:T(8,128)(2,1)}, bf16[1,256,1536]{1,2,0:T(8,128)(2,1)S(1)}, u32[]{:S(2)}) copy-start(bf16[1,256,1536]{1,2,0:T(8,128)(2,1)S(1)} %copy.70) | copy-start | bytes 2359300
  47.0 1.1 copy-start
  66.1 1.9 %copy-start.6 = (f32[12,256,128]{1,2,0:T(8,128)S(1)}, f32[12,256,128]{1,2,0:T(8,128)}, u32[]{:S(2)}) copy-start(f32[12,256,128]{1,2,0:T(8,128)} %fusion.22) | copy-start | bytes 4718596
  73.2 26.8 %all-to-all-start.2 = ((f32[32,48,128]{2,1,0:T(8,128)}), f32[32,48,128]{2,1,0:T(8,128)}, u32[]{:S(2)}, u32[]{:S(2)}) async-start(f32[32,48,128]{2,1,0:T(8,128)} %bitcast.104), calls=%async_computation.2 | async-start | bytes 1572864 | tf_op jit(solution)/shard_map/all_to_all | solution.py:18
  78.3 1.3 collective-permute-start
  79.6 7.0 %collective-permute-start.3 = (f32[1536]{0:T(1024)S(1)}, f32[1536]{0:T(1024)S(1)}, u32[]{:S(2)}, u32[]{:S(2)}) collective-permute-start(f32[1536]{0:T(1024)S(1)} %add.89), channel_id=1, source_target_pairs={{0,192},{32,224},{64,128},{96,160},{128,64},{160,96},{192,0},{224,... | collective-permute-start | bytes 18440 | tf_op jit(solution)/shard_map/ppermute | solution.py:44
  80.1 6.6 %collective-permute-start.2 = (f32[1536]{0:T(1024)S(1)}, f32[1536]{0:T(1024)S(1)}, u32[]{:S(2)}, u32[]{:S(2)}) collective-permute-start(f32[1536]{0:T(1024)S(1)} %add.89), channel_id=1, source_target_pairs={{0,128},{32,160},{64,192},{96,224},{128,0},{160,32},{192,64},{224,... | collective-permute-start | bytes 18440 | tf_op jit(solution)/shard_map/ppermute | solution.py:44
  83.0 3.7 %collective-permute-start.1 = (f32[1536]{0:T(1024)S(1)}, f32[1536]{0:T(1024)S(1)}, u32[]{:S(2)}, u32[]{:S(2)}) collective-permute-start(f32[1536]{0:T(1024)S(1)} %add.89), channel_id=1, source_target_pairs={{0,64},{32,96},{64,0},{96,32},{128,192},{160,224},{192,128},{224,1... | collective-permute-start | bytes 18440 | tf_op jit(solution)/shard_map/ppermute | solution.py:44
  103.4 32.8 %all-to-all-start.3 = ((f32[32,48,128]{2,1,0:T(8,128)}), f32[32,48,128]{2,1,0:T(8,128)}, u32[]{:S(2)}, u32[]{:S(2)}) async-start(f32[32,48,128]{2,1,0:T(8,128)} %copy.76), calls=%async_computation.3 | async-start | bytes 1572864 | tf_op jit(solution)/shard_map/all_to_all | solution.py:31
  110.0 5.7 %collective-permute-start.6 = (f32[1536]{0:T(1024)S(1)}, f32[1536]{0:T(1024)S(1)}, u32[]{:S(2)}, u32[]{:S(2)}) collective-permute-start(f32[1536]{0:T(1024)S(1)} %add_add_fusion.2), channel_id=1, source_target_pairs={{0,3},{1,2},{2,1},{3,0},{4,7},{5,6},{6,5},{7,4},{8,11},{9,10},{10,... | collective-permute-start | bytes 18440 | tf_op jit(solution)/shard_map/ppermute | solution.py:44
  112.9 5.2 %collective-permute-start.5 = (f32[1536]{0:T(1024)S(1)}, f32[1536]{0:T(1024)S(1)}, u32[]{:S(2)}, u32[]{:S(2)}) collective-permute-start(f32[1536]{0:T(1024)S(1)} %add_add_fusion.2), channel_id=1, source_target_pairs={{0,2},{1,3},{2,0},{3,1},{4,6},{5,7},{6,4},{7,5},{8,10},{9,11},{10,... | collective-permute-start | bytes 18440 | tf_op jit(solution)/shard_map/ppermute | solution.py:44
  113.7 4.4 %collective-permute-start.4 = (f32[1536]{0:T(1024)S(1)}, f32[1536]{0:T(1024)S(1)}, u32[]{:S(2)}, u32[]{:S(2)}) collective-permute-start(f32[1536]{0:T(1024)S(1)} %add_add_fusion.2), channel_id=1, source_target_pairs={{0,1},{1,0},{2,3},{3,2},{4,5},{5,4},{6,7},{7,6},{8,9},{9,8},{10,11... | collective-permute-start | bytes 18440 | tf_op jit(solution)/shard_map/ppermute | solution.py:44
  118.1 8.0 %collective-permute-start.9 = (f32[1536]{0:T(1024)S(1)}, f32[1536]{0:T(1024)S(1)}, u32[]{:S(2)}, u32[]{:S(2)}) collective-permute-start(f32[1536]{0:T(1024)S(1)} %add_add_fusion.1), channel_id=1, source_target_pairs={{0,12},{1,13},{2,14},{3,15},{4,8},{5,9},{6,10},{7,11},{8,4},{9,5},... | collective-permute-start | bytes 18440 | tf_op jit(solution)/shard_map/ppermute | solution.py:44
  121.7 4.6 %collective-permute-start.8 = (f32[1536]{0:T(1024)S(1)}, f32[1536]{0:T(1024)S(1)}, u32[]{:S(2)}, u32[]{:S(2)}) collective-permute-start(f32[1536]{0:T(1024)S(1)} %add_add_fusion.1), channel_id=1, source_target_pairs={{0,8},{1,9},{2,10},{3,11},{4,12},{5,13},{6,14},{7,15},{8,0},{9,1},... | collective-permute-start | bytes 18440 | tf_op jit(solution)/shard_map/ppermute | solution.py:44
  121.7 4.6 %collective-permute-start.7 = (f32[1536]{0:T(1024)S(1)}, f32[1536]{0:T(1024)S(1)}, u32[]{:S(2)}, u32[]{:S(2)}) collective-permute-start(f32[1536]{0:T(1024)S(1)} %add_add_fusion.1), channel_id=1, source_target_pairs={{0,4},{1,5},{2,6},{3,7},{4,0},{5,1},{6,2},{7,3},{8,12},{9,13},{10,... | collective-permute-start | bytes 18440 | tf_op jit(solution)/shard_map/ppermute | solution.py:44
  126.3 9.3 %collective-permute-start.10 = (f32[1536]{0:T(1024)S(1)}, f32[1536]{0:T(1024)S(1)}, u32[]{:S(2)}, u32[]{:S(2)}) collective-permute-start(f32[1536]{0:T(1024)S(1)} %add_add_fusion), channel_id=1, source_target_pairs={{0,16},{1,17},{2,18},{3,19},{4,20},{5,21},{6,22},{7,23},{8,24},{9,... | collective-permute-start | bytes 18440 | tf_op jit(solution)/shard_map/ppermute | solution.py:44
  132.0 2.4 %copy-start.7 = (bf16[12,128,256]{2,1,0:T(8,128)(2,1)S(1)}, bf16[12,128,256]{2,1,0:T(8,128)(2,1)}, u32[]{:S(2)}) copy-start(bf16[12,128,256]{2,1,0:T(8,128)(2,1)} %fusion.7) | copy-start | bytes 2359300
  132.0 4.2 %copy-start.2 = (f32[12,128,128]{1,2,0:T(8,128)S(1)}, f32[12,128,128]{1,2,0:T(8,128)}, u32[]{:S(2)}) copy-start(f32[12,128,128]{1,2,0:T(8,128)} %fusion.24) | copy-start | bytes 2359300
  136.2 1.6 %copy-start.4 = (f32[12,128,256]{2,1,0:T(8,128)S(1)}, f32[12,128,256]{2,1,0:T(8,128)}, u32[]{:S(2)}) copy-start(f32[12,128,256]{2,1,0:T(8,128)} %fusion.25) | copy-start | bytes 4718596
  138.3 1.7 %copy-start.5 = (f32[12,256,128]{1,2,0:T(8,128)S(1)}, f32[12,256,128]{1,2,0:T(8,128)}, u32[]{:S(2)}) copy-start(f32[12,256,128]{1,2,0:T(8,128)} %fusion.26) | copy-start | bytes 4718596
  (2 other events, 1.4 us)

commit v11 on v8

--- a/solution.py
+++ b/solution.py
@@ -32,10 +32,10 @@
     return back.reshape(value.shape)
 
 
-def butterfly_sum(value, axis, step=1, stop=None):
+def butterfly_sum(value, axis):
     count = lax.axis_size(axis)
-    stop = count if stop is None else stop
-    while step < stop:
+    step = 1
+    while step < count:
         radix = 4 if step * 4 <= count else 2
         got = [
             lax.ppermute(value, axis, [(i, i ^ (k * step)) for i in range(count)])
@@ -92,9 +92,9 @@
     query_parts = jnp.einsum(
         "nchd,nche->nhde", queries, grad_blocks, preferred_element_type=jnp.float32
     )
-    gain_near = butterfly_sum(butterfly_sum(gain_terms, "dp"), "seq", 1, 4)
-    suffix = carried_in(jnp.sum(query_parts, axis=0), "seq", True, gain_near[0])
-    grad_gain = butterfly_sum(gain_near, "seq", 4)
+    gain_dp = butterfly_sum(gain_terms, "dp")
+    suffix = carried_in(jnp.sum(query_parts, axis=0), "seq", True, gain_dp[0])
+    grad_gain = butterfly_sum(gain_dp, "seq")
     from_end = lax.cumsum(query_parts, axis=0, reverse=True)
     behind = jnp.concatenate([from_end[1:], query_parts[-1:] * 0.0], axis=0)
     suffix_states = (suffix[None] + behind).astype(jnp.bfloat16)
@@ -138,7 +138,7 @@
         P(),
         P("dp", "seq", None),
     )
-    return jax.shard_map(
+    return (jax.shard_map(
         local_body,
         mesh=mesh,
         in_specs=placed,
@@ -150,4 +150,4 @@
             P(),
         ),
         check_vma=False,
-    )
+    ))

time: 143 us -> 142 us (level)
  waiting for transfers between devices: 38.7 us -> 36.8 us
    ppermute x11, waiting for transfers between devices: 19.5 us -> 9.23 us  [butterfly_sum(): lax.ppermute(value, axis, [(i, i ^ k * step) for i in range(count)])]
    all_to_all x1, waiting for transfers between devices: 3.06 us -> 11.4 us  [carried_in(): parts = lax.all_to_all(rows, axis, 0, 0)]
    unnamed x34 -> x32, local copies, waits for them, and re-layouts: 12.1 us -> 12.1 us
  transfers between devices with their start and end apart: 14 -> 14, of which waited for: 9 -> 8; matrix products, arithmetic and copies ran while one was open for 11% -> 12% of each run, Pallas kernels for 0% -> 0%
where the time goes in v11:
time: 142 us; the launch traced here: 141 us
  waiting for transfers between devices  36.8 us (26%)
  blocking collectives  34 us (24%)
  starting transfers between devices  31.1 us (22%)
  matrix products  15.9 us (11%)
  local copies, waits for them, and re-layouts  15.3 us (11%)
  other arithmetic  6.82 us (5%)
  between operations  1.55 us (1%)
    all_to_all x1, blocking collectives, carried_in(): parts = lax.all_to_all(rows, axis, 0, 0)  34 us
    all_to_all x2, waiting for transfers between devices, carried_in(): back = lax.all_to_all(shifted, axis, 0, 0)  16.2 us
    ppermute x11, starting transfers between devices, butterfly_sum(): lax.ppermute(value, axis, [(i, i ^ k * step) for i in range(count)])  15.5 us
    unnamed x32, local copies, waits for them, and re-layouts  12.1 us
    all_to_all x1, waiting for transfers between devices, carried_in(): parts = lax.all_to_all(rows, axis, 0, 0)  11.4 us
    all_to_all x2, starting transfers between devices, carried_in(): back = lax.all_to_all(shifted, axis, 0, 0)  10.5 us
    ppermute x11, waiting for transfers between devices, butterfly_sum(): lax.ppermute(value, axis, [(i, i ^ k * step) for i in range(count)])  9.23 us
    all_to_all x1, starting transfers between devices, carried_in(): parts = lax.all_to_all(rows, axis, 0, 0)  5.14 us
  transfers between devices with their start and end apart: 14, of which 8 were waited for; matrix products, arithmetic and copies ran while one was open for 12% of the time, Pallas kernels for 0%

profile of v11, /device:TPU:16, one launch (start us, length us, event | category | flops | bytes accessed | tf_op | source)
XLA Modules:
  0.0 141.5 jit_solution(10535958473844103807)
XLA Ops:
  0.6 1.5 %copy.60 = bf16[1,256,1536]{1,2,0:T(8,128)(2,1)S(1)} copy(bf16[1,256,1536]{2,1,0:T(8,128)(2,1)} %param.6) | data formatting | bytes 1572864 | tf_op args[1]
  2.8 34.0 %all_to_all.20 = f32[32,48,128]{2,1,0:T(8,128)S(1)} all-to-all(f32[32,48,128]{2,1,0:T(8,128)S(1)} %bitcast.105), channel_id=1, replica_groups=mesh['dp'=8,'seq'=32] {'seq'}, dimensions={0} | all-to-all | bytes 1572864 | tf_op jit(solution)/shard_map/all_to_all | solution.py:18
  38.9 5.4 %all-to-all-start.1 = ((f32[32,48,128]{2,1,0:T(8,128)}), f32[32,48,128]{2,1,0:T(8,128)}, u32[]{:S(2)}, u32[]{:S(2)}) async-start(f32[32,48,128]{2,1,0:T(8,128)} %copy.64), calls=%async_computation.1 | async-start | bytes 1572864 | tf_op jit(solution)/shard_map/all_to_all | solution.py:31
  44.6 1.7 %copy.65 = bf16[1,256,1536]{1,2,0:T(8,128)(2,1)S(1)} copy(bf16[1,256,1536]{2,1,0:T(8,128)(2,1)} %param.5) | data formatting | bytes 1572864 | tf_op args[0]
  48.1 1.8 %fusion.22 = f32[12,256,128]{1,2,0:T(8,128)} fusion(bf16[12,256,256]{2,1,0:T(8,128)(2,1)S(1)} %select_convert_fusion.1, bf16[256,12,128]{0,2,1:T(8,128)(2,1)S(1)} %bitcast.89), kind=kOutput, calls=%fused_computation.42 | convolution fusion | flops 201326592 | bytes 3932160 | tf_op jit(solution)/shard_map/nhct,nthe->nche/dot_general | solution.py:78
  49.9 16.2 %all-to-all-done.1 = f32[32,48,128]{2,1,0:T(8,128)} async-done(((f32[32,48,128]{2,1,0:T(8,128)}), f32[32,48,128]{2,1,0:T(8,128)}, u32[]{:S(2)}, u32[]{:S(2)}) %all-to-all-start.1) | async-done | bytes 786464 | tf_op jit(solution)/shard_map/all_to_all | solution.py:31
  66.1 1.6 %add_convert_fusion.1 = bf16[12,128,128]{2,1,0:T(8,128)(2,1)S(1)} fusion(f32[12,128,128]{2,1,0:T(8,128)} %bitcast.4, f32[12,128,128]{2,1,0:T(8,128)} %copy-done.3), kind=kLoop, calls=%fused_computation.27 | loop fusion | flops 589824 | bytes 1966080 | tf_op jit(solution)/shard_map/convert_element_type | solution.py:74
  69.5 2.5 %fusion.4 = (bf16[1,256,1536]{1,2,0:T(8,128)(2,1)S(1)}, bf16[1,256,1536]{1,2,0:T(8,128)(2,1)}) fusion(bf16[1,256,1536]{1,2,0:T(8,128)(2,1)} %copy-done.1, f32[12,128,256]{2,1,0:T(8,128)S(1)} %get-tuple-element.25, f32[256]{0:T(256)S(1)} %broadcast_multiply_fusion, f32[1536]{0:T(1024)S(1)} %copy-done.11, f32[256]{0:T(256)S(1)} %add_rsqrt_fusion), kind=kLoop, calls=%fused_computation.8 | loop fusion | flops 3538944 | bytes 3940352 | tf_op jit(solution)/shard_map/convert_element_type | solution.py:91
  73.2 5.1 %all-to-all-start.2 = ((f32[32,48,128]{2,1,0:T(8,128)}), f32[32,48,128]{2,1,0:T(8,128)}, u32[]{:S(2)}, u32[]{:S(2)}) async-start(f32[32,48,128]{2,1,0:T(8,128)} %bitcast.104), calls=%async_computation.2 | async-start | bytes 1572864 | tf_op jit(solution)/shard_map/all_to_all | solution.py:18
  78.4 1.4 collective-permute-start.1
  82.6 2.9 %fusion.25 = f32[12,128,256]{2,1,0:T(8,128)} fusion(bf16[256,12,128]{0,2,1:T(8,128)(2,1)S(1)} %bitcast.97, bf16[12,256,256]{2,1,0:T(8,128)(2,1)} %copy-done), kind=kOutput, calls=%fused_computation.45 | convolution fusion | flops 201326592 | bytes 3932160 | tf_op jit(solution)/shard_map/nhct,nche->nthe/dot_general | solution.py:120
  85.6 1.9 %collective-permute-done.3 = f32[1536]{0:T(1024)S(1)} collective-permute-done((f32[1536]{0:T(1024)S(1)}, f32[1536]{0:T(1024)S(1)}, u32[]{:S(2)}, u32[]{:S(2)}) %collective-permute-start.3) | collective-permute-done | bytes 6176 | tf_op jit(solution)/shard_map/ppermute | solution.py:41
  88.6 11.4 %all-to-all-done.2 = f32[32,48,128]{2,1,0:T(8,128)} async-done(((f32[32,48,128]{2,1,0:T(8,128)}), f32[32,48,128]{2,1,0:T(8,128)}, u32[]{:S(2)}, u32[]{:S(2)}) %all-to-all-start.2) | async-done | bytes 786464 | tf_op jit(solution)/shard_map/all_to_all | solution.py:18
  100.0 2.1 %fusion.11 = f32[32,48,128]{2,0,1:T(8,128)S(1)} fusion(f32[32,48,128]{2,1,0:T(8,128)} %all-to-all-done.2, f32[]{:T(128)} %bitcast.16), kind=kOutput, calls=%fused_computation.23 | convolution fusion | flops 75500544 | bytes 1572868 | tf_op jit(solution)/shard_map/ij,jkl->ikl/dot_general | solution.py:24
  102.1 1.4 copy.76
  103.4 5.1 %all-to-all-start.3 = ((f32[32,48,128]{2,1,0:T(8,128)}), f32[32,48,128]{2,1,0:T(8,128)}, u32[]{:S(2)}, u32[]{:S(2)}) async-start(f32[32,48,128]{2,1,0:T(8,128)} %copy.76), calls=%async_computation.3 | async-start | bytes 1572864 | tf_op jit(solution)/shard_map/all_to_all | solution.py:31
  108.5 1.5 %select_convert_fusion = bf16[12,256,256]{2,1,0:T(8,128)(2,1)S(1)} fusion(bf16[256,12,128]{0,2,1:T(8,128)(2,1)S(1)} %bitcast.98, bf16[256,12,128]{0,2,1:T(8,128)(2,1)S(1)} %bitcast.90, pred[256,256]{1,0:T(8,128)(4,1)} %copy-done.10), kind=kOutput, calls=%fused_computation | convolution fusion | flops 202899456 | bytes 3211264 | tf_op jit(solution)/shard_map/nche,nthe->nhct/dot_general | solution.py:101
  110.0 2.9 %collective-permute-start.6 = (f32[1536]{0:T(1024)S(1)}, f32[1536]{0:T(1024)S(1)}, u32[]{:S(2)}, u32[]{:S(2)}) collective-permute-start(f32[1536]{0:T(1024)S(1)} %add.92), channel_id=1, source_target_pairs={{0,3},{1,2},{2,1},{3,0},{4,7},{5,6},{6,5},{7,4},{8,11},{9,10},{10,... | collective-permute-start | bytes 18440 | tf_op jit(solution)/shard_map/ppermute | solution.py:41
  114.2 1.5 %fusion.26 = f32[12,256,128]{1,2,0:T(8,128)} fusion(bf16[256,12,128]{0,2,1:T(8,128)(2,1)S(1)} %bitcast.103, bf16[12,256,256]{2,1,0:T(8,128)(2,1)S(1)} %select_convert_fusion), kind=kOutput, calls=%fused_computation.46 | convolution fusion | flops 201326592 | bytes 3932160 | tf_op jit(solution)/shard_map/nhct,nchd->nthd/dot_general | solution.py:114
  115.7 2.4 %collective-permute-done.5 = f32[1536]{0:T(1024)S(1)} collective-permute-done((f32[1536]{0:T(1024)S(1)}, f32[1536]{0:T(1024)S(1)}, u32[]{:S(2)}, u32[]{:S(2)}) %collective-permute-start.5) | collective-permute-done | bytes 6176 | tf_op jit(solution)/shard_map/ppermute | solution.py:41
  118.1 3.6 %collective-permute-start.9 = (f32[1536]{0:T(1024)S(1)}, f32[1536]{0:T(1024)S(1)}, u32[]{:S(2)}, u32[]{:S(2)}) collective-permute-start(f32[1536]{0:T(1024)S(1)} %add_add_fusion.1), channel_id=1, source_target_pairs={{0,12},{1,13},{2,14},{3,15},{4,8},{5,9},{6,10},{7,11},{8,4},{9,5},... | collective-permute-start | bytes 18440 | tf_op jit(solution)/shard_map/ppermute | solution.py:41
  123.2 2.9 %collective-permute-done.9 = f32[1536]{0:T(1024)S(1)} collective-permute-done((f32[1536]{0:T(1024)S(1)}, f32[1536]{0:T(1024)S(1)}, u32[]{:S(2)}, u32[]{:S(2)}) %collective-permute-start.9) | collective-permute-done | bytes 6176 | tf_op jit(solution)/shard_map/ppermute | solution.py:41
  126.3 4.5 %collective-permute-start.10 = (f32[1536]{0:T(1024)S(1)}, f32[1536]{0:T(1024)S(1)}, u32[]{:S(2)}, u32[]{:S(2)}) collective-permute-start(f32[1536]{0:T(1024)S(1)} %add_add_fusion), channel_id=1, source_target_pairs={{0,16},{1,17},{2,18},{3,19},{4,20},{5,21},{6,22},{7,23},{8,24},{9,... | collective-permute-start | bytes 18440 | tf_op jit(solution)/shard_map/ppermute | solution.py:41
  132.0 2.4 %copy.80 = bf16[1,256,1536]{2,1,0:T(8,128)(2,1)} copy(bf16[1,256,1536]{1,2,0:T(8,128)(2,1)} %get-tuple-element.23) | data formatting | bytes 1572864
  (66 shorter events, 22.5 us)
Async XLA Ops:
  0.6 1.5 %copy-start.8 = (bf16[1,256,1536]{2,1,0:T(8,128)(2,1)S(1)}, bf16[1,256,1536]{2,1,0:T(8,128)(2,1)}, u32[]{:S(2)}) copy-start(bf16[1,256,1536]{2,1,0:T(8,128)(2,1)} %param.7) | copy-start | bytes 2359300
  2.8 34.8 %copy-start.3 = (f32[12,128,128]{2,1,0:T(8,128)}, f32[12,128,128]{2,1,0:T(8,128)S(1)}, u32[]{:S(2)}) copy-start(f32[12,128,128]{2,1,0:T(8,128)S(1)} %fusion.21) | copy-start | bytes 2359300
  38.9 5.4 %copy-start.9 = (bf16[1,256,1536]{2,1,0:T(8,128)(2,1)S(1)}, bf16[1,256,1536]{2,1,0:T(8,128)(2,1)}, u32[]{:S(2)}) copy-start(bf16[1,256,1536]{2,1,0:T(8,128)(2,1)} %param.9) | copy-start | bytes 2359300
  38.9 27.2 %all-to-all-start.1 = ((f32[32,48,128]{2,1,0:T(8,128)}), f32[32,48,128]{2,1,0:T(8,128)}, u32[]{:S(2)}, u32[]{:S(2)}) async-start(f32[32,48,128]{2,1,0:T(8,128)} %copy.64), calls=%async_computation.1 | async-start | bytes 1572864 | tf_op jit(solution)/shard_map/all_to_all | solution.py:31
  44.6 23.9 %copy-start.1 = (bf16[1,256,1536]{1,2,0:T(8,128)(2,1)}, bf16[1,256,1536]{1,2,0:T(8,128)(2,1)S(1)}, u32[]{:S(2)}) copy-start(bf16[1,256,1536]{1,2,0:T(8,128)(2,1)S(1)} %copy.70) | copy-start | bytes 2359300
  47.0 1.1 copy-start
  66.1 1.9 %copy-start.6 = (f32[12,256,128]{1,2,0:T(8,128)S(1)}, f32[12,256,128]{1,2,0:T(8,128)}, u32[]{:S(2)}) copy-start(f32[12,256,128]{1,2,0:T(8,128)} %fusion.22) | copy-start | bytes 4718596
  73.2 26.8 %all-to-all-start.2 = ((f32[32,48,128]{2,1,0:T(8,128)}), f32[32,48,128]{2,1,0:T(8,128)}, u32[]{:S(2)}, u32[]{:S(2)}) async-start(f32[32,48,128]{2,1,0:T(8,128)} %bitcast.104), calls=%async_computation.2 | async-start | bytes 1572864 | tf_op jit(solution)/shard_map/all_to_all | solution.py:18
  78.3 3.2 %collective-permute-start.2 = (f32[1536]{0:T(1024)S(1)}, f32[1536]{0:T(1024)S(1)}, u32[]{:S(2)}, u32[]{:S(2)}) collective-permute-start(f32[1536]{0:T(1024)S(1)} %get-tuple-element.20), channel_id=1, source_target_pairs={{0,96},{32,64},{64,32},{96,0},{128,224},{160,192},{192,160},{224,1... | collective-permute-start | bytes 18440 | tf_op jit(solution)/shard_map/ppermute | solution.py:41
  78.4 3.7 %collective-permute-start.1 = (f32[1536]{0:T(1024)S(1)}, f32[1536]{0:T(1024)S(1)}, u32[]{:S(2)}, u32[]{:S(2)}) collective-permute-start(f32[1536]{0:T(1024)S(1)} %get-tuple-element.20), channel_id=1, source_target_pairs={{0,64},{32,96},{64,0},{96,32},{128,192},{160,224},{192,128},{224,1... | collective-permute-start | bytes 18440 | tf_op jit(solution)/shard_map/ppermute | solution.py:41
  79.8 2.4 %collective-permute-start = (f32[1536]{0:T(1024)S(1)}, f32[1536]{0:T(1024)S(1)}, u32[]{:S(2)}, u32[]{:S(2)}) collective-permute-start(f32[1536]{0:T(1024)S(1)} %get-tuple-element.20), channel_id=1, source_target_pairs={{0,32},{32,0},{64,96},{96,64},{128,160},{160,128},{192,224},{224,1... | collective-permute-start | bytes 18440 | tf_op jit(solution)/shard_map/ppermute | solution.py:41
  82.2 5.2 %collective-permute-start.3 = (f32[1536]{0:T(1024)S(1)}, f32[1536]{0:T(1024)S(1)}, u32[]{:S(2)}, u32[]{:S(2)}) collective-permute-start(f32[1536]{0:T(1024)S(1)} %add_add_fusion.2), channel_id=1, source_target_pairs={{0,128},{32,160},{64,192},{96,224},{128,0},{160,32},{192,64},{224,... | collective-permute-start | bytes 18440 | tf_op jit(solution)/shard_map/ppermute | solution.py:41
  103.4 32.8 %all-to-all-start.3 = ((f32[32,48,128]{2,1,0:T(8,128)}), f32[32,48,128]{2,1,0:T(8,128)}, u32[]{:S(2)}, u32[]{:S(2)}) async-start(f32[32,48,128]{2,1,0:T(8,128)} %copy.76), calls=%async_computation.3 | async-start | bytes 1572864 | tf_op jit(solution)/shard_map/all_to_all | solution.py:31
  110.0 5.7 %collective-permute-start.6 = (f32[1536]{0:T(1024)S(1)}, f32[1536]{0:T(1024)S(1)}, u32[]{:S(2)}, u32[]{:S(2)}) collective-permute-start(f32[1536]{0:T(1024)S(1)} %add.92), channel_id=1, source_target_pairs={{0,3},{1,2},{2,1},{3,0},{4,7},{5,6},{6,5},{7,4},{8,11},{9,10},{10,... | collective-permute-start | bytes 18440 | tf_op jit(solution)/shard_map/ppermute | solution.py:41
  112.9 5.2 %collective-permute-start.5 = (f32[1536]{0:T(1024)S(1)}, f32[1536]{0:T(1024)S(1)}, u32[]{:S(2)}, u32[]{:S(2)}) collective-permute-start(f32[1536]{0:T(1024)S(1)} %add.92), channel_id=1, source_target_pairs={{0,2},{1,3},{2,0},{3,1},{4,6},{5,7},{6,4},{7,5},{8,10},{9,11},{10,... | collective-permute-start | bytes 18440 | tf_op jit(solution)/shard_map/ppermute | solution.py:41
  113.7 4.4 %collective-permute-start.4 = (f32[1536]{0:T(1024)S(1)}, f32[1536]{0:T(1024)S(1)}, u32[]{:S(2)}, u32[]{:S(2)}) collective-permute-start(f32[1536]{0:T(1024)S(1)} %add.92), channel_id=1, source_target_pairs={{0,1},{1,0},{2,3},{3,2},{4,5},{5,4},{6,7},{7,6},{8,9},{9,8},{10,11... | collective-permute-start | bytes 18440 | tf_op jit(solution)/shard_map/ppermute | solution.py:41
  118.1 8.0 %collective-permute-start.9 = (f32[1536]{0:T(1024)S(1)}, f32[1536]{0:T(1024)S(1)}, u32[]{:S(2)}, u32[]{:S(2)}) collective-permute-start(f32[1536]{0:T(1024)S(1)} %add_add_fusion.1), channel_id=1, source_target_pairs={{0,12},{1,13},{2,14},{3,15},{4,8},{5,9},{6,10},{7,11},{8,4},{9,5},... | collective-permute-start | bytes 18440 | tf_op jit(solution)/shard_map/ppermute | solution.py:41
  121.7 4.6 %collective-permute-start.8 = (f32[1536]{0:T(1024)S(1)}, f32[1536]{0:T(1024)S(1)}, u32[]{:S(2)}, u32[]{:S(2)}) collective-permute-start(f32[1536]{0:T(1024)S(1)} %add_add_fusion.1), channel_id=1, source_target_pairs={{0,8},{1,9},{2,10},{3,11},{4,12},{5,13},{6,14},{7,15},{8,0},{9,1},... | collective-permute-start | bytes 18440 | tf_op jit(solution)/shard_map/ppermute | solution.py:41
  121.7 4.6 %collective-permute-start.7 = (f32[1536]{0:T(1024)S(1)}, f32[1536]{0:T(1024)S(1)}, u32[]{:S(2)}, u32[]{:S(2)}) collective-permute-start(f32[1536]{0:T(1024)S(1)} %add_add_fusion.1), channel_id=1, source_target_pairs={{0,4},{1,5},{2,6},{3,7},{4,0},{5,1},{6,2},{7,3},{8,12},{9,13},{10,... | collective-permute-start | bytes 18440 | tf_op jit(solution)/shard_map/ppermute | solution.py:41
  126.3 9.3 %collective-permute-start.10 = (f32[1536]{0:T(1024)S(1)}, f32[1536]{0:T(1024)S(1)}, u32[]{:S(2)}, u32[]{:S(2)}) collective-permute-start(f32[1536]{0:T(1024)S(1)} %add_add_fusion), channel_id=1, source_target_pairs={{0,16},{1,17},{2,18},{3,19},{4,20},{5,21},{6,22},{7,23},{8,24},{9,... | collective-permute-start | bytes 18440 | tf_op jit(solution)/shard_map/ppermute | solution.py:41
  132.0 2.4 %copy-start.7 = (bf16[12,128,256]{2,1,0:T(8,128)(2,1)S(1)}, bf16[12,128,256]{2,1,0:T(8,128)(2,1)}, u32[]{:S(2)}) copy-start(bf16[12,128,256]{2,1,0:T(8,128)(2,1)} %fusion.7) | copy-start | bytes 2359300
  132.0 4.2 %copy-start.2 = (f32[12,128,128]{1,2,0:T(8,128)S(1)}, f32[12,128,128]{1,2,0:T(8,128)}, u32[]{:S(2)}) copy-start(f32[12,128,128]{1,2,0:T(8,128)} %fusion.24) | copy-start | bytes 2359300
  136.2 1.6 %copy-start.4 = (f32[12,128,256]{2,1,0:T(8,128)S(1)}, f32[12,128,256]{2,1,0:T(8,128)}, u32[]{:S(2)}) copy-start(f32[12,128,256]{2,1,0:T(8,128)} %fusion.25) | copy-start | bytes 4718596
  138.3 1.7 %copy-start.5 = (f32[12,256,128]{1,2,0:T(8,128)S(1)}, f32[12,256,128]{1,2,0:T(8,128)}, u32[]{:S(2)}) copy-start(f32[12,256,128]{1,2,0:T(8,128)} %fusion.26) | copy-start | bytes 4718596
  (2 other events, 1.4 us)
